TPU v7x, 32 devices: a whole 2x2x4 slice. The times are simulated.
32 devices in a mesh: groups: 2 (over y), ctx: 4 (over z), head: 2 (over x), role: 2 (over core).
Axes of the slice: x: 2, y: 2, z: 4, core: 2. Of those that a mesh axis runs over, the one named last changes fastest.
Arguments:
- prompt_query: bfloat16 [768, 64, 192], P(('groups', 'ctx'), ('head', 'role')), parts along dimension 0, may hold values from -200 to 200
- prompt_latent: bfloat16 [768, 576], P(('groups', 'ctx')), parts along dimension 0, may hold values from -60 to 60
- block_order: int32 [8], P('groups'), parts along dimension 0, may hold values from 0 to 3, as said below
- key_up: bfloat16 [64, 128, 512], P(('head', 'role')), may hold values from -0.5 to 0.5
- value_up: bfloat16 [64, 512, 128], P(('head', 'role')), may hold values from -1.796875 to 1.796875
- out_weight: bfloat16 [8192, 7168], P(('head', 'role'), 'ctx'), may hold values from -0.0625 to 0.0625
- step_query: bfloat16 [4, 8, 64, 192], P(None, 'groups', ('head', 'role')), parts along dimension 1, may hold values from -200 to 200
- cache_latent: bfloat16 [8, 1536, 576], P('groups', 'ctx'), parts along dimension 0, may hold values from -60 to 60
- step_latent: bfloat16 [4, 8, 576], P(None, 'groups'), parts along dimension 1, may hold values from -5 to 5
- cache_length: int32 [8], P('groups'), parts along dimension 0, may hold values from 2 to 1536
- block_dest: int32 [8], P('groups'), parts along dimension 0, may hold values from 0 to 3
Outputs:
- prompt_out: bfloat16 [768, 8192], P(('groups', 'ctx'), ('head', 'role')), parts along dimension 0
- step_out: bfloat16 [4, 8, 7168], P(None, 'groups', ('ctx', 'head', 'role')), parts along dimension 1
There are 2 independent parts, one for each index of `groups`. A program takes and returns all parts, laid end to end along the dimension named above; an argument that names none is the same for every part. Nothing has to cross between parts.
Inputs may be any that keep to these rules, and one draw needn't show every extreme that they name: `block_order`: a permutation: each block position appears once.
All inputs are finite; a program needn't handle non-finite values.
Results may differ from a plain program's by a relative error of at most 0.039.
Values may be sent and summed in bfloat16 or wider, within the bound.
No kernel may reach another device: no remote copies, remote signals or barrier semaphores. Data moves between devices by JAX's collectives and lax.ppermute only.
A program may use at most 64 MiB of HBM per device.

v0:
```python
import jax
import jax.numpy as jnp
from jax import lax
from jax.sharding import PartitionSpec as P


def absorbed(queries, key_up):
    nope_width = key_up.shape[1]
    latent_part = jnp.einsum(
        "...hn,hnc->...hc", queries[..., :nope_width], key_up, preferred_element_type=jnp.float32
    ).astype(jnp.bfloat16)
    return jnp.concatenate([latent_part, queries[..., nope_width:]], axis=-1)


def combine(first_part, second_part):
    high_a, totals_a, summed_a = first_part
    high_b, totals_b, summed_b = second_part
    highest = jnp.maximum(high_a, high_b)
    factor_a = jnp.exp(high_a - highest)
    factor_b = jnp.exp(high_b - highest)
    return (
        highest,
        totals_a * factor_a + totals_b * factor_b,
        summed_a * factor_a[..., None] + summed_b * factor_b[..., None],
    )


def partial_softmax(scores, mask, values, form):
    scores = jnp.where(mask, scores, -1e30)
    highest = jnp.max(scores, axis=-1)
    weights = jnp.where(mask, jnp.exp(scores - highest[..., None]), 0.0)
    summed = jnp.einsum(
        form, weights.astype(jnp.bfloat16), values, preferred_element_type=jnp.float32
    )
    return (highest, jnp.sum(weights, axis=-1), summed)


def fresh_part(queries, latents, score_scale, latent_width):
    step_count = queries.shape[0]
    scores = (
        jnp.einsum("sbhc,ubc->sbhu", queries, latents, preferred_element_type=jnp.float32)
        * score_scale
    )
    step_ids = jnp.arange(step_count)
    order_mask = (step_ids[None, :] <= step_ids[:, None])[:, None, None, :]
    return partial_softmax(scores, order_mask, latents[..., :latent_width], "sbhu,ubc->sbhc")


def finish_heads(running, value_up):
    highest, totals, summed = running
    attended = (summed / totals[..., None]).astype(jnp.bfloat16)
    heads_out = jnp.einsum(
        "sbhc,hcv->sbhv", attended, value_up, preferred_element_type=jnp.float32
    ).astype(jnp.bfloat16)
    return heads_out.reshape(
        heads_out.shape[0], heads_out.shape[1], heads_out.shape[2] * heads_out.shape[3]
    )


def per_device(
    prompt_query,
    prompt_latent,
    block_order,
    key_up,
    value_up,
    out_weight,
    step_query,
    cache_latent,
    step_latent,
    cache_length,
    block_dest,
):
    tokens, head_count, query_width = prompt_query.shape
    latent_width = key_up.shape[2]
    score_scale = query_width ** (-0.5)
    context_size = lax.axis_size("ctx")
    place = lax.axis_index("ctx")
    slot_ids = jnp.arange(context_size)
    own_block = jnp.sum(jnp.where(slot_ids == place, block_order, 0))
    own_dest = jnp.sum(jnp.where(slot_ids == place, block_dest, 0))
    query_pos = own_block * tokens + jnp.arange(tokens)
    row_pos = jnp.repeat(query_pos, head_count)
    absorbed_rows = absorbed(prompt_query, key_up)
    query_rows = absorbed_rows.reshape(tokens * head_count, absorbed_rows.shape[2])
    query_count = tokens * head_count
    shard_rows = lax.all_gather(prompt_latent, "ctx", axis=0, tiled=True)
    indices = jnp.arange(shard_rows.shape[0])
    onehot = (indices // tokens)[:, None] == slot_ids[None, :]
    key_pos = (
        jnp.sum(jnp.where(onehot, block_order[None, :], 0), axis=1) * tokens + indices % tokens
    )
    highest = jnp.full((query_count,), -1e30, jnp.float32)
    scores = (
        lax.dot_general(
            query_rows, shard_rows, (((1,), (1,)), ((), ())), preferred_element_type=jnp.float32
        )
        * score_scale
    )
    visible = key_pos[None, :] <= row_pos[:, None]
    scores = jnp.where(visible, scores, -1e30)
    peak_now = jnp.maximum(highest, jnp.max(scores, axis=1))
    weights = jnp.where(visible, jnp.exp(scores - peak_now[:, None]), 0.0)
    totals = jnp.sum(weights, axis=1)
    summed = jnp.dot(
        weights.astype(jnp.bfloat16),
        shard_rows[:, :latent_width],
        preferred_element_type=jnp.float32,
    )
    highest, totals, summed = (peak_now, totals, summed)
    attended = (
        (summed / totals[:, None]).astype(jnp.bfloat16).reshape(tokens, head_count, latent_width)
    )
    prompt_out = jnp.einsum(
        "thc,hcv->thv", attended, value_up, preferred_element_type=jnp.float32
    ).astype(jnp.bfloat16)
    prompt_out = prompt_out.reshape(tokens, head_count * value_up.shape[2])
    step_count, row_count = (step_query.shape[0], step_query.shape[1])
    cache_span = cache_latent.shape[1]
    queries = absorbed(step_query, key_up)
    cache_scores = (
        jnp.einsum("sbhc,bpc->sbhp", queries, cache_latent, preferred_element_type=jnp.float32)
        * score_scale
    )
    cache_pos = place * cache_span + jnp.arange(cache_span)
    live_mask = (cache_pos[None, :] < cache_length[:, None])[None, :, None, :]
    cache_part = partial_softmax(
        cache_scores, live_mask, cache_latent[..., :latent_width], "sbhp,bpc->sbhc"
    )
    handed_scores = (
        jnp.einsum("sbhc,pc->sbhp", queries, prompt_latent, preferred_element_type=jnp.float32)
        * score_scale
    )
    handed = (jnp.arange(row_count) == own_dest)[None, :, None, None]
    handed_part = partial_softmax(
        handed_scores, handed, prompt_latent[:, :latent_width], "sbhp,pc->sbhc"
    )
    highest, totals, summed = combine(cache_part, handed_part)
    peak_score = lax.pmax(highest, "ctx")
    factor = jnp.exp(highest - peak_score)
    totals, summed = (
        lax.psum((totals * factor).astype(jnp.bfloat16), "ctx").astype(jnp.float32),
        lax.psum((summed * factor[..., None]).astype(jnp.bfloat16), "ctx").astype(jnp.float32),
    )
    merged = (peak_score, totals, summed)
    running = combine(merged, fresh_part(queries, step_latent, score_scale, latent_width))
    step_heads = finish_heads(running, value_up)
    flat_heads = step_heads.reshape(step_count * row_count, step_heads.shape[2])
    partial_value = jnp.dot(flat_heads, out_weight, preferred_element_type=jnp.float32).reshape(
        step_count, row_count, out_weight.shape[1]
    )
    step_out = lax.psum_scatter(
        partial_value, ("head", "role"), scatter_dimension=2, tiled=True
    ).astype(jnp.bfloat16)
    return (prompt_out, step_out)


def solution(mesh):
    return jax.shard_map(
        per_device,
        mesh=mesh,
        in_specs=(
            P(("groups", "ctx"), ("head", "role"), None),
            P(("groups", "ctx"), None),
            P("groups"),
            P(("head", "role"), None, None),
            P(("head", "role"), None, None),
            P(("head", "role"), "ctx"),
            P(None, "groups", ("head", "role"), None),
            P("groups", "ctx", None),
            P(None, "groups", None),
            P("groups"),
            P("groups"),
        ),
        out_specs=(
            P(("groups", "ctx"), ("head", "role")),
            P(None, "groups", ("ctx", "head", "role")),
        ),
        check_vma=False,
    )
```

profile of v0, /device:TPU:0, one launch (start us, length us, event | category | flops | bytes accessed | tf_op | source)
XLA Modules:
  0.0 112.9 jit_solution(10005748408280748228)
XLA Ops:
  7.2 0.0 copy-start
  7.2 0.0 all-reduce.2.cloned.1.call-start
  7.2 1.0 slice.27
  8.2 0.8 slice.28
  9.1 1.3 %fusion.112 = (s32[]{:T(128)}, s32[]{:T(128)}) fusion(s32[4]{0:T(128)} %param.13, s32[]{:T(128)S(6)} %axis_index.15, s32[4]{0:T(128)} %param.21), kind=kLoop, calls=%fused_computation.116 | loop fusion | flops 18 | bytes 44 | tf_op jit(solution)/shard_map/reduce_sum | solution.py:79
  10.4 0.6 iota_compare_fusion.2
  11.1 0.7 broadcast_compare_fusion
  11.8 0.0 copy-done
  11.8 0.0 copy-start.1
  11.8 0.4 fusion.59
  12.2 0.0 copy-start.3
  12.2 0.2 pad_maximum_fusion.1
  12.4 0.9 copy-done.1
  13.3 0.5 fusion.121
  13.8 0.2 fusion.74
  14.1 0.0 copy-done.3
  14.1 0.3 fusion.120
  14.4 13.7 %pmax.7 = f32[4,4,16]{2,0,1:T(4,128)S(1)} all-reduce(f32[4,4,16]{2,0,1:T(4,128)S(1)} %copy_maximum_fusion), channel_id=1, replica_groups=mesh['groups'=2,'ctx'=4,'head'=2,'role'=2] {'ctx'}, use_global_device_ids=true, to_apply=%region_7.8 | all-reduce | flops 256 | bytes 2048 | tf_op jit(solution)/shard_map/pmax | solution.py:138
  28.2 0.2 fusion.85
  28.4 0.2 convolution_multiply_fusion.1
  28.6 0.0 copy-start.5
  28.7 0.0 slice-start
  28.7 2.8 %fusion.38 = bf16[4,4,16,512]{3,2,0,1:T(8,128)(2,1)} fusion(f32[4,4,16,512]{3,2,0,1:T(8,128)S(1)} %convolution_multiply_fusion.1, bf16[4,384,576]{1,2,0:T(8,128)(2,1)} %param.18, f32[4,4,16]{2,0,1:T(4,128)S(1)} %get-tuple-element.7, f32[4,4,16]{2,0,1:T(4,128)S(1)} %get-tuple-element.6, f32[4,4,16,384]{3,2,0,1:T(8,128)S(1)} %get-tuple-element.16, ...), kind=kOutput, calls=%fused_computation.33 | convolution fusion | flops 101482496 | bytes 2757120 | tf_op jit(solution)/shard_map/sbhp,bpc->sbhc/dot_general | solution.py:32
  31.5 0.0 all-reduce.2.cloned.1.call-update
  31.5 0.0 reduce-scatter.4.cloned.1.call-start
  31.6 16.9 %all_gather.3 = bf16[384,576]{1,0:T(8,128)(2,1)} all-gather(bf16[96,576]{1,0:T(8,128)(2,1)S(1)} %copy-done.3), channel_id=1, replica_groups=mesh['groups'=2,'ctx'=4,'head'=2,'role'=2] {'ctx'}, dimensions={0}, use_global_device_ids=true | all-gather | bytes 552960 | tf_op jit(solution)/shard_map/all_gather | solution.py:86
  48.4 0.0 slice-start.1
  49.2 0.1 broadcast_in_dim.113
  49.2 0.1 le.39
  49.3 0.0 copy-done.5
  49.3 0.1 select_reduce_fusion
  49.4 0.0 slice-done
  49.4 0.6 fusion.16
  50.0 0.0 slice-done.1
  50.0 0.1 copy.124
  50.1 0.2 pad_maximum_fusion
  50.3 0.0 copy-start.2
  50.3 0.6 copy.93
  51.0 0.4 copy-done.2
  51.3 1.2 %fusion.119 = (f32[1536]{0:T(1024)S(1)}, f32[1536,384]{0,1:T(8,128)S(1)}) fusion(bf16[1536,576]{1,0:T(8,128)(2,1)S(1)} %bitcast.122, bf16[384,576]{1,0:T(8,128)(2,1)S(1)} %copy-done.2, s32[1536]{0:T(1024)S(1)} %le.39, s32[384]{0:T(512)S(1)} %fusion.108), kind=kOutput, calls=%fused_computation.123 | convolution fusion | flops 681835008 | bytes 4584960 | tf_op jit(solution)/shard_map/dot_general | solution.py:94
  52.5 0.5 fusion.7
  53.0 0.0 copy-start.4
  53.0 2.3 %divide_convert_fusion = bf16[1536,512]{1,0:T(8,128)(2,1)} fusion(f32[1536]{0:T(1024)S(1)} %fusion.7, f32[1536,384]{0,1:T(8,128)S(1)} %get-tuple-element.12, f32[1536]{0:T(1024)S(1)} %broadcast_maximum_fusion, s32[1536]{0:T(1024)S(1)} %le.39, s32[384]{0:T(512)S(1)} %fusion.108, bf16[384,576]{1,0:T(8,128)(2,1)S(1)} %copy-done.2), kind=kOutput, calls=%fused_computation.2 | convolution fusion | flops 607911936 | bytes 4352000 | tf_op jit(solution)/shard_map/dot_general | solution.py:104
  55.3 0.0 copy-done.4
  55.3 0.6 fusion.122
  55.9 0.1 fusion.92
  56.1 9.2 %psum.15 = bf16[4,4,16]{2,0,1:T(4,128)(2,1)S(1)} all-reduce(bf16[4,4,16]{2,0,1:T(4,128)(2,1)S(1)} %get-tuple-element.5), channel_id=1, replica_groups=mesh['groups'=2,'ctx'=4,'head'=2,'role'=2] {'ctx'}, use_global_device_ids=true, to_apply=%region_12.13 | all-reduce | flops 256 | bytes 1024 | tf_op jit(solution)/shard_map/psum | solution.py:141
  65.3 1.1 all-reduce.2.cloned.1.call-done
  66.4 0.0 copy-start.6
  66.4 1.5 %fusion.41 = bf16[4,4,16,512]{3,2,0,1:T(8,128)(2,1)S(1)} fusion(bf16[4,4,16,512]{3,2,0,1:T(8,128)(2,1)} %all-reduce.2.cloned.1.call-done, f32[4,4,16]{2,0,1:T(4,128)S(1)} %bitcast.130, f32[4,4,16]{2,0,1:T(4,128)S(1)} %bitcast.132, f32[4,4,16]{2,0,1:T(4,128)S(1)} %bitcast.131, f32[4,4,16,4]{2,3,0,1:T(4,128)S(1)} %get-tuple-element.18, ...), kind=kOutput, calls=%fused_computation.34 | convolution fusion | flops 1838080 | bytes 548880 | tf_op jit(solution)/shard_map/sbhu,ubc->sbhc/dot_general | solution.py:32
  68.0 0.1 copy-done.6
  68.1 0.5 fusion.66
  68.6 4.2 %fusion = f32[4,4,1792]{2,1,0:T(4,128)S(1)} fusion(bf16[2048,1792]{1,0:T(8,128)(2,1)} %param.16, bf16[16,4,1,4,128]{4,3,2,1,0:T(4,128)(2,1)S(1)} %fusion.66), kind=kOutput, calls=%fused_computation | convolution fusion | flops 117440512 | bytes 7520256 | tf_op jit(solution)/shard_map/dot_general | solution.py:148
  72.8 3.0 %copy.121 = f32[4,4,1792]{1,0,2:T(4,128)} copy(f32[4,4,1792]{2,1,0:T(4,128)S(1)} %fusion) | data formatting | bytes 229376
  75.8 4.1 %reshape.125 = f32[1792,16]{1,0:T(8,128)} reshape(f32[1792,4,4]{2,1,0:T(4,128)} %bitcast.121) | data formatting | bytes 229376
  80.0 0.0 reduce-scatter.4.cloned.1.call-update
  80.0 4.0 %fusion.35 = bf16[16,12,8,128]{3,2,1,0:T(8,128)(2,1)S(1)} fusion(bf16[16,512,128]{2,1,0:T(8,128)(2,1)} %param.15, bf16[96,16,512]{2,1,0:T(8,128)(2,1)} %bitcast.133), kind=kOutput, calls=%fused_computation.32 | convolution fusion | flops 201523200 | bytes 4063232 | tf_op jit(solution)/shard_map/thc,hcv->thv/dot_general | solution.py:113
  83.9 0.8 copy.178
  84.8 19.1 %reduce-scatter.4.cloned.1.call-done = f32[448,16]{1,0:T(8,128)} async-done(((f32[1792,16]{1,0:T(8,128)}), f32[448,16]{1,0:T(8,128)}) %reduce-scatter.4.cloned.1.call-update) | async-done | bytes 28688
  103.9 1.2 %reshape.126 = bf16[448,4,4]{2,1,0:T(4,128)(2,1)S(1)} reshape(f32[448,16]{1,0:T(8,128)} %reduce-scatter.4.cloned.1.call-done) | data formatting | bytes 43008
  105.1 0.9 copy.122
  (11 shorter events, 0.1 us)
Async XLA Ops:
  7.2 4.6 %copy-start = (bf16[16,128,512]{2,1,0:T(8,128)(2,1)S(1)}, bf16[16,128,512]{2,1,0:T(8,128)(2,1)}, u32[]{:S(2)}) copy-start(bf16[16,128,512]{2,1,0:T(8,128)(2,1)} %param.14) | copy-start | bytes 6291460
  7.2 59.2 %all-reduce.2.cloned.1.call-start = ((), (), s32[]{:S(2)}) async-start(), calls=%async_computation.1 | async-start | bytes 524288 | tf_op jit(solution)/shard_map/psum | solution.py:142
  11.8 1.5 %copy-start.1 = (bf16[4,384,576]{1,2,0:T(8,128)(2,1)S(1)}, bf16[4,384,576]{1,2,0:T(8,128)(2,1)}, u32[]{:S(2)}) copy-start(bf16[4,384,576]{1,2,0:T(8,128)(2,1)} %param.18) | copy-start | bytes 5308420
  12.2 1.9 %copy-start.3 = (bf16[96,576]{1,0:T(8,128)(2,1)S(1)}, bf16[96,576]{1,0:T(8,128)(2,1)}, u32[]{:S(2)}) copy-start(bf16[96,576]{1,0:T(8,128)(2,1)} %param.12) | copy-start | bytes 331780
  28.6 20.7 %copy-start.5 = (s32[4]{0:T(128)S(1)}, s32[4]{0:T(128)}, u32[]{:S(2)}) copy-start(s32[4]{0:T(128)} %param.13) | copy-start | bytes 52
  28.7 20.8 %slice-start = ((bf16[96,16,192]{2,1,0:T(8,128)(2,1)}), bf16[96,16,128]{2,1,0:T(8,128)(2,1)S(1)}, s32[]{:S(2)}) async-start(bf16[96,16,192]{2,1,0:T(8,128)(2,1)} %param.11), calls=%async_computation.3 | async-start | bytes 786432 | tf_op jit(solution)/shard_map/slice | solution.py:10
  31.5 72.4 %reduce-scatter.4.cloned.1.call-start = ((), (), s32[]{:S(2)}) async-start(), calls=%async_computation.2 | async-start | bytes 1146880
  48.4 1.6 %slice-start.1 = ((bf16[96,16,192]{2,1,0:T(8,128)(2,1)}), bf16[96,16,64]{2,1,0:T(8,128)(2,1)S(1)}, s32[]{:S(2)}) async-start(bf16[96,16,192]{2,1,0:T(8,128)(2,1)} %param.11), calls=%async_computation.4 | async-start | bytes 786432 | tf_op jit(solution)/shard_map/slice | solution.py:12
  50.3 1.0 copy-start.2
  53.0 2.3 %copy-start.4 = (bf16[4,4,576]{2,1,0:T(4,128)(2,1)S(1)}, bf16[4,4,576]{2,1,0:T(4,128)(2,1)}, u32[]{:S(2)}) copy-start(bf16[4,4,576]{2,1,0:T(4,128)(2,1)} %param.19) | copy-start | bytes 55300
  66.4 1.7 %copy-start.6 = (bf16[16,512,128]{2,1,0:T(8,128)(2,1)S(1)}, bf16[16,512,128]{2,1,0:T(8,128)(2,1)}, u32[]{:S(2)}) copy-start(bf16[16,512,128]{2,1,0:T(8,128)(2,1)} %param.15) | copy-start | bytes 6291460
Sparse Core Ops, SparseCore 0:
  31.6 34.7 all-reduce.1
  80.1 23.7 reduce-scatter.3
where the time goes:
time: 113 us
  blocking collectives  39.8 us (35%)
  waiting for transfers between devices  20.2 us (18%)
  matrix products  19.1 us (17%)
  between operations  15 us (13%)
  local copies, waits for them, and re-layouts  14.3 us (13%)
  other arithmetic  4.26 us (4%)
    unnamed x3, waiting for transfers between devices  19.1 us
    all_gather x1, blocking collectives, per_device(): shard_rows = lax.all_gather(prompt_latent, 'ctx', axis=0, tiled=True)  16.9 us
    pmax x1, blocking collectives, per_device(): peak_score = lax.pmax(highest, 'ctx')  13.7 us
    unnamed x20, local copies, waits for them, and re-layouts  10.8 us
    psum x1, blocking collectives, per_device(): lax.psum((totals * factor).astype(jnp.bfloat16), 'ctx').astype(jnp.float32)  9.23 us
    dot_general x3, matrix products, partial_softmax(): jnp.einsum(form, weights.astype(jnp.bfloat16), values, preferred_element_...  4.56 us
    dot_general x1, matrix products, per_device(): jnp.dot(flat_heads, out_weight, preferred_element_type=jnp.float32)  4.22 us
    dot_general x1, matrix products, per_device(): jnp.einsum('thc,hcv->thv', attended, value_up, preferred_element_type=jnp...  3.96 us
  transfers between devices with their start and end apart: 2, of which 2 were waited for; matrix products, arithmetic and copies ran while one was open for 10% of the time, Pallas kernels for 0%

commit v1 on v0

v1 whole, which is shorter than its diff:
```python
import jax
import jax.numpy as jnp
from jax import lax
from jax.sharding import PartitionSpec as P


def absorbed(queries, key_up):
    nope_width = key_up.shape[1]
    latent_part = jnp.einsum(
        "...hn,hnc->...hc", queries[..., :nope_width], key_up, preferred_element_type=jnp.float32
    ).astype(jnp.bfloat16)
    return jnp.concatenate([latent_part, queries[..., nope_width:]], axis=-1)


def swap(value, axis, step):
    size = lax.axis_size(axis)
    return lax.ppermute(value, axis, [(i, i ^ step) for i in range(size)])


def doublings(size):
    steps = []
    step = 1
    while step < size:
        steps.append(step)
        step *= 2
    assert step == size
    return steps


def combine(first_part, second_part):
    high_a, totals_a, mixed_a = first_part
    high_b, totals_b, mixed_b = second_part
    highest = jnp.maximum(high_a, high_b)
    share_a = totals_a * jnp.exp(high_a - highest)
    share_b = totals_b * jnp.exp(high_b - highest)
    totals = share_a + share_b
    safe = jnp.maximum(totals, 1e-30)
    mixed = (
        mixed_a.astype(jnp.float32) * (share_a / safe)[..., None]
        + mixed_b.astype(jnp.float32) * (share_b / safe)[..., None]
    )
    return highest, totals, mixed


def per_device(
    prompt_query,
    prompt_latent,
    block_order,
    key_up,
    value_up,
    out_weight,
    step_query,
    cache_latent,
    step_latent,
    cache_length,
    block_dest,
):
    tokens, head_count, query_width = prompt_query.shape
    latent_width = key_up.shape[2]
    score_scale = query_width ** (-0.5)
    context_size = lax.axis_size("ctx")
    place = lax.axis_index("ctx")
    slot_ids = jnp.arange(context_size)
    step_count, row_count = (step_query.shape[0], step_query.shape[1])
    cache_span = cache_latent.shape[1]

    role_count = lax.axis_size("role")
    part = tokens // role_count
    role = lax.axis_index("role")
    own_part = lax.dynamic_slice_in_dim(prompt_latent, role * part, part, axis=0)
    gathered = own_part[None]
    for step in doublings(context_size):
        gathered = jnp.concatenate([gathered, swap(gathered, "ctx", step)], axis=0)
    other = swap(gathered[1:], "role", 1)
    far_first = jnp.where(role == 0, gathered[1:], other)
    far_second = jnp.where(role == 0, other, gathered[1:])
    shard_rows = jnp.concatenate(
        [prompt_latent[None], jnp.concatenate([far_first, far_second], axis=1)], axis=0
    ).reshape(context_size * tokens, prompt_latent.shape[1])
    sources = slot_ids ^ place
    block_pos = jnp.sum(
        jnp.where(sources[:, None] == slot_ids[None, :], block_order[None, :], 0), axis=1
    )
    key_pos = jnp.repeat(block_pos * tokens, tokens) + jnp.tile(jnp.arange(tokens), context_size)

    own_block = jnp.sum(jnp.where(slot_ids == place, block_order, 0))
    own_dest = jnp.sum(jnp.where(slot_ids == place, block_dest, 0))

    queries = absorbed(step_query, key_up)
    cache_scores = jnp.einsum(
        "sbhc,bpc->sbhp", queries, cache_latent, preferred_element_type=jnp.float32
    )
    cache_pos = place * cache_span + jnp.arange(cache_span)
    live_mask = jnp.broadcast_to(
        (cache_pos[None, :] < cache_length[:, None])[None, :, None, :], cache_scores.shape
    )
    handed_scores = jnp.einsum(
        "sbhc,pc->sbhp", queries, prompt_latent, preferred_element_type=jnp.float32
    )
    handed = jnp.broadcast_to(
        (jnp.arange(row_count) == own_dest)[None, :, None, None], handed_scores.shape
    )
    fresh_scores = jnp.einsum(
        "sbhc,ubc->sbhu", queries, step_latent, preferred_element_type=jnp.float32
    )
    step_ids = jnp.arange(step_count)
    order_mask = (step_ids[None, :] <= step_ids[:, None])[:, None, None, :] & (place == 0)
    order_mask = jnp.broadcast_to(order_mask, fresh_scores.shape)
    scores = jnp.concatenate([cache_scores, handed_scores, fresh_scores], axis=-1) * score_scale
    mask = jnp.concatenate([live_mask, handed, order_mask], axis=-1)
    scores = jnp.where(mask, scores, -1e30)
    highest = jnp.max(scores, axis=-1)
    weights = jnp.where(mask, jnp.exp(scores - highest[..., None]), 0.0)
    totals = jnp.sum(weights, axis=-1)
    weights = weights.astype(jnp.bfloat16)
    edge = cache_span + tokens
    summed = (
        jnp.einsum(
            "sbhp,bpc->sbhc",
            weights[..., :cache_span],
            cache_latent[..., :latent_width],
            preferred_element_type=jnp.float32,
        )
        + jnp.einsum(
            "sbhp,pc->sbhc",
            weights[..., cache_span:edge],
            prompt_latent[:, :latent_width],
            preferred_element_type=jnp.float32,
        )
        + jnp.einsum(
            "sbhu,ubc->sbhc",
            weights[..., edge:],
            step_latent[..., :latent_width],
            preferred_element_type=jnp.float32,
        )
    )
    attended_part = (summed / jnp.maximum(totals, 1e-30)[..., None]).astype(jnp.bfloat16)
    mixed = jnp.einsum(
        "sbhc,hcv->sbhv", attended_part, value_up, preferred_element_type=jnp.float32
    ).astype(jnp.bfloat16)
    running = (highest, totals, mixed)
    for step in doublings(context_size):
        stats = jnp.stack(running[:2])
        far_stats = swap(stats, "ctx", step)
        far_mixed = swap(running[2], "ctx", step)
        highest, totals, mixed = combine(running, (far_stats[0], far_stats[1], far_mixed))
        running = (highest, totals, mixed.astype(jnp.bfloat16))
    flat_heads = running[2].reshape(step_count * row_count, head_count * value_up.shape[2])
    share = jnp.dot(flat_heads, out_weight, preferred_element_type=jnp.float32)
    head_size = lax.axis_size("head")
    share = share.reshape(step_count * row_count, head_size, role_count, -1)
    for axis, place_dim, size in (("role", 2, role_count), ("head", 1, head_size)):
        index = lax.axis_index(axis)
        for step in reversed(doublings(size)):
            halves = share.shape[place_dim] // 2
            low = lax.slice_in_dim(share, 0, halves, axis=place_dim)
            high = lax.slice_in_dim(share, halves, 2 * halves, axis=place_dim)
            upper = (index & step) != 0
            keep = jnp.where(upper, high, low)
            give = jnp.where(upper, low, high)
            share = keep + swap(give, axis, step)
    step_out = share.reshape(step_count, row_count, -1).astype(jnp.bfloat16)

    query_pos = own_block * tokens + jnp.arange(tokens)
    row_pos = jnp.repeat(query_pos, head_count)
    query_rows = absorbed(prompt_query, key_up).reshape(tokens * head_count, -1)
    scores = (
        lax.dot_general(
            query_rows, shard_rows, (((1,), (1,)), ((), ())), preferred_element_type=jnp.float32
        )
        * score_scale
    )
    visible = key_pos[None, :] <= row_pos[:, None]
    scores = jnp.where(visible, scores, -1e30)
    peak_now = jnp.max(scores, axis=1)
    weights = jnp.where(visible, jnp.exp(scores - peak_now[:, None]), 0.0)
    totals = jnp.sum(weights, axis=1)
    summed = jnp.dot(
        weights.astype(jnp.bfloat16),
        shard_rows[:, :latent_width],
        preferred_element_type=jnp.float32,
    )
    attended = (
        (summed / totals[:, None]).astype(jnp.bfloat16).reshape(tokens, head_count, latent_width)
    )
    prompt_out = jnp.einsum(
        "thc,hcv->thv", attended, value_up, preferred_element_type=jnp.float32
    ).astype(jnp.bfloat16)
    prompt_out = prompt_out.reshape(tokens, head_count * value_up.shape[2])
    return (prompt_out, step_out)


def solution(mesh):
    return jax.shard_map(
        per_device,
        mesh=mesh,
        in_specs=(
            P(("groups", "ctx"), ("head", "role"), None),
            P(("groups", "ctx"), None),
            P("groups"),
            P(("head", "role"), None, None),
            P(("head", "role"), None, None),
            P(("head", "role"), "ctx"),
            P(None, "groups", ("head", "role"), None),
            P("groups", "ctx", None),
            P(None, "groups", None),
            P("groups"),
            P("groups"),
        ),
        out_specs=(
            P(("groups", "ctx"), ("head", "role")),
            P(None, "groups", ("ctx", "head", "role")),
        ),
        check_vma=False,
    )
```

time: 113 us -> 66.6 us (0.59)
  blocking collectives: 39.8 us -> 0 us
  between operations: 15 us -> 1.68 us
  starting transfers between devices: 0.08 us -> 11.6 us
  waiting for transfers between devices: 20.2 us -> 11.3 us
  local copies, waits for them, and re-layouts: 14.3 us -> 21.3 us
  matrix products: 19.1 us -> 14.3 us
  other arithmetic: 4.26 us -> 5.78 us
    unnamed x3 -> x0, waiting for transfers between devices: 19.1 us -> none
    all_gather x1 -> x0, blocking collectives: 16.9 us -> none  [per_device(): shard_rows = lax.all_gather(prompt_latent, 'ctx', axis=0, tiled=True)]
    pmax x1 -> x0, blocking collectives: 13.7 us -> none  [per_device(): peak_score = lax.pmax(highest, 'ctx')]
    ppermute x0 -> x9, starting transfers between devices: none -> 11.6 us  [swap(): return lax.ppermute(value, axis, [(i, i ^ step) for i in range(size)])]
    ppermute x0 -> x9, waiting for transfers between devices: none -> 11.3 us  [swap(): return lax.ppermute(value, axis, [(i, i ^ step) for i in range(size)])]
    psum x1 -> x0, blocking collectives: 9.23 us -> none  [per_device(): lax.psum((totals * factor).astype(jnp.bfloat16), 'ctx').astype(jnp.float32)]
    concatenate x1, local copies, waits for them, and re-layouts: 0.64 us -> 3.61 us  [absorbed(): return jnp.concatenate([latent_part, queries[..., nope_width:]], axis=-1)]
    dot_general x6, matrix products: 9.86 us -> 6.89 us  [the longest x1 5.08 us: per_device(): share = jnp.dot(flat_heads, out_weight, preferred_element_type=jnp.float32)]
  transfers between devices with their start and end apart: 2 -> 9, of which waited for: 2 -> 4; matrix products, arithmetic and copies ran while one was open for 10% -> 38% of each run, Pallas kernels for 0% -> 0%
where the time goes in v1:
time: 66.6 us; the launch traced here: 66 us
  local copies, waits for them, and re-layouts  21.3 us (32%)
  matrix products  14.3 us (21%)
  starting transfers between devices  11.6 us (17%)
  waiting for transfers between devices  11.3 us (17%)
  other arithmetic  5.78 us (9%)
  between operations  1.68 us (3%)
    unnamed x22, local copies, waits for them, and re-layouts  13.4 us
    ppermute x9, starting transfers between devices, swap(): return lax.ppermute(value, axis, [(i, i ^ step) for i in range(size)])  11.6 us
    ppermute x9, waiting for transfers between devices, swap(): return lax.ppermute(value, axis, [(i, i ^ step) for i in range(size)])  11.3 us
    dot_general x1, matrix products, per_device(): share = jnp.dot(flat_heads, out_weight, preferred_element_type=jnp.float32)  5.08 us
    concatenate x1, local copies, waits for them, and re-layouts, absorbed(): return jnp.concatenate([latent_part, queries[..., nope_width:]], axis=-1)  3.61 us
    dot_general x1, matrix products, per_device(): lax.dot_general(query_rows, shard_rows, (((1,), (1,)), ((), ())), preferr...  2.71 us
    dot_general x1, matrix products, per_device(): jnp.einsum('thc,hcv->thv', attended, value_up, preferred_element_type=jnp...  1.89 us
    concatenate x2, other arithmetic, absorbed(): return jnp.concatenate([latent_part, queries[..., nope_width:]], axis=-1)  1.69 us
  transfers between devices with their start and end apart: 9, of which 4 were waited for; matrix products, arithmetic and copies ran while one was open for 38% of the time, Pallas kernels for 0%

profile of v1, /device:TPU:0, one launch (start us, length us, event | category | flops | bytes accessed | tf_op | source)
XLA Modules:
  0.0 66.0 jit_solution(9548413246214997885)
XLA Ops:
  0.6 0.0 copy-start
  0.6 1.0 %slice.64 = bf16[4,4,16,128]{3,2,1,0:T(8,128)(2,1)S(1)} slice(bf16[4,4,16,192]{3,2,1,0:T(8,128)(2,1)} %param.17), slice={[0:4], [0:4], [0:16], [0:128]} | slice | bytes 131072 | tf_op jit(solution)/shard_map/slice | solution.py:10
  1.6 0.8 %slice.65 = bf16[4,4,16,64]{3,2,1,0:T(8,128)(2,1)S(1)} slice(bf16[4,4,16,192]{3,2,1,0:T(8,128)(2,1)} %param.17), slice={[0:4], [0:4], [0:16], [128:192]} | slice | bytes 65536 | tf_op jit(solution)/shard_map/slice | solution.py:12
  2.5 1.3 %fusion.79 = (s32[]{:T(128)}, s32[]{:T(128)}) fusion(s32[4]{0:T(128)} %param.13, s32[]{:T(128)S(6)} %axis_index.37, s32[4]{0:T(128)} %param.21), kind=kLoop, calls=%fused_computation.110 | loop fusion | flops 18 | bytes 44 | tf_op jit(solution)/shard_map/reduce_sum | solution.py:86
  3.8 0.6 iota_compare_fusion.2
  4.5 0.0 copy-start.1
  4.5 0.4 fusion.41
  4.9 0.0 copy-start.4
  5.0 0.0 copy-start.3
  5.0 0.0 copy-start.6
  5.0 0.2 pad_maximum_fusion.1
  5.2 0.9 %copy-done.1 = bf16[4,384,576]{1,2,0:T(8,128)(2,1)S(1)} copy-done((bf16[4,384,576]{1,2,0:T(8,128)(2,1)S(1)}, bf16[4,384,576]{1,2,0:T(8,128)(2,1)}, u32[]{:S(2)}) %copy-start.1) | copy-done | bytes 1769496
  6.0 0.4 fusion.29
  6.5 0.2 convolution_bitcast_fusion.1
  6.7 0.2 fusion.57
  7.0 0.1 broadcast_compare_fusion
  7.0 0.1 broadcast_in_dim.87
  7.2 0.2 fusion.82
  7.4 0.4 fusion.53
  7.8 3.1 %collective-permute-start.3 = (f32[2,4,4,16]{3,1,2,0:T(4,128)S(1)}, f32[2,4,4,16]{3,1,2,0:T(4,128)S(1)}, u32[]{:S(2)}, u32[]{:S(2)}) collective-permute-start(f32[2,4,4,16]{3,1,2,0:T(4,128)S(1)} %pad_maximum_fusion.3), channel_id=1, source_target_pairs={{0,4},{4,0},{8,12},{12,8},{1,5},{5,1},{9,13},{13,9},{2,6},{6,2},{1... | collective-permute-start | bytes 6152 | tf_op jit(solution)/shard_map/ppermute | solution.py:17
  11.0 0.1 collective-permute-start
  11.1 0.2 fusion.62
  11.3 1.1 %copy-done.2 = bf16[4,384,576]{1,2,0:T(8,128)(2,1)S(1)} copy-done((bf16[4,384,576]{1,2,0:T(8,128)(2,1)S(1)}, bf16[4,384,576]{1,2,0:T(8,128)(2,1)}, u32[]{:S(2)}) %copy-start.2) | copy-done | bytes 1769496
  12.4 0.6 fusion.22
  13.1 0.0 slice-start.1
  13.1 0.2 select_reduce_fusion
  13.3 0.1 iota_add_fusion.1
  13.3 0.6 fusion.14
  13.9 0.1 slice-done.1
  14.1 0.1 copy.92
  14.2 1.5 %pad_maximum_fusion = bf16[96,16,576]{2,0,1:T(8,128)(2,1)} fusion(bf16[96,16,64]{2,0,1:T(8,128)(2,1)S(1)} %copy.92, bf16[96,16,512]{2,0,1:T(8,128)(2,1)S(1)} %fusion.14), kind=kLoop, calls=%fused_computation.8 | loop fusion | flops 3538944 | bytes 3538944 | tf_op jit(solution)/shard_map/concatenate | solution.py:12
  16.4 2.7 %collective-permute-start.5 = (f32[2,4,4,16]{3,1,2,0:T(4,128)S(1)}, f32[2,4,4,16]{3,1,2,0:T(4,128)S(1)}, u32[]{:S(2)}, u32[]{:S(2)}) collective-permute-start(f32[2,4,4,16]{3,1,2,0:T(4,128)S(1)} %pad_maximum_fusion.4), channel_id=1, source_target_pairs={{0,8},{4,12},{8,0},{12,4},{1,9},{5,13},{9,1},{13,5},{2,10},{6,14},... | collective-permute-start | bytes 6152 | tf_op jit(solution)/shard_map/ppermute | solution.py:17
  19.1 10.7 %copy.74 = bf16[2048,1792]{0,1:T(8,128)(2,1)} copy(bf16[2048,1792]{1,0:T(8,128)(2,1)} %param.16) | data formatting | bytes 14680064 | tf_op args[5]
  29.8 0.1 broadcast_in_dim.81
  29.9 0.1 le.31
  29.9 0.1 add.77
  30.0 3.6 %copy.52 = bf16[96,16,576]{2,1,0:T(8,128)(2,1)} copy(bf16[96,16,576]{2,0,1:T(8,128)(2,1)} %pad_maximum_fusion) | data formatting | bytes 3538944 | tf_op jit(solution)/shard_map/concatenate | solution.py:12
  33.7 0.3 fusion.35
  34.0 0.5 fusion.47
  34.5 0.9 %collective-permute-start.4 = (bf16[4,4,16,128]{3,1,0,2:T(4,128)(2,1)S(1)}, bf16[4,4,16,128]{3,1,0,2:T(4,128)(2,1)S(1)}, u32[]{:S(2)}, u32[]{:S(2)}) collective-permute-start(bf16[4,4,16,128]{3,1,0,2:T(4,128)(2,1)S(1)} %fusion.47), channel_id=1, source_target_pairs={{0,4},{4,0},{8,12},{12,8},{1,5},{5,1},{9,13},{13,9},{2,6},{6,2},{1... | collective-permute-start | bytes 196616 | tf_op jit(solution)/shard_map/ppermute | solution.py:17
  35.4 0.1 copy.72
  35.6 0.1 copy.69
  35.7 0.1 copy.70
  35.8 0.1 copy.71
  35.9 2.9 %collective-permute-done.4 = bf16[4,4,16,128]{3,1,0,2:T(4,128)(2,1)S(1)} collective-permute-done((bf16[4,4,16,128]{3,1,0,2:T(4,128)(2,1)S(1)}, bf16[4,4,16,128]{3,1,0,2:T(4,128)(2,1)S(1)}, u32[]{:S(2)}, u32[]{:S(2)}) %collective-permute-start.4) | collective-permute-done | bytes 65568 | tf_op jit(solution)/shard_map/ppermute | solution.py:17
  38.8 0.2 add_convert_fusion.1
  39.0 0.4 collective-permute-start.6
  39.4 2.6 %collective-permute-start.1 = (bf16[2,48,576]{2,1,0:T(8,128)(2,1)S(1)}, bf16[2,48,576]{2,1,0:T(8,128)(2,1)S(1)}, u32[]{:S(2)}, u32[]{:S(2)}) collective-permute-start(bf16[2,48,576]{2,1,0:T(8,128)(2,1)S(1)} %pad_maximum_fusion.2), channel_id=1, source_target_pairs={{0,8},{4,12},{8,0},{12,4},{1,9},{5,13},{9,1},{13,5},{2,10},{6,14},... | collective-permute-start | bytes 331784 | tf_op jit(solution)/shard_map/ppermute | solution.py:17
  42.1 4.9 %collective-permute-done.6 = bf16[4,4,16,128]{3,1,0,2:T(4,128)(2,1)S(1)} collective-permute-done((bf16[4,4,16,128]{3,1,0,2:T(4,128)(2,1)S(1)}, bf16[4,4,16,128]{3,1,0,2:T(4,128)(2,1)S(1)}, u32[]{:S(2)}, u32[]{:S(2)}) %collective-permute-start.6) | collective-permute-done | bytes 65568 | tf_op jit(solution)/shard_map/ppermute | solution.py:17
  47.0 0.2 add_convert_fusion
  47.2 5.1 %fusion.68 = f32[16,2,2,448]{3,0,2,1:T(8,128)S(1)} fusion(bf16[2,2,448,2048]{3,2,1,0:T(8,128)(2,1)} %bitcast.140, bf16[16,2048,1,1]{1,0,2,3:T(8,128)(2,1)S(1)} %reshape.201), kind=kOutput, calls=%fused_computation.67 | convolution fusion | flops 117440512 | bytes 7520256 | tf_op jit(solution)/shard_map/dot_general | solution.py:149
  52.3 0.1 collective-permute-start.7
  52.4 1.2 %collective-permute-done.7 = f32[16,2,1,448]{3,0,2,1:T(8,128)S(1)} collective-permute-done((f32[16,2,1,448]{3,0,2,1:T(8,128)S(1)}, f32[16,2,1,448]{3,0,2,1:T(8,128)S(1)}, u32[]{:S(2)}, u32[]{:S(2)}) %collective-permute-start.7) | collective-permute-done | bytes 57376 | tf_op jit(solution)/shard_map/ppermute | solution.py:17
  53.7 1.6 %collective-permute-start.8 = (f32[16,1,1,448]{3,0,2,1:T(8,128)S(1)}, f32[16,1,1,448]{3,0,2,1:T(8,128)S(1)}, u32[]{:S(2)}, u32[]{:S(2)}) collective-permute-start(f32[16,1,1,448]{3,0,2,1:T(8,128)S(1)} %slice_select_fusion.1), channel_id=1, source_target_pairs={{0,2},{2,0},{1,3},{3,1},{4,6},{6,4},{5,7},{7,5},{8,10},{10,8},{9,1... | collective-permute-start | bytes 86024 | tf_op jit(solution)/shard_map/ppermute | solution.py:17
  55.3 0.1 collective-permute-start.2
  55.3 2.3 %collective-permute-done.8 = f32[16,1,1,448]{3,0,2,1:T(8,128)S(1)} collective-permute-done((f32[16,1,1,448]{3,0,2,1:T(8,128)S(1)}, f32[16,1,1,448]{3,0,2,1:T(8,128)S(1)}, u32[]{:S(2)}, u32[]{:S(2)}) %collective-permute-start.8) | collective-permute-done | bytes 28704 | tf_op jit(solution)/shard_map/ppermute | solution.py:17
  57.7 0.6 convert_element_type.79
  58.4 2.7 %fusion.85 = (f32[1536]{0:T(1024)S(1)}, f32[1536,384]{0,1:T(8,128)S(1)}) fusion(bf16[1536,576]{1,0:T(8,128)(2,1)} %bitcast.141, bf16[384,576]{1,0:T(8,128)(2,1)S(1)} %bitcast.143, s32[1536]{0:T(1024)S(1)} %le.31, s32[384]{0:T(512)S(1)} %add.77), kind=kOutput, calls=%fused_computation.118 | convolution fusion | flops 681835008 | bytes 4584960 | tf_op jit(solution)/shard_map/dot_general | solution.py:168
  61.1 0.5 fusion.5
  61.6 0.0 copy-start.8
  61.6 1.1 %divide_convert_fusion = bf16[1536,512]{1,0:T(8,128)(2,1)S(1)} fusion(f32[1536]{0:T(1024)S(1)} %fusion.5, f32[1536,384]{0,1:T(8,128)S(1)} %get-tuple-element.17, f32[1536]{0:T(1024)S(1)} %get-tuple-element.16, s32[1536]{0:T(1024)S(1)} %le.31, s32[384]{0:T(512)S(1)} %add.77, bf16[384,576]{1,0:T(8,128)(2,1)S(1)} %bitcast.144), kind=kOutput, calls=%fused_computation | convolution fusion | flops 607911936 | bytes 4352000 | tf_op jit(solution)/shard_map/dot_general | solution.py:178
  62.8 0.4 copy-done.8
  63.2 1.9 %fusion.26 = bf16[16,12,8,128]{3,2,1,0:T(8,128)(2,1)S(1)} fusion(bf16[16,512,128]{2,1,0:T(8,128)(2,1)S(1)} %copy-done.8, bf16[96,16,512]{2,1,0:T(8,128)(2,1)S(1)} %bitcast.149), kind=kOutput, calls=%fused_computation.26 | convolution fusion | flops 201523200 | bytes 4063232 | tf_op jit(solution)/shard_map/thc,hcv->thv/dot_general | solution.py:186
  65.1 0.8 %copy.121 = bf16[16,12,8,128]{3,2,0,1:T(8,128)(2,1)} copy(bf16[16,12,8,128]{3,2,1,0:T(8,128)(2,1)S(1)} %fusion.26) | data formatting | bytes 786432 | tf_op jit(solution)/shard_map/reshape | solution.py:189
  (43 shorter events, 0.5 us)
Async XLA Ops:
  0.6 3.9 %copy-start = (bf16[16,128,512]{2,1,0:T(8,128)(2,1)S(1)}, bf16[16,128,512]{2,1,0:T(8,128)(2,1)}, u32[]{:S(2)}) copy-start(bf16[16,128,512]{2,1,0:T(8,128)(2,1)} %param.14) | copy-start | bytes 6291460
  4.5 1.5 %copy-start.1 = (bf16[4,384,576]{1,2,0:T(8,128)(2,1)S(1)}, bf16[4,384,576]{1,2,0:T(8,128)(2,1)}, u32[]{:S(2)}) copy-start(bf16[4,384,576]{1,2,0:T(8,128)(2,1)} %param.18) | copy-start | bytes 5308420
  4.9 1.5 %copy-start.4 = (bf16[4,4,576]{2,1,0:T(4,128)(2,1)S(1)}, bf16[4,4,576]{2,1,0:T(4,128)(2,1)}, u32[]{:S(2)}) copy-start(bf16[4,4,576]{2,1,0:T(4,128)(2,1)} %param.19) | copy-start | bytes 55300
  5.0 1.7 %copy-start.3 = (bf16[96,576]{1,0:T(8,128)(2,1)S(1)}, bf16[96,576]{1,0:T(8,128)(2,1)}, u32[]{:S(2)}) copy-start(bf16[96,576]{1,0:T(8,128)(2,1)} %param.12) | copy-start | bytes 331780
  5.0 2.0 %copy-start.6 = (s32[4]{0:T(128)S(1)}, s32[4]{0:T(128)}, u32[]{:S(2)}) copy-start(s32[4]{0:T(128)} %param.20) | copy-start | bytes 52
  7.8 8.5 %collective-permute-start.3 = (f32[2,4,4,16]{3,1,2,0:T(4,128)S(1)}, f32[2,4,4,16]{3,1,2,0:T(4,128)S(1)}, u32[]{:S(2)}, u32[]{:S(2)}) collective-permute-start(f32[2,4,4,16]{3,1,2,0:T(4,128)S(1)} %pad_maximum_fusion.3), channel_id=1, source_target_pairs={{0,4},{4,0},{8,12},{12,8},{1,5},{5,1},{9,13},{13,9},{2,6},{6,2},{1... | collective-permute-start | bytes 6152 | tf_op jit(solution)/shard_map/ppermute | solution.py:17
  10.9 1.5 %copy-start.2 = (bf16[4,384,576]{1,2,0:T(8,128)(2,1)S(1)}, bf16[4,384,576]{1,2,0:T(8,128)(2,1)}, u32[]{:S(2)}) copy-start(bf16[4,384,576]{1,2,0:T(8,128)(2,1)} %param.18) | copy-start | bytes 5308420
  11.0 28.5 %collective-permute-start = (bf16[1,48,576]{2,1,0:T(8,128)(2,1)S(1)}, bf16[1,48,576]{2,1,0:T(8,128)(2,1)S(1)}, u32[]{:S(2)}, u32[]{:S(2)}) collective-permute-start(bf16[1,48,576]{2,1,0:T(8,128)(2,1)S(1)} %dynamic-slice_bitcast_fusion), channel_id=1, source_target_pairs={{0,4},{4,0},{8,12},{12,8},{1,5},{5,1},{9,13},{13,9},{2,6},{6,2},{1... | collective-permute-start | bytes 165896 | tf_op jit(solution)/shard_map/ppermute | solution.py:17
  11.1 2.0 %copy-start.5 = (s32[4]{0:T(128)S(1)}, s32[4]{0:T(128)}, u32[]{:S(2)}) copy-start(s32[4]{0:T(128)} %param.13) | copy-start | bytes 52
  11.1 2.3 %slice-start = ((bf16[96,16,192]{2,1,0:T(8,128)(2,1)}), bf16[96,16,128]{2,1,0:T(8,128)(2,1)S(1)}, s32[]{:S(2)}) async-start(bf16[96,16,192]{2,1,0:T(8,128)(2,1)} %param.11), calls=%async_computation | async-start | bytes 786432 | tf_op jit(solution)/shard_map/slice | solution.py:10
  13.1 1.0 %slice-start.1 = ((bf16[96,16,192]{2,1,0:T(8,128)(2,1)}), bf16[96,16,64]{2,1,0:T(8,128)(2,1)S(1)}, s32[]{:S(2)}) async-start(bf16[96,16,192]{2,1,0:T(8,128)(2,1)} %param.11), calls=%async_computation.1 | async-start | bytes 786432 | tf_op jit(solution)/shard_map/slice | solution.py:12
  16.4 17.3 %collective-permute-start.5 = (f32[2,4,4,16]{3,1,2,0:T(4,128)S(1)}, f32[2,4,4,16]{3,1,2,0:T(4,128)S(1)}, u32[]{:S(2)}, u32[]{:S(2)}) collective-permute-start(f32[2,4,4,16]{3,1,2,0:T(4,128)S(1)} %pad_maximum_fusion.4), channel_id=1, source_target_pairs={{0,8},{4,12},{8,0},{12,4},{1,9},{5,13},{9,1},{13,5},{2,10},{6,14},... | collective-permute-start | bytes 6152 | tf_op jit(solution)/shard_map/ppermute | solution.py:17
  30.0 3.9 %copy-start.7 = (bf16[16,512,128]{2,1,0:T(8,128)(2,1)S(1)}, bf16[16,512,128]{2,1,0:T(8,128)(2,1)}, u32[]{:S(2)}) copy-start(bf16[16,512,128]{2,1,0:T(8,128)(2,1)} %param.15) | copy-start | bytes 6291460
  34.5 4.3 %collective-permute-start.4 = (bf16[4,4,16,128]{3,1,0,2:T(4,128)(2,1)S(1)}, bf16[4,4,16,128]{3,1,0,2:T(4,128)(2,1)S(1)}, u32[]{:S(2)}, u32[]{:S(2)}) collective-permute-start(bf16[4,4,16,128]{3,1,0,2:T(4,128)(2,1)S(1)} %fusion.47), channel_id=1, source_target_pairs={{0,4},{4,0},{8,12},{12,8},{1,5},{5,1},{9,13},{13,9},{2,6},{6,2},{1... | collective-permute-start | bytes 196616 | tf_op jit(solution)/shard_map/ppermute | solution.py:17
  39.0 7.9 %collective-permute-start.6 = (bf16[4,4,16,128]{3,1,0,2:T(4,128)(2,1)S(1)}, bf16[4,4,16,128]{3,1,0,2:T(4,128)(2,1)S(1)}, u32[]{:S(2)}, u32[]{:S(2)}) collective-permute-start(bf16[4,4,16,128]{3,1,0,2:T(4,128)(2,1)S(1)} %add_convert_fusion.1), channel_id=1, source_target_pairs={{0,8},{4,12},{8,0},{12,4},{1,9},{5,13},{9,1},{13,5},{2,10},{6,14},... | collective-permute-start | bytes 196616 | tf_op jit(solution)/shard_map/ppermute | solution.py:17
  39.4 15.8 %collective-permute-start.1 = (bf16[2,48,576]{2,1,0:T(8,128)(2,1)S(1)}, bf16[2,48,576]{2,1,0:T(8,128)(2,1)S(1)}, u32[]{:S(2)}, u32[]{:S(2)}) collective-permute-start(bf16[2,48,576]{2,1,0:T(8,128)(2,1)S(1)} %pad_maximum_fusion.2), channel_id=1, source_target_pairs={{0,8},{4,12},{8,0},{12,4},{1,9},{5,13},{9,1},{13,5},{2,10},{6,14},... | collective-permute-start | bytes 331784 | tf_op jit(solution)/shard_map/ppermute | solution.py:17
  52.3 1.3 %collective-permute-start.7 = (f32[16,2,1,448]{3,0,2,1:T(8,128)S(1)}, f32[16,2,1,448]{3,0,2,1:T(8,128)S(1)}, u32[]{:S(2)}, u32[]{:S(2)}) collective-permute-start(f32[16,2,1,448]{3,0,2,1:T(8,128)S(1)} %slice_select_fusion), channel_id=1, source_target_pairs={{0,1},{1,0},{2,3},{3,2},{4,5},{5,4},{6,7},{7,6},{8,9},{9,8},{10,11... | collective-permute-start | bytes 172040 | tf_op jit(solution)/shard_map/ppermute | solution.py:17
  53.7 4.0 %collective-permute-start.8 = (f32[16,1,1,448]{3,0,2,1:T(8,128)S(1)}, f32[16,1,1,448]{3,0,2,1:T(8,128)S(1)}, u32[]{:S(2)}, u32[]{:S(2)}) collective-permute-start(f32[16,1,1,448]{3,0,2,1:T(8,128)S(1)} %slice_select_fusion.1), channel_id=1, source_target_pairs={{0,2},{2,0},{1,3},{3,1},{4,6},{6,4},{5,7},{7,5},{8,10},{10,8},{9,1... | collective-permute-start | bytes 86024 | tf_op jit(solution)/shard_map/ppermute | solution.py:17
  55.3 3.0 %collective-permute-start.2 = (bf16[3,48,576]{2,1,0:T(8,128)(2,1)S(1)}, bf16[3,48,576]{2,1,0:T(8,128)(2,1)S(1)}, u32[]{:S(2)}, u32[]{:S(2)}) collective-permute-start(bf16[3,48,576]{2,1,0:T(8,128)(2,1)S(1)} %constant_dynamic-update-slice_fusion), channel_id=1, source_target_pairs={{0,1},{1,0},{2,3},{3,2},{4,5},{5,4},{6,7},{7,6},{8,9},{9,8},{10,11... | collective-permute-start | bytes 497672 | tf_op jit(solution)/shard_map/ppermute | solution.py:17
  61.6 1.6 %copy-start.8 = (bf16[16,512,128]{2,1,0:T(8,128)(2,1)S(1)}, bf16[16,512,128]{2,1,0:T(8,128)(2,1)}, u32[]{:S(2)}) copy-start(bf16[16,512,128]{2,1,0:T(8,128)(2,1)} %param.15) | copy-start | bytes 6291460

commit v2 on v0

v2 whole, which is shorter than its diff:
```python
import functools
import math

import jax
import jax.numpy as jnp
from jax import lax
from jax.experimental import pallas as pl
from jax.experimental.pallas import tpu as pltpu
from jax.sharding import PartitionSpec as P

BF16 = jnp.bfloat16
F32 = jnp.float32
LANES = 128
HIDDEN = -1e30
FLOOR = -1e29
TINY = 1e-30
MIB = 1 << 20

VMEM = pl.BlockSpec(memory_space=pltpu.VMEM)
ANY = pl.BlockSpec(memory_space=pl.ANY)
NT = (((1,), (1,)), ((), ()))


def dot(left, right):
    return jnp.dot(left, right, preferred_element_type=F32)


def dot_nt(left, right):
    return lax.dot_general(left, right, NT, preferred_element_type=F32)


def doublings(size):
    steps = []
    step = 1
    while step < size:
        steps.append(step)
        step *= 2
    assert step == size
    return steps


def swap(value, axis, step):
    size = lax.axis_size(axis)
    return lax.ppermute(value, axis, [(i, i ^ step) for i in range(size)])


def in_hbm(value):
    return pltpu.with_memory_space_constraint(value, pltpu.HBM)


def in_vmem(value):
    return pltpu.with_memory_space_constraint(value, pltpu.VMEM)


def params(mib):
    return pltpu.CompilerParams(vmem_limit_bytes=mib * MIB)


def split_three(value):
    high = value.astype(BF16).astype(F32)
    rest = value - high
    middle = rest.astype(BF16).astype(F32)
    return high, middle, (rest - middle).astype(BF16).astype(F32)


def pick_piece(pieces, piece_ids):
    picked = pieces[-1]
    for index in reversed(range(len(pieces) - 1)):
        picked = jnp.where(piece_ids == index, pieces[index], picked)
    return picked


def step_kernel(
    rate,
    order_hbm,
    length_hbm,
    dest_hbm,
    query_hbm,
    key_up_hbm,
    cache_hbm,
    latent_hbm,
    fresh_hbm,
    value_up_hbm,
    prompt_hbm,
    weight_hbm,
    out_ref,
    key_up_ref,
    value_up_ref,
    latent_ref,
    prompt_ref,
    weight_ref,
    key_pos_ref,
    query_pos_ref,
    order_ref,
    length_ref,
    dest_ref,
    query_ref,
    cache_ref,
    fresh_ref,
    nope_ref,
    row_ref,
    extra_ref,
    mixed_ref,
    sems,
):
    steps, requests, heads, width = query_ref.shape
    nope, latent = key_up_ref.shape[1:]
    span = cache_ref.shape[2]
    tokens = latent_ref.shape[0]
    pairs = steps * requests
    rows = pairs * heads
    block = steps * heads
    place = lax.axis_index("ctx")
    role = lax.axis_index("role")

    copies = []

    def fetch(source, target):
        copies.append(pltpu.make_async_copy(source, target, sems.at[len(copies)]))
        copies[-1].start()
        return copies[-1]

    query_copy = fetch(query_hbm, query_ref)
    quarter = heads // 4
    key_up_copies = [
        fetch(key_up_hbm.at[at : at + quarter], key_up_ref.at[at : at + quarter])
        for at in range(0, heads, quarter)
    ]
    latent_copy = fetch(latent_hbm, latent_ref)
    fresh_copy = fetch(fresh_hbm, fresh_ref)
    scalar_copies = [
        fetch(length_hbm, length_ref),
        fetch(dest_hbm, dest_ref),
        fetch(order_hbm, order_ref),
    ]
    cache_copy = fetch(cache_hbm, cache_ref)
    value_up_copy = fetch(value_up_hbm, value_up_ref)
    prompt_copy = fetch(prompt_hbm, prompt_ref)
    weight_copy = fetch(weight_hbm.at[: weight_ref.shape[0]], weight_ref)

    query_copy.wait()
    query = query_ref[...].astype(F32)
    query = jnp.concatenate(
        [query[:, request].reshape(block, width) for request in range(requests)], axis=0
    )
    nope_ref[...] = query[:, :nope]
    rope = query[:, nope:]
    for head in range(heads):
        if head % quarter == 0:
            key_up_copies[head // quarter].wait()
        part = nope_ref[pl.ds(head, pairs, stride=heads), :].astype(BF16)
        lifted = dot(part, key_up_ref[head]).astype(BF16).astype(F32)
        for lane in range(0, latent, LANES):
            row_ref[lane // LANES, pl.ds(head, pairs, stride=heads), :] = lifted[
                :, lane : lane + LANES
            ]
    row_parts = [row_ref[index] for index in range(latent // LANES)] + [rope]
    query_rows = jnp.concatenate(row_parts, axis=1).astype(BF16)

    latent_copy.wait()
    fresh_copy.wait()
    extra_ref[:tokens, :] = latent_ref[...].astype(F32)
    for step in range(steps):
        extra_ref[tokens + step * requests : tokens + (step + 1) * requests, :] = fresh_ref[
            step
        ].astype(F32)
    extra = extra_ref[...].astype(BF16)
    more = dot_nt(query_rows, extra)
    for copy in scalar_copies:
        copy.wait()
    column = lax.broadcasted_iota(jnp.int32, more.shape, 1)
    row = lax.broadcasted_iota(jnp.int32, more.shape, 0)
    fresh_id = column - tokens
    seen = ((column < tokens) & (row // block == dest_ref[place])) | (
        (column >= tokens)
        & (fresh_id % requests == row // block)
        & (fresh_id // requests <= row // heads % steps)
        & (place == 0)
    )
    more = jnp.where(seen, more, HIDDEN)
    position = place * span + lax.broadcasted_iota(jnp.int32, (1, span), 1)
    cache_copy.wait()
    scores = [
        jnp.where(
            position < length_ref[request],
            dot(query_rows[request * block : (request + 1) * block], cache_ref[request]),
            HIDDEN,
        )
        for request in range(requests)
    ]
    scores = jnp.concatenate(scores, axis=0)
    high = jnp.maximum(
        jnp.max(scores, axis=1, keepdims=True), jnp.max(more, axis=1, keepdims=True)
    )
    high = jnp.maximum(high, FLOOR)
    weights = jnp.exp2((scores - high) * rate)
    more = jnp.exp2((more - high) * rate)
    total = jnp.sum(weights, axis=1, keepdims=True) + jnp.sum(more, axis=1, keepdims=True)
    weights = weights.astype(BF16)
    mixed = jnp.concatenate(
        [
            dot_nt(weights[request * block : (request + 1) * block], cache_ref[request, :latent])
            for request in range(requests)
        ],
        axis=0,
    )
    mixed = mixed + dot(more.astype(BF16), extra[:, :latent])
    mixed = mixed / jnp.maximum(total, TINY)
    for lane in range(0, latent, LANES):
        mixed_ref[lane // LANES] = mixed[:, lane : lane + LANES]
    high = jnp.broadcast_to(high, (rows, LANES))
    total = jnp.broadcast_to(total, (rows, LANES))

    value_up_copy.wait()
    value_width = value_up_ref.shape[2]
    for head in range(heads):
        parts = [
            mixed_ref[index, pl.ds(head, pairs, stride=heads), :]
            for index in range(latent // LANES)
        ]
        part = jnp.concatenate(parts, axis=1).astype(BF16)
        out_ref[:, head * value_width : (head + 1) * value_width] = dot(
            part, value_up_ref[head]
        ).astype(BF16)
    lane = lax.broadcasted_iota(jnp.int32, (rows, LANES), 1)
    head_of_row = lax.broadcasted_iota(jnp.int32, (rows, LANES), 0) % heads
    pieces = split_three(high) + split_three(total)
    packed = pick_piece(pieces, lane // heads)
    packed = jnp.where((lane % heads == head_of_row) & (lane < 6 * heads), packed, 0.0)
    packed = jnp.sum(packed.reshape(pairs, heads, LANES), axis=1)
    out_ref[:, heads * value_width :] = packed.astype(BF16)

    size = lax.axis_size("ctx")
    half = tokens // lax.axis_size("role")
    key_id = lax.broadcasted_iota(jnp.int32, key_pos_ref.shape, 1)
    near = 2 * tokens
    far = (size - 2) * half
    in_other = key_id >= near + far
    local = key_id - near - jnp.where(in_other, far, 0)
    is_near = key_id < near
    slot = jnp.where(is_near, key_id // tokens, 2 + local // half)
    base = jnp.where(
        is_near, key_id % tokens, local % half + half * jnp.where(in_other, 1 - role, role)
    )
    for index in range(size):
        base = base + jnp.where(slot == index, order_ref[place ^ index] * tokens, 0)
    key_pos_ref[...] = base
    query_pos_ref[...] = order_ref[place] * tokens + lax.broadcasted_iota(
        jnp.int32, query_pos_ref.shape, 0
    )
    prompt_copy.wait()
    weight_copy.wait()


def step_part(
    rate,
    early_rows,
    block_order,
    cache_length,
    block_dest,
    step_query,
    key_up,
    cache,
    latent,
    fresh,
    value_up,
    prompt_query,
    out_weight,
):
    steps, requests, heads, width = step_query.shape
    nope, latent_width = key_up.shape[1:]
    full = cache.shape[1]
    tokens = latent.shape[0]
    pairs = steps * requests
    rows = pairs * heads
    shape = pltpu.VMEM
    return pl.pallas_call(
        functools.partial(step_kernel, rate),
        out_shape=(
            shape((pairs, heads * value_up.shape[2] + LANES), BF16),
            shape(key_up.shape, BF16),
            shape(value_up.shape, BF16),
            shape(latent.shape, BF16),
            shape(prompt_query.shape, BF16),
            shape((early_rows, out_weight.shape[1]), BF16),
            shape((8, tokens * lax.axis_size("ctx")), jnp.int32),
            shape((tokens, LANES), jnp.int32),
        ),
        in_specs=[ANY] * 11,
        out_specs=[VMEM] * 8,
        scratch_shapes=[
            pltpu.SMEM(block_order.shape, jnp.int32),
            pltpu.SMEM(cache_length.shape, jnp.int32),
            pltpu.SMEM(block_dest.shape, jnp.int32),
            pltpu.VMEM(step_query.shape, BF16),
            pltpu.VMEM(cache.shape, BF16),
            pltpu.VMEM(fresh.shape, BF16),
            pltpu.VMEM((rows, nope), F32),
            pltpu.VMEM((latent_width // LANES, rows, LANES), F32),
            pltpu.VMEM((tokens + pairs, full), F32),
            pltpu.VMEM((latent_width // LANES, rows, LANES), F32),
            pltpu.SemaphoreType.DMA((14,)),
        ],
        compiler_params=params(24),
        cost_estimate=pl.CostEstimate(flops=10**9, bytes_accessed=10**7, transcendentals=10**5),
        name="step_part",
    )(
        *(
            in_hbm(value)
            for value in (
                block_order,
                cache_length,
                block_dest,
                step_query,
                key_up,
                cache,
                latent,
                fresh,
                value_up,
                prompt_query,
                out_weight,
            )
        )
    )


def read_stats(packed, heads):
    def piece(index):
        if index == 0:
            return packed
        return pltpu.roll(packed, LANES - index * heads, 1)

    return piece(0) + piece(1) + piece(2), piece(3) + piece(4) + piece(5)


def merge(rate, first_ref, second_ref, heads):
    split = first_ref.shape[1] - LANES
    value_width = split // heads
    high_a, total_a = read_stats(first_ref[:, split:].astype(F32), heads)
    high_b, total_b = read_stats(second_ref[:, split:].astype(F32), heads)
    high = jnp.maximum(high_a, high_b)
    share_a = total_a * jnp.exp2((high_a - high) * rate)
    share_b = total_b * jnp.exp2((high_b - high) * rate)
    total = share_a + share_b
    safe = jnp.maximum(total, TINY)
    share_a = share_a / safe
    share_b = share_b / safe
    merged = []
    for head in range(heads):
        at = slice(head * value_width, (head + 1) * value_width)
        merged.append(
            (
                first_ref[:, at].astype(F32) * share_a[:, head : head + 1]
                + second_ref[:, at].astype(F32) * share_b[:, head : head + 1]
            ).astype(BF16)
        )
    return merged, high, total


def merge_kernel(rate, heads, first_ref, second_ref, out_ref):
    merged, high, total = merge(rate, first_ref, second_ref, heads)
    value_width = merged[0].shape[1]
    for head in range(heads):
        out_ref[:, head * value_width : (head + 1) * value_width] = merged[head]
    pieces = split_three(high) + split_three(total)
    lane = lax.broadcasted_iota(jnp.int32, high.shape, 1)
    moved = [p if i == 0 else pltpu.roll(p, i * heads, 1) for i, p in enumerate(pieces)]
    packed = jnp.where(lane < 6 * heads, pick_piece(moved, lane // heads), 0.0)
    out_ref[:, heads * value_width :] = packed.astype(BF16)


def merge_parts(rate, heads, first, second):
    return pl.pallas_call(
        functools.partial(merge_kernel, rate, heads),
        out_shape=pltpu.VMEM(first.shape, BF16),
        in_specs=[VMEM] * 2,
        out_specs=VMEM,
        compiler_params=params(2),
        cost_estimate=pl.CostEstimate(flops=10**5, bytes_accessed=2 * 10**5, transcendentals=10**4),
        name="merge_parts",
    )(in_vmem(first), in_vmem(second))


def join_kernel(half, first_ref, second_ref, out_ref):
    rows = first_ref.shape[0]
    if half:
        role = lax.axis_index("role")
        for index in range(rows // half):

            @pl.when(role == index)
            def _():
                at = slice(index * half, (index + 1) * half)
                out_ref[:half, :] = first_ref[at, :]
                out_ref[half:, :] = second_ref[at, :]
    else:
        out_ref[:rows, :] = first_ref[...]
        out_ref[rows:, :] = second_ref[...]


def join_rows(half, first, second):
    rows, full = first.shape
    return pl.pallas_call(
        functools.partial(join_kernel, half),
        out_shape=pltpu.VMEM((2 * (half or rows), full), BF16),
        in_specs=[VMEM] * 2,
        out_specs=VMEM,
        compiler_params=params(1),
        cost_estimate=pl.CostEstimate(flops=10**4, bytes_accessed=2 * 10**5, transcendentals=0),
        name="join_rows",
    )(in_vmem(first), in_vmem(second))


def finish_kernel(
    rate, heads, parts, first_ref, second_ref, early_ref, late_ref, keep_ref, give_ref
):
    merged, _, _ = merge(rate, first_ref, second_ref, heads)
    rows = jnp.concatenate(merged, axis=1)
    early = early_ref.shape[0]
    product = dot(rows[:, :early], early_ref[...]) + dot(rows[:, early:], late_ref[...])
    width = product.shape[1] // parts
    upper = lax.axis_index("role") == 1
    for index in range(parts // 2):
        low, high = (
            product[:, part * width : (part + 1) * width] for part in (2 * index, 2 * index + 1)
        )
        keep_ref[index] = jnp.where(upper, high, low)
        give_ref[index] = jnp.where(upper, low, high).astype(BF16)


def finish_steps(rate, heads, parts, first, second, early, late):
    pairs = first.shape[0]
    shape = (parts // 2, pairs, early.shape[1] // parts)
    return pl.pallas_call(
        functools.partial(finish_kernel, rate, heads, parts),
        out_shape=(pltpu.VMEM(shape, F32), pltpu.VMEM(shape, BF16)),
        in_specs=[VMEM] * 4,
        out_specs=[VMEM] * 2,
        compiler_params=params(4),
        cost_estimate=pl.CostEstimate(
            flops=5 * 10**8, bytes_accessed=8 * 10**6, transcendentals=10**4
        ),
        name="finish_steps",
    )(*(in_vmem(v) for v in (first, second, early, late)))


def fold_kernel(step, keep_ref, received_ref, new_keep_ref, give_ref):
    share = keep_ref[...] + received_ref[...].astype(F32)
    middle = share.shape[0] // 2
    upper = lax.axis_index("head") & step != 0
    new_keep_ref[...] = jnp.where(upper, share[middle:], share[:middle])
    give_ref[...] = jnp.where(upper, share[:middle], share[middle:]).astype(BF16)


def fold_steps(step, keep, received):
    shape = (keep.shape[0] // 2, *keep.shape[1:])
    return pl.pallas_call(
        functools.partial(fold_kernel, step),
        out_shape=(pltpu.VMEM(shape, F32), pltpu.VMEM(shape, BF16)),
        in_specs=[VMEM] * 2,
        out_specs=[VMEM] * 2,
        compiler_params=params(1),
        cost_estimate=pl.CostEstimate(flops=10**5, bytes_accessed=10**5, transcendentals=0),
        name="fold_steps",
    )(in_vmem(keep), in_vmem(received))


def sum_kernel(keep_ref, received_ref, out_ref):
    share = keep_ref[0] + received_ref[0].astype(F32)
    steps, requests, _ = out_ref.shape
    for step in range(steps):
        rows = [share[at : at + 1] for at in range(step, steps * requests, steps)]
        out_ref[step] = jnp.concatenate(rows, axis=0).astype(BF16)


def sum_steps(steps, keep, received):
    pairs, width = keep.shape[1:]
    return pl.pallas_call(
        sum_kernel,
        out_shape=jax.ShapeDtypeStruct((steps, pairs // steps, width), BF16),
        in_specs=[VMEM] * 2,
        out_specs=VMEM,
        compiler_params=params(1),
        cost_estimate=pl.CostEstimate(flops=10**5, bytes_accessed=10**5, transcendentals=0),
        name="sum_steps",
    )(in_vmem(keep), in_vmem(received))


def lift_kernel(query_ref, key_up_ref, weight_hbm, row_ref, weight_ref, nope_ref, rope_ref, sem):
    tokens, heads, width = query_ref.shape
    nope, latent = key_up_ref.shape[1:]
    skipped = weight_hbm.shape[0] - weight_ref.shape[0]
    copy = pltpu.make_async_copy(weight_hbm.at[skipped:], weight_ref, sem)
    copy.start()
    nope_ref[...] = query_ref[:, :, :nope].astype(F32).reshape(tokens * heads, nope)
    rope_ref[:, : width - nope] = (
        query_ref[:, :, nope:].astype(F32).reshape(tokens * heads, width - nope)
    )
    for head in range(heads):
        at = slice(head * tokens, (head + 1) * tokens)
        part = nope_ref[pl.ds(head, tokens, stride=heads), :].astype(BF16)
        row_ref[at, :latent] = dot(part, key_up_ref[head]).astype(BF16)
        rope = rope_ref[pl.ds(head, tokens, stride=heads), :]
        row_ref[at, latent:] = rope[:, : width - nope].astype(BF16)
    copy.wait()


def prompt_lift(prompt_query, key_up, out_weight, late_rows):
    tokens, heads, width = prompt_query.shape
    nope, latent_width = key_up.shape[1:]
    rows = tokens * heads
    shape = pltpu.VMEM
    return pl.pallas_call(
        lift_kernel,
        out_shape=(
            shape((rows, latent_width + width - nope), BF16),
            shape((late_rows, out_weight.shape[1]), BF16),
        ),
        in_specs=[VMEM] * 2 + [ANY],
        out_specs=[VMEM] * 2,
        scratch_shapes=[
            pltpu.VMEM((rows, nope), F32),
            pltpu.VMEM((rows, LANES), F32),
            pltpu.SemaphoreType.DMA,
        ],
        compiler_params=params(8),
        cost_estimate=pl.CostEstimate(
            flops=3 * 10**8, bytes_accessed=6 * 10**6, transcendentals=0
        ),
        name="prompt_lift",
    )(in_vmem(prompt_query), in_vmem(key_up), in_hbm(out_weight))


def attend(rate, group, heads, row_ref, key_ref, key_pos_ref, query_pos_ref, value_up_ref, put):
    tokens = query_pos_ref.shape[0]
    count = key_ref.shape[0]
    latent = value_up_ref.shape[1]
    visible = (key_pos_ref[:1, :] <= query_pos_ref[:, :1])[None]
    for first in range(heads.start, heads.stop, group):
        at = slice(first * tokens, (first + group) * tokens)
        scores = dot_nt(row_ref[at, :], key_ref[...])
        scores = jnp.where(visible, scores.reshape(group, tokens, count), HIDDEN)
        scores = scores.reshape(group * tokens, count)
        weights = jnp.exp2((scores - jnp.max(scores, axis=1, keepdims=True)) * rate)
        total = jnp.sum(weights, axis=1, keepdims=True)
        mixed = dot(weights.astype(BF16), key_ref[:, :latent])
        mixed = (mixed / total).astype(BF16)
        for index in range(group):
            put(
                first + index,
                dot(
                    mixed[index * tokens : (index + 1) * tokens], value_up_ref[first + index]
                ).astype(BF16),
            )


def front_kernel(rate, group, heads, skipped, *refs):
    row_ref, *part_refs = refs[: 1 + len(skipped)]
    key_pos_ref, query_pos_ref, value_up_ref, out_ref, key_ref = refs[1 + len(skipped) :]
    at = 0
    for part_ref, skip in zip(part_refs, skipped):
        count = part_ref.shape[0] - skip
        key_ref[at : at + count, :] = part_ref[skip:, :]
        at += count
    assert at == key_ref.shape[0]
    width = value_up_ref.shape[2]

    def put(head, value):
        out_ref[:, head * width : (head + 1) * width] = value

    attend(
        rate, group, heads, row_ref, key_ref, key_pos_ref, query_pos_ref, value_up_ref, put
    )


def prompt_front(rate, group, heads, rows, parts, key_pos, query_pos, value_up):
    tokens = query_pos.shape[0]
    shape = pltpu.VMEM
    return pl.pallas_call(
        functools.partial(front_kernel, rate, group, heads, [skip for _, skip in parts]),
        out_shape=(
            shape((tokens, len(heads) * value_up.shape[2]), BF16),
            shape((key_pos.shape[1], rows.shape[1]), BF16),
        ),
        in_specs=[VMEM] * (4 + len(parts)),
        out_specs=[VMEM] * 2,
        compiler_params=params(16),
        cost_estimate=pl.CostEstimate(
            flops=8 * 10**8, bytes_accessed=6 * 10**6, transcendentals=3 * 10**5
        ),
        name="prompt_front",
    )(*(in_vmem(v) for v in (rows, *(part for part, _ in parts), key_pos, query_pos, value_up)))


def back_kernel(
    rate,
    group,
    heads,
    row_ref,
    key_ref,
    key_pos_ref,
    query_pos_ref,
    value_up_ref,
    front_ref,
    out_hbm,
    back_ref,
    sems,
):
    width = value_up_ref.shape[2]
    edge = heads.start * width
    copies = [pltpu.make_async_copy(front_ref, out_hbm.at[:, :edge], sems.at[0])]
    copies[0].start()

    def put(head, value):
        at = (head - heads.start) * width
        back_ref[:, at : at + width] = value
        if (head - heads.start + 1) % group == 0:
            start = at + width - group * width
            copies.append(
                pltpu.make_async_copy(
                    back_ref.at[:, start : at + width],
                    out_hbm.at[:, edge + start : edge + at + width],
                    sems.at[len(copies)],
                )
            )
            copies[-1].start()

    attend(
        rate, group, heads, row_ref, key_ref, key_pos_ref, query_pos_ref, value_up_ref, put
    )
    for copy in copies:
        copy.wait()


def prompt_back(rate, group, heads, rows, keys, key_pos, query_pos, value_up, front):
    tokens = query_pos.shape[0]
    width = value_up.shape[2]
    return pl.pallas_call(
        functools.partial(back_kernel, rate, group, heads),
        out_shape=jax.ShapeDtypeStruct((tokens, heads.stop * width), BF16),
        in_specs=[VMEM] * 6,
        out_specs=ANY,
        scratch_shapes=[
            pltpu.VMEM((tokens, len(heads) * width), BF16),
            pltpu.SemaphoreType.DMA((1 + len(heads) // group,)),
        ],
        compiler_params=params(16),
        cost_estimate=pl.CostEstimate(
            flops=8 * 10**8, bytes_accessed=6 * 10**6, transcendentals=3 * 10**5
        ),
        name="prompt_back",
    )(*(in_vmem(v) for v in (rows, keys, key_pos, query_pos, value_up, front)))


def per_device(
    prompt_query,
    prompt_latent,
    block_order,
    key_up,
    value_up,
    out_weight,
    step_query,
    cache_latent,
    step_latent,
    cache_length,
    block_dest,
):
    tokens, heads, width = prompt_query.shape
    rate = width ** (-0.5) * math.log2(math.e)
    context_size = lax.axis_size("ctx")
    steps = step_query.shape[0]
    head_size = lax.axis_size("head")
    role_size = lax.axis_size("role")
    contracted = out_weight.shape[0]
    early_rows = contracted // 2

    rounds = doublings(context_size)
    near = swap(prompt_latent, "ctx", rounds[0])
    (
        running,
        key_up,
        value_up,
        latent,
        prompt_query,
        early_weight,
        key_pos,
        query_pos,
    ) = step_part(
        rate,
        early_rows,
        block_order,
        cache_length,
        block_dest,
        step_query,
        key_up,
        jnp.swapaxes(cache_latent, 1, 2),
        prompt_latent,
        step_latent,
        value_up,
        prompt_query,
        out_weight,
    )
    rows, late_weight = prompt_lift(prompt_query, key_up, out_weight, contracted - early_rows)
    sent = join_rows(tokens // role_size, latent, near)
    for step in rounds:
        far_running = swap(running, "ctx", step)
        if step == rounds[-1]:
            break
        running = merge_parts(rate, heads, running, far_running)
    for step in rounds[1:]:
        received = swap(sent, "ctx", step)
        if step == rounds[-1]:
            break
        sent = join_rows(None, sent, received)
    keep, give = finish_steps(
        rate, heads, head_size * role_size, running, far_running, early_weight, late_weight
    )
    same = [(sent, 2 * tokens // role_size), (received, 0)]
    same = [(part, skip) for part, skip in same if part.shape[0] > skip]
    parts = [(latent, 0), (near, 0)] + same
    parts += [(swap(part, "role", 1), skip) for part, skip in same]
    group = 4 if heads % 8 == 0 else 1
    middle = heads // 2
    front, keys = prompt_front(
        rate, group, range(middle), rows, parts, key_pos, query_pos, value_up
    )
    prompt_out = prompt_back(
        rate, group, range(middle, heads), rows, keys, key_pos, query_pos, value_up, front
    )
    partial = swap(give, "role", 1)
    for step in reversed(doublings(head_size)):
        keep, give = fold_steps(step, keep, partial)
        partial = swap(give, "head", step)
    step_out = sum_steps(steps, keep, partial)
    return (prompt_out, step_out)


def solution(mesh):
    return jax.shard_map(
        per_device,
        mesh=mesh,
        in_specs=(
            P(("groups", "ctx"), ("head", "role"), None),
            P(("groups", "ctx"), None),
            P("groups"),
            P(("head", "role"), None, None),
            P(("head", "role"), None, None),
            P(("head", "role"), "ctx"),
            P(None, "groups", ("head", "role"), None),
            P("groups", "ctx", None),
            P(None, "groups", None),
            P("groups"),
            P("groups"),
        ),
        out_specs=(
            P(("groups", "ctx"), ("head", "role")),
            P(None, "groups", ("ctx", "head", "role")),
        ),
        check_vma=False,
    )
```

time: 113 us -> 32.6 us (0.29)
  blocking collectives: 39.8 us -> 0 us
  matrix products: 19.1 us -> 0 us
  between operations: 15 us -> 0.68 us
  local copies, waits for them, and re-layouts: 14.3 us -> 0 us
  Pallas kernels: 0 us -> 13 us
  waiting for transfers between devices: 20.2 us -> 8.04 us
  starting transfers between devices: 0.08 us -> 10.7 us
  other arithmetic: 4.26 us -> 0 us
    dot_general x13 -> x0, matrix products: 19.1 us -> none  [the longest x3 4.56 us: partial_softmax(): jnp.einsum(form, weights.astype(jnp.bfloat16), values, preferred_element_...]
    unnamed x3 -> x0, waiting for transfers between devices: 19.1 us -> none
    all_gather x1 -> x0, blocking collectives: 16.9 us -> none  [per_device(): shard_rows = lax.all_gather(prompt_latent, 'ctx', axis=0, tiled=True)]
    pmax x1 -> x0, blocking collectives: 13.7 us -> none  [per_device(): peak_score = lax.pmax(highest, 'ctx')]
    pallas_call x0 -> x9, Pallas kernels: none -> 13 us  [the longest x1 4.29 us: step_part(): pl.pallas_call(functools.partial(step_kernel, rate), out_shape=(shape((pa...]
    unnamed x20 -> x0, local copies, waits for them, and re-layouts: 10.8 us -> none
    ppermute x0 -> x7, starting transfers between devices: none -> 10.7 us  [swap(): return lax.ppermute(value, axis, [(i, i ^ step) for i in range(size)])]
    psum x1 -> x0, blocking collectives: 9.23 us -> none  [per_device(): lax.psum((totals * factor).astype(jnp.bfloat16), 'ctx').astype(jnp.float32)]
  transfers between devices with their start and end apart: 2 -> 7, of which waited for: 2 -> 4; matrix products, arithmetic and copies ran while one was open for 10% -> 0% of each run, Pallas kernels for 0% -> 27%
where the time goes in v2:
time: 32.6 us; the launch traced here: 32.4 us
  Pallas kernels  13 us (40%)
  starting transfers between devices  10.7 us (33%)
  waiting for transfers between devices  8.04 us (25%)
  between operations  0.68 us (2%)
    ppermute x7, starting transfers between devices, swap(): return lax.ppermute(value, axis, [(i, i ^ step) for i in range(size)])  10.7 us
    ppermute x7, waiting for transfers between devices, swap(): return lax.ppermute(value, axis, [(i, i ^ step) for i in range(size)])  8.04 us
    pallas_call x1, Pallas kernels, step_part(): pl.pallas_call(functools.partial(step_kernel, rate), out_shape=(shape((pa...  4.29 us
    pallas_call x1, Pallas kernels, prompt_back(): pl.pallas_call(functools.partial(back_kernel, rate, group, heads), out_sh...  2.49 us
    pallas_call x1, Pallas kernels, prompt_lift(): pl.pallas_call(lift_kernel, out_shape=(shape((rows, latent_width + width...  2.05 us
    pallas_call x1, Pallas kernels, prompt_front(): pl.pallas_call(functools.partial(front_kernel, rate, group, heads, [skip...  1.85 us
    pallas_call x1, Pallas kernels, finish_steps(): pl.pallas_call(functools.partial(finish_kernel, rate, heads, parts), out_...  1.34 us
  transfers between devices with their start and end apart: 7, of which 4 were waited for; matrix products, arithmetic and copies ran while one was open for 0% of the time, Pallas kernels for 27%

profile of v2, /device:TPU:0, one launch (start us, length us, event | category | flops | bytes accessed | tf_op | source)
XLA Modules:
  0.0 32.4 jit_solution(8620897687091645633)
XLA Ops:
  0.6 3.1 %collective-permute-start = (bf16[96,576]{1,0:T(8,128)(2,1)}, bf16[96,576]{1,0:T(8,128)(2,1)S(1)}, u32[]{:S(2)}, u32[]{:S(2)}) collective-permute-start(bf16[96,576]{1,0:T(8,128)(2,1)} %latent_hbm.1), channel_id=1, source_target_pairs={{0,4},{4,0},{8,12},{12,8},{1,5},{5,1},{9,13},{13,9},{2,6},{6,2},{1... | collective-permute-start | bytes 331784 | tf_op jit(solution)/shard_map/ppermute | solution.py:44
  3.8 4.3 %step_part.1 = (bf16[16,2176]{1,0:T(8,128)(2,1)S(1)}, bf16[16,128,512]{2,1,0:T(8,128)(2,1)S(1)}, bf16[16,512,128]{2,1,0:T(8,128)(2,1)S(1)}, bf16[96,576]{1,0:T(8...) custom-call(s32[4]{0:T(128)} %order_hbm.1, ...), custom_call_target="tpu_custom_call" | custom-call | flops 1000000000 | bytes 10000000 | tf_op jit(solution)/shard_map/step_part/pallas_call | solution.py:277
  8.1 0.1 collective-permute-start.3
  8.1 0.0 collective-permute-done.second_ref.refs_2_
  8.2 3.1 %collective-permute-start.1 = (bf16[96,576]{1,0:T(8,128)(2,1)S(1)}, bf16[96,576]{1,0:T(8,128)(2,1)S(1)}, u32[]{:S(2)}, u32[]{:S(2)}) collective-permute-start(bf16[96,576]{1,0:T(8,128)(2,1)S(1)} %join_rows.1), channel_id=1, source_target_pairs={{0,8},{4,12},{8,0},{12,4},{1,9},{5,13},{9,1},{13,5},{2,10},{6,14},... | collective-permute-start | bytes 331784 | tf_op jit(solution)/shard_map/ppermute | solution.py:44
  11.2 2.5 %collective-permute-done.3.second_ref = bf16[16,2176]{1,0:T(8,128)(2,1)S(1)} collective-permute-done((bf16[16,2176]{1,0:T(8,128)(2,1)S(1)}, bf16[16,2176]{1,0:T(8,128)(2,1)S(1)}, u32[]{:S(2)}, u32[]{:S(2)}) %collective-permute-start.3) | collective-permute-done | bytes 69664 | tf_op jit(solution)/shard_map/ppermute | solution.py:44
  13.8 0.3 merge_parts.1.first_ref
  14.1 2.0 %collective-permute-start.4 = (bf16[16,2176]{1,0:T(8,128)(2,1)S(1)}, bf16[16,2176]{1,0:T(8,128)(2,1)S(1)}, u32[]{:S(2)}, u32[]{:S(2)}) collective-permute-start(bf16[16,2176]{1,0:T(8,128)(2,1)S(1)} %merge_parts.1.first_ref), channel_id=1, source_target_pairs={{0,8},{4,12},{8,0},{12,4},{1,9},{5,13},{9,1},{13,5},{2,10},{6,14},... | collective-permute-start | bytes 208904 | tf_op jit(solution)/shard_map/ppermute | solution.py:44
  16.0 2.8 %collective-permute-done.1.refs_3_ = bf16[96,576]{1,0:T(8,128)(2,1)S(1)} collective-permute-done((bf16[96,576]{1,0:T(8,128)(2,1)S(1)}, bf16[96,576]{1,0:T(8,128)(2,1)S(1)}, u32[]{:S(2)}, u32[]{:S(2)}) %collective-permute-start.1) | collective-permute-done | bytes 110624 | tf_op jit(solution)/shard_map/ppermute | solution.py:44
  18.8 0.0 collective-permute-start.2
  18.8 2.1 %prompt_lift.1 = (bf16[1536,576]{1,0:T(8,128)(2,1)S(1)}, bf16[1024,1792]{1,0:T(8,128)(2,1)S(1)}) custom-call(bf16[96,16,192]{2,1,0:T(8,128)(2,1)S(1)} %get-tuple-element.18.query_ref, bf16[16,128,512]{2,1,0:T(8,128)(2,1)S(1)} %get-tuple-element.19.key_up_ref, bf16[2048,1792]{1,0:T(8,128)(2,1)} %weight_hbm.3), custom_call_target="tpu_custom_call" | custom-call | flops 300000000 | bytes 6000000 | tf_op jit(solution)/shard_map/prompt_lift/pallas_call | solution.py:512
  20.9 0.0 collective-permute-done.4.second_ref
  20.9 1.3 %finish_steps.1 = (f32[2,16,448]{2,1,0:T(8,128)S(1)}, bf16[2,16,448]{2,1,0:T(8,128)(2,1)S(1)}) custom-call(bf16[16,2176]{1,0:T(8,128)(2,1)S(1)} %merge_parts.1.first_ref, bf16[16,2176]{1,0:T(8,128)(2,1)S(1)} %collective-permute-done.4.second_ref, bf16[1024,1792]{1,0:T(8,128)(2,1)S(1)} %get-tuple-element.28.early_ref, ...), custom_call_target="tpu_custom_call" | custom-call | flops 500000000 | bytes 8000000 | tf_op jit(solution)/shard_map/finish_steps/pallas_call | solution.py:433
  22.2 0.5 %collective-permute-start.5 = (bf16[2,16,448]{2,1,0:T(8,128)(2,1)S(1)}, bf16[2,16,448]{2,1,0:T(8,128)(2,1)S(1)}, u32[]{:S(2)}, u32[]{:S(2)}) collective-permute-start(bf16[2,16,448]{2,1,0:T(8,128)(2,1)S(1)} %get-tuple-element.31), channel_id=1, source_target_pairs={{0,1},{1,0},{2,3},{3,2},{4,5},{5,4},{6,7},{7,6},{8,9},{9,8},{10,11... | collective-permute-start | bytes 86024 | tf_op jit(solution)/shard_map/ppermute | solution.py:44
  22.8 0.9 %collective-permute-done.5.received_ref = bf16[2,16,448]{2,1,0:T(8,128)(2,1)S(1)} collective-permute-done((bf16[2,16,448]{2,1,0:T(8,128)(2,1)S(1)}, bf16[2,16,448]{2,1,0:T(8,128)(2,1)S(1)}, u32[]{:S(2)}, u32[]{:S(2)}) %collective-permute-start.5) | collective-permute-done | bytes 28704 | tf_op jit(solution)/shard_map/ppermute | solution.py:44
  23.6 2.0 %collective-permute-start.6 = (bf16[1,16,448]{2,1,0:T(8,128)(2,1)S(1)}, bf16[1,16,448]{2,1,0:T(8,128)(2,1)S(1)}, u32[]{:S(2)}, u32[]{:S(2)}) collective-permute-start(bf16[1,16,448]{2,1,0:T(8,128)(2,1)S(1)} %get-tuple-element.33), channel_id=1, source_target_pairs={{0,2},{2,0},{1,3},{3,1},{4,6},{6,4},{5,7},{7,5},{8,10},{10,8},{9,1... | collective-permute-start | bytes 43016 | tf_op jit(solution)/shard_map/ppermute | solution.py:44
  25.6 1.8 %collective-permute-done.6.received_ref = bf16[1,16,448]{2,1,0:T(8,128)(2,1)S(1)} collective-permute-done((bf16[1,16,448]{2,1,0:T(8,128)(2,1)S(1)}, bf16[1,16,448]{2,1,0:T(8,128)(2,1)S(1)}, u32[]{:S(2)}, u32[]{:S(2)}) %collective-permute-start.6) | collective-permute-done | bytes 14368 | tf_op jit(solution)/shard_map/ppermute | solution.py:44
  27.4 0.6 %sum_steps.1 = bf16[4,4,448]{2,1,0:T(4,128)(2,1)} custom-call(f32[1,16,448]{2,1,0:T(8,128)S(1)} %get-tuple-element.32.keep_ref, bf16[1,16,448]{2,1,0:T(8,128)(2,1)S(1)} %collective-permute-done.6.received_ref), custom_call_target="tpu_custom_call" | custom-call | flops 100000 | bytes 100000 | tf_op jit(solution)/shard_map/sum_steps/pallas_call | solution.py:477
  28.1 0.0 collective-permute-done.2.refs_4_
  28.1 1.8 %prompt_front.1 = (bf16[96,1024]{1,0:T(8,128)(2,1)S(1)}, bf16[384,576]{1,0:T(8,128)(2,1)S(1)}) custom-call(bf16[1536,576]{1,0:T(8,128)(2,1)S(1)} %get-tuple-element.20.refs_0_.row_ref, bf16[96,576]{1,0:T(8,128)(2,1)S(1)} %get-tuple-element.21.first_ref.refs_1_, bf16[96,576]{1,0:T(8,128)(2,1)S(1)} %collective-permute-done.second_ref.refs_2_, ...), custom_call_target="tpu_custom_call" | custom-call | flops 800000000 | bytes 6000000 | tf_op jit(solution)/shard_map/prompt_front/pallas_call | solution.py:578
  29.9 2.5 %prompt_back.1 = bf16[96,2048]{1,0:T(8,128)(2,1)} custom-call(bf16[1536,576]{1,0:T(8,128)(2,1)S(1)} %get-tuple-element.20.refs_0_.row_ref, bf16[384,576]{1,0:T(8,128)(2,1)S(1)} %get-tuple-element.25.key_ref, s32[8,384]{1,0:T(8,128)S(1)} %get-tuple-element.22.refs_5_.key_pos_ref, s32[96,128]{1,0:T(8,128)S(1)} %get-tuple-element.23.refs_6_.query_pos_ref, ...), custom_call_target="tpu_custom_call" | custom-call | flops 800000000 | bytes 6000000 | tf_op jit(solution)/shard_map/prompt_back/pallas_call | solution.py:637
  (2 shorter events, 0.0 us)
Async XLA Ops:
  0.6 7.5 %collective-permute-start = (bf16[96,576]{1,0:T(8,128)(2,1)}, bf16[96,576]{1,0:T(8,128)(2,1)S(1)}, u32[]{:S(2)}, u32[]{:S(2)}) collective-permute-start(bf16[96,576]{1,0:T(8,128)(2,1)} %latent_hbm.1), channel_id=1, source_target_pairs={{0,4},{4,0},{8,12},{12,8},{1,5},{5,1},{9,13},{13,9},{2,6},{6,2},{1... | collective-permute-start | bytes 331784 | tf_op jit(solution)/shard_map/ppermute | solution.py:44
  8.1 5.7 %collective-permute-start.3 = (bf16[16,2176]{1,0:T(8,128)(2,1)S(1)}, bf16[16,2176]{1,0:T(8,128)(2,1)S(1)}, u32[]{:S(2)}, u32[]{:S(2)}) collective-permute-start(bf16[16,2176]{1,0:T(8,128)(2,1)S(1)} %get-tuple-element.27.first_ref), channel_id=1, source_target_pairs={{0,4},{4,0},{8,12},{12,8},{1,5},{5,1},{9,13},{13,9},{2,6},{6,2},{1... | collective-permute-start | bytes 208904 | tf_op jit(solution)/shard_map/ppermute | solution.py:44
  8.2 10.6 %collective-permute-start.1 = (bf16[96,576]{1,0:T(8,128)(2,1)S(1)}, bf16[96,576]{1,0:T(8,128)(2,1)S(1)}, u32[]{:S(2)}, u32[]{:S(2)}) collective-permute-start(bf16[96,576]{1,0:T(8,128)(2,1)S(1)} %join_rows.1), channel_id=1, source_target_pairs={{0,8},{4,12},{8,0},{12,4},{1,9},{5,13},{9,1},{13,5},{2,10},{6,14},... | collective-permute-start | bytes 331784 | tf_op jit(solution)/shard_map/ppermute | solution.py:44
  14.1 6.8 %collective-permute-start.4 = (bf16[16,2176]{1,0:T(8,128)(2,1)S(1)}, bf16[16,2176]{1,0:T(8,128)(2,1)S(1)}, u32[]{:S(2)}, u32[]{:S(2)}) collective-permute-start(bf16[16,2176]{1,0:T(8,128)(2,1)S(1)} %merge_parts.1.first_ref), channel_id=1, source_target_pairs={{0,8},{4,12},{8,0},{12,4},{1,9},{5,13},{9,1},{13,5},{2,10},{6,14},... | collective-permute-start | bytes 208904 | tf_op jit(solution)/shard_map/ppermute | solution.py:44
  18.8 9.3 %collective-permute-start.2 = (bf16[96,576]{1,0:T(8,128)(2,1)S(1)}, bf16[96,576]{1,0:T(8,128)(2,1)S(1)}, u32[]{:S(2)}, u32[]{:S(2)}) collective-permute-start(bf16[96,576]{1,0:T(8,128)(2,1)S(1)} %collective-permute-done.1.refs_3_), channel_id=1, source_target_pairs={{0,1},{1,0},{2,3},{3,2},{4,5},{5,4},{6,7},{7,6},{8,9},{9,8},{10,11... | collective-permute-start | bytes 331784 | tf_op jit(solution)/shard_map/ppermute | solution.py:44
  22.2 1.4 %collective-permute-start.5 = (bf16[2,16,448]{2,1,0:T(8,128)(2,1)S(1)}, bf16[2,16,448]{2,1,0:T(8,128)(2,1)S(1)}, u32[]{:S(2)}, u32[]{:S(2)}) collective-permute-start(bf16[2,16,448]{2,1,0:T(8,128)(2,1)S(1)} %get-tuple-element.31), channel_id=1, source_target_pairs={{0,1},{1,0},{2,3},{3,2},{4,5},{5,4},{6,7},{7,6},{8,9},{9,8},{10,11... | collective-permute-start | bytes 86024 | tf_op jit(solution)/shard_map/ppermute | solution.py:44
  23.6 3.8 %collective-permute-start.6 = (bf16[1,16,448]{2,1,0:T(8,128)(2,1)S(1)}, bf16[1,16,448]{2,1,0:T(8,128)(2,1)S(1)}, u32[]{:S(2)}, u32[]{:S(2)}) collective-permute-start(bf16[1,16,448]{2,1,0:T(8,128)(2,1)S(1)} %get-tuple-element.33), channel_id=1, source_target_pairs={{0,2},{2,0},{1,3},{3,1},{4,6},{6,4},{5,7},{7,5},{8,10},{10,8},{9,1... | collective-permute-start | bytes 43016 | tf_op jit(solution)/shard_map/ppermute | solution.py:44

commit v3 on v2

--- a/solution.py
+++ b/solution.py
@@ -7,6 +7,7 @@
 from jax.experimental import pallas as pl
 from jax.experimental.pallas import tpu as pltpu
 from jax.sharding import PartitionSpec as P
+
 
 BF16 = jnp.bfloat16
 F32 = jnp.float32
@@ -111,7 +112,6 @@
     rows = pairs * heads
     block = steps * heads
     place = lax.axis_index("ctx")
-    role = lax.axis_index("role")
 
     copies = []
 
@@ -230,20 +230,11 @@
     packed = jnp.sum(packed.reshape(pairs, heads, LANES), axis=1)
     out_ref[:, heads * value_width :] = packed.astype(BF16)
 
-    size = lax.axis_size("ctx")
-    half = tokens // lax.axis_size("role")
     key_id = lax.broadcasted_iota(jnp.int32, key_pos_ref.shape, 1)
-    near = 2 * tokens
-    far = (size - 2) * half
-    in_other = key_id >= near + far
-    local = key_id - near - jnp.where(in_other, far, 0)
-    is_near = key_id < near
-    slot = jnp.where(is_near, key_id // tokens, 2 + local // half)
-    base = jnp.where(
-        is_near, key_id % tokens, local % half + half * jnp.where(in_other, 1 - role, role)
-    )
-    for index in range(size):
-        base = base + jnp.where(slot == index, order_ref[place ^ index] * tokens, 0)
+    base = key_id
+    for slot in range(key_pos_ref.shape[1] // tokens):
+        move = (order_ref[place ^ slot] - slot) * tokens
+        base = base + jnp.where(key_id // tokens == slot, move, 0)
     key_pos_ref[...] = base
     query_pos_ref[...] = order_ref[place] * tokens + lax.broadcasted_iota(
         jnp.int32, query_pos_ref.shape, 0
@@ -267,7 +258,7 @@
     prompt_query,
     out_weight,
 ):
-    steps, requests, heads, width = step_query.shape
+    steps, requests, heads, _ = step_query.shape
     nope, latent_width = key_up.shape[1:]
     full = cache.shape[1]
     tokens = latent.shape[0]
@@ -381,33 +372,62 @@
     )(in_vmem(first), in_vmem(second))
 
 
-def join_kernel(half, first_ref, second_ref, out_ref):
-    rows = first_ref.shape[0]
-    if half:
-        role = lax.axis_index("role")
-        for index in range(rows // half):
-
-            @pl.when(role == index)
-            def _():
-                at = slice(index * half, (index + 1) * half)
-                out_ref[:half, :] = first_ref[at, :]
-                out_ref[half:, :] = second_ref[at, :]
-    else:
-        out_ref[:rows, :] = first_ref[...]
-        out_ref[rows:, :] = second_ref[...]
-
-
-def join_rows(half, first, second):
-    rows, full = first.shape
-    return pl.pallas_call(
-        functools.partial(join_kernel, half),
-        out_shape=pltpu.VMEM((2 * (half or rows), full), BF16),
-        in_specs=[VMEM] * 2,
+def halves_kernel(first_ref, second_ref, out_ref):
+    half = first_ref.shape[0] // 2
+    for index in range(2):
+
+        @pl.when(lax.axis_index("role") == index)
+        def _():
+            at = slice(index * half, (index + 1) * half)
+            out_ref[:half, :] = first_ref[at, :]
+            out_ref[half:, :] = second_ref[at, :]
+
+
+def gather_kernel(own_ref, far_ref, mine_ref, other_ref, out_ref):
+    tokens = own_ref.shape[0]
+    half = tokens // 2
+    out_ref[:tokens, :] = own_ref[...]
+    out_ref[2 * tokens : 3 * tokens, :] = far_ref[...]
+    for index, sources in enumerate(((mine_ref, other_ref), (other_ref, mine_ref))):
+
+        @pl.when(lax.axis_index("role") == index)
+        def _():
+            for part, source in enumerate(sources):
+                for slot in range(2):
+                    at = (2 * slot + 1) * tokens + part * half
+                    out_ref[at : at + half, :] = source[slot * half : (slot + 1) * half, :]
+
+
+def half_kernel(keys_ref, out_ref):
+    rows = out_ref.shape[0]
+    for index in range(2):
+
+        @pl.when(lax.axis_index("role") == index)
+        def _():
+            out_ref[...] = keys_ref[index * rows : (index + 1) * rows, :]
+
+
+def extend_kernel(keys_ref, mine_ref, other_ref, out_ref):
+    rows = keys_ref.shape[0]
+    half = mine_ref.shape[0]
+    out_ref[:rows, :] = keys_ref[...]
+    for index, sources in enumerate(((mine_ref, other_ref), (other_ref, mine_ref))):
+
+        @pl.when(lax.axis_index("role") == index)
+        def _():
+            out_ref[rows : rows + half, :] = sources[0][...]
+            out_ref[rows + half :, :] = sources[1][...]
+
+
+def move_rows(body, rows, *sources):
+    return pl.pallas_call(
+        body,
+        out_shape=pltpu.VMEM((rows, sources[0].shape[1]), BF16),
+        in_specs=[VMEM] * len(sources),
         out_specs=VMEM,
         compiler_params=params(1),
-        cost_estimate=pl.CostEstimate(flops=10**4, bytes_accessed=2 * 10**5, transcendentals=0),
-        name="join_rows",
-    )(in_vmem(first), in_vmem(second))
+        cost_estimate=pl.CostEstimate(flops=10**4, bytes_accessed=4 * 10**5, transcendentals=0),
+    )(*(in_vmem(source) for source in sources))
 
 
 def finish_kernel(
@@ -485,49 +505,39 @@
     )(in_vmem(keep), in_vmem(received))
 
 
-def lift_kernel(query_ref, key_up_ref, weight_hbm, row_ref, weight_ref, nope_ref, rope_ref, sem):
-    tokens, heads, width = query_ref.shape
+def lift_kernel(heads, query_ref, key_up_ref, row_ref, nope_ref, rope_ref):
+    tokens, every, width = query_ref.shape
     nope, latent = key_up_ref.shape[1:]
-    skipped = weight_hbm.shape[0] - weight_ref.shape[0]
-    copy = pltpu.make_async_copy(weight_hbm.at[skipped:], weight_ref, sem)
-    copy.start()
-    nope_ref[...] = query_ref[:, :, :nope].astype(F32).reshape(tokens * heads, nope)
+    nope_ref[...] = query_ref[:, :, :nope].astype(F32).reshape(tokens * every, nope)
     rope_ref[:, : width - nope] = (
-        query_ref[:, :, nope:].astype(F32).reshape(tokens * heads, width - nope)
-    )
-    for head in range(heads):
-        at = slice(head * tokens, (head + 1) * tokens)
-        part = nope_ref[pl.ds(head, tokens, stride=heads), :].astype(BF16)
+        query_ref[:, :, nope:].astype(F32).reshape(tokens * every, width - nope)
+    )
+    for index, head in enumerate(heads):
+        at = slice(index * tokens, (index + 1) * tokens)
+        part = nope_ref[pl.ds(head, tokens, stride=every), :].astype(BF16)
         row_ref[at, :latent] = dot(part, key_up_ref[head]).astype(BF16)
-        rope = rope_ref[pl.ds(head, tokens, stride=heads), :]
+        rope = rope_ref[pl.ds(head, tokens, stride=every), :]
         row_ref[at, latent:] = rope[:, : width - nope].astype(BF16)
-    copy.wait()
-
-
-def prompt_lift(prompt_query, key_up, out_weight, late_rows):
-    tokens, heads, width = prompt_query.shape
+
+
+def prompt_lift(heads, prompt_query, key_up):
+    tokens, every, width = prompt_query.shape
     nope, latent_width = key_up.shape[1:]
-    rows = tokens * heads
-    shape = pltpu.VMEM
-    return pl.pallas_call(
-        lift_kernel,
-        out_shape=(
-            shape((rows, latent_width + width - nope), BF16),
-            shape((late_rows, out_weight.shape[1]), BF16),
-        ),
-        in_specs=[VMEM] * 2 + [ANY],
-        out_specs=[VMEM] * 2,
+    return pl.pallas_call(
+        functools.partial(lift_kernel, heads),
+        out_shape=pltpu.VMEM((tokens * len(heads), latent_width + width - nope), BF16),
+        in_specs=[VMEM] * 2,
+        out_specs=VMEM,
         scratch_shapes=[
-            pltpu.VMEM((rows, nope), F32),
-            pltpu.VMEM((rows, LANES), F32),
-            pltpu.SemaphoreType.DMA,
+            pltpu.VMEM((tokens * every, nope), F32),
+            pltpu.VMEM((tokens * every, LANES), F32),
         ],
         compiler_params=params(8),
         cost_estimate=pl.CostEstimate(
-            flops=3 * 10**8, bytes_accessed=6 * 10**6, transcendentals=0
+            flops=2 * 10**8, bytes_accessed=3 * 10**6, transcendentals=0
         ),
         name="prompt_lift",
-    )(in_vmem(prompt_query), in_vmem(key_up), in_hbm(out_weight))
+    )(in_vmem(prompt_query), in_vmem(key_up))
 
 
 def attend(rate, group, heads, row_ref, key_ref, key_pos_ref, query_pos_ref, value_up_ref, put):
@@ -536,7 +546,7 @@
     latent = value_up_ref.shape[1]
     visible = (key_pos_ref[:1, :] <= query_pos_ref[:, :1])[None]
     for first in range(heads.start, heads.stop, group):
-        at = slice(first * tokens, (first + group) * tokens)
+        at = slice((first - heads.start) * tokens, (first - heads.start + group) * tokens)
         scores = dot_nt(row_ref[at, :], key_ref[...])
         scores = jnp.where(visible, scores.reshape(group, tokens, count), HIDDEN)
         scores = scores.reshape(group * tokens, count)
@@ -553,16 +563,24 @@
             )
 
 
-def front_kernel(rate, group, heads, skipped, *refs):
-    row_ref, *part_refs = refs[: 1 + len(skipped)]
-    key_pos_ref, query_pos_ref, value_up_ref, out_ref, key_ref = refs[1 + len(skipped) :]
-    at = 0
-    for part_ref, skip in zip(part_refs, skipped):
-        count = part_ref.shape[0] - skip
-        key_ref[at : at + count, :] = part_ref[skip:, :]
-        at += count
-    assert at == key_ref.shape[0]
+def front_kernel(
+    rate,
+    group,
+    heads,
+    row_ref,
+    key_ref,
+    key_pos_ref,
+    query_pos_ref,
+    value_up_ref,
+    weight_hbm,
+    out_ref,
+    weight_ref,
+    sem,
+):
     width = value_up_ref.shape[2]
+    skipped = weight_hbm.shape[0] - weight_ref.shape[0]
+    copy = pltpu.make_async_copy(weight_hbm.at[skipped:], weight_ref, sem)
+    copy.start()
 
     def put(head, value):
         out_ref[:, head * width : (head + 1) * width] = value
@@ -570,25 +588,29 @@
     attend(
         rate, group, heads, row_ref, key_ref, key_pos_ref, query_pos_ref, value_up_ref, put
     )
-
-
-def prompt_front(rate, group, heads, rows, parts, key_pos, query_pos, value_up):
+    copy.wait()
+
+
+def prompt_front(
+    rate, group, heads, rows, keys, key_pos, query_pos, value_up, out_weight, late_rows
+):
     tokens = query_pos.shape[0]
     shape = pltpu.VMEM
     return pl.pallas_call(
-        functools.partial(front_kernel, rate, group, heads, [skip for _, skip in parts]),
+        functools.partial(front_kernel, rate, group, heads),
         out_shape=(
             shape((tokens, len(heads) * value_up.shape[2]), BF16),
-            shape((key_pos.shape[1], rows.shape[1]), BF16),
+            shape((late_rows, out_weight.shape[1]), BF16),
         ),
-        in_specs=[VMEM] * (4 + len(parts)),
+        in_specs=[VMEM] * 5 + [ANY],
         out_specs=[VMEM] * 2,
+        scratch_shapes=[pltpu.SemaphoreType.DMA],
         compiler_params=params(16),
         cost_estimate=pl.CostEstimate(
             flops=8 * 10**8, bytes_accessed=6 * 10**6, transcendentals=3 * 10**5
         ),
         name="prompt_front",
-    )(*(in_vmem(v) for v in (rows, *(part for part, _ in parts), key_pos, query_pos, value_up)))
+    )(*(in_vmem(v) for v in (rows, keys, key_pos, query_pos, value_up)), in_hbm(out_weight))
 
 
 def back_kernel(
@@ -664,7 +686,7 @@
     cache_length,
     block_dest,
 ):
-    tokens, heads, width = prompt_query.shape
+    heads, width = prompt_query.shape[1:]
     rate = width ** (-0.5) * math.log2(math.e)
     context_size = lax.axis_size("ctx")
     steps = step_query.shape[0]
@@ -674,7 +696,8 @@
     early_rows = contracted // 2
 
     rounds = doublings(context_size)
-    near = swap(prompt_latent, "ctx", rounds[0])
+    assert role_size == 2 and context_size >= 4
+    far = swap(prompt_latent, "ctx", 2)
     (
         running,
         key_up,
@@ -699,32 +722,41 @@
         prompt_query,
         out_weight,
     )
-    rows, late_weight = prompt_lift(prompt_query, key_up, out_weight, contracted - early_rows)
-    sent = join_rows(tokens // role_size, latent, near)
+    group = 4 if heads % 8 == 0 else 1
+    middle = heads // 2
+    rows = prompt_lift(range(middle), prompt_query, key_up)
+    more_rows = prompt_lift(range(middle, heads), prompt_query, key_up)
     for step in rounds:
         far_running = swap(running, "ctx", step)
-        if step == rounds[-1]:
-            break
-        running = merge_parts(rate, heads, running, far_running)
-    for step in rounds[1:]:
-        received = swap(sent, "ctx", step)
-        if step == rounds[-1]:
-            break
-        sent = join_rows(None, sent, received)
+        if step != rounds[-1]:
+            running = merge_parts(rate, heads, running, far_running)
+    tokens = latent.shape[0]
+    mine = swap(move_rows(halves_kernel, tokens, latent, far), "ctx", 1)
+    other = swap(mine, "role", 1)
+    keys = move_rows(gather_kernel, 4 * tokens, latent, far, mine, other)
+    for step in rounds[2:]:
+        half = move_rows(half_kernel, keys.shape[0] // 2, keys)
+        received = swap(half, "ctx", step)
+        keys = move_rows(
+            extend_kernel, 2 * keys.shape[0], keys, received, swap(received, "role", 1)
+        )
+    front, late_weight = prompt_front(
+        rate,
+        group,
+        range(middle),
+        rows,
+        keys,
+        key_pos,
+        query_pos,
+        value_up,
+        out_weight,
+        contracted - early_rows,
+    )
+    prompt_out = prompt_back(
+        rate, group, range(middle, heads), more_rows, keys, key_pos, query_pos, value_up, front
+    )
     keep, give = finish_steps(
         rate, heads, head_size * role_size, running, far_running, early_weight, late_weight
-    )
-    same = [(sent, 2 * tokens // role_size), (received, 0)]
-    same = [(part, skip) for part, skip in same if part.shape[0] > skip]
-    parts = [(latent, 0), (near, 0)] + same
-    parts += [(swap(part, "role", 1), skip) for part, skip in same]
-    group = 4 if heads % 8 == 0 else 1
-    middle = heads // 2
-    front, keys = prompt_front(
-        rate, group, range(middle), rows, parts, key_pos, query_pos, value_up
-    )
-    prompt_out = prompt_back(
-        rate, group, range(middle, heads), rows, keys, key_pos, query_pos, value_up, front
     )
     partial = swap(give, "role", 1)
     for step in reversed(doublings(head_size)):

time: 32.6 us -> 34.9 us (1.071)
  waiting for transfers between devices: 8.04 us -> 11.1 us
  Pallas kernels: 13 us -> 12.4 us
    ppermute x7, waiting for transfers between devices: 8.04 us -> 11.1 us  [swap(): return lax.ppermute(value, axis, [(i, i ^ step) for i in range(size)])]
    pallas_call x3 -> x5, Pallas kernels: 3.92 us -> 3.35 us  [the longest x1 2.06 us: prompt_front(): pl.pallas_call(functools.partial(front_kernel, rate, group, heads), out_s...]
  transfers between devices with their start and end apart: 7 -> 7, of which waited for: 4 -> 5; matrix products, arithmetic and copies ran while one was open for 0% -> 0% of each run, Pallas kernels for 27% -> 30%
where the time goes in v3:
time: 34.9 us; the launch traced here: 34.8 us
  Pallas kernels  12.4 us (36%)
  waiting for transfers between devices  11.1 us (32%)
  starting transfers between devices  10.6 us (30%)
  between operations  0.7 us (2%)
    ppermute x7, waiting for transfers between devices, swap(): return lax.ppermute(value, axis, [(i, i ^ step) for i in range(size)])  11.1 us
    ppermute x7, starting transfers between devices, swap(): return lax.ppermute(value, axis, [(i, i ^ step) for i in range(size)])  10.6 us
    pallas_call x1, Pallas kernels, step_part(): pl.pallas_call(functools.partial(step_kernel, rate), out_shape=(shape((pa...  4.29 us
    pallas_call x1, Pallas kernels, prompt_back(): pl.pallas_call(functools.partial(back_kernel, rate, group, heads), out_sh...  2.5 us
    pallas_call x1, Pallas kernels, prompt_front(): pl.pallas_call(functools.partial(front_kernel, rate, group, heads), out_s...  2.06 us
    pallas_call x1, Pallas kernels, finish_steps(): pl.pallas_call(functools.partial(finish_kernel, rate, heads, parts), out_...  1.34 us
    pallas_call x2, Pallas kernels, prompt_lift(): pl.pallas_call(functools.partial(lift_kernel, heads), out_shape=pltpu.VME...  1.23 us
  transfers between devices with their start and end apart: 7, of which 5 were waited for; matrix products, arithmetic and copies ran while one was open for 0% of the time, Pallas kernels for 30%

profile of v3, /device:TPU:0, one launch (start us, length us, event | category | flops | bytes accessed | tf_op | source)
XLA Modules:
  0.0 34.8 jit_solution(5083570114953465565)
XLA Ops:
  0.6 4.1 %collective-permute-start = (bf16[96,576]{1,0:T(8,128)(2,1)}, bf16[96,576]{1,0:T(8,128)(2,1)S(1)}, u32[]{:S(2)}, u32[]{:S(2)}) collective-permute-start(bf16[96,576]{1,0:T(8,128)(2,1)} %latent_hbm.1), channel_id=1, source_target_pairs={{0,8},{4,12},{8,0},{12,4},{1,9},{5,13},{9,1},{13,5},{2,10},{6,14},... | collective-permute-start | bytes 331784 | tf_op jit(solution)/shard_map/ppermute | solution.py:45
  4.8 4.3 %step_part.1 = (bf16[16,2176]{1,0:T(8,128)(2,1)S(1)}, bf16[16,128,512]{2,1,0:T(8,128)(2,1)S(1)}, bf16[16,512,128]{2,1,0:T(8,128)(2,1)S(1)}, bf16[96,576]{1,0:T(8...) custom-call(s32[4]{0:T(128)} %order_hbm.1, ...), custom_call_target="tpu_custom_call" | custom-call | flops 1000000000 | bytes 10000000 | tf_op jit(solution)/shard_map/step_part/pallas_call | solution.py:268
  9.1 1.9 %collective-permute-done.second_ref.far_ref = bf16[96,576]{1,0:T(8,128)(2,1)S(1)} collective-permute-done((bf16[96,576]{1,0:T(8,128)(2,1)}, bf16[96,576]{1,0:T(8,128)(2,1)S(1)}, u32[]{:S(2)}, u32[]{:S(2)}) %collective-permute-start) | collective-permute-done | bytes 110624 | tf_op jit(solution)/shard_map/ppermute | solution.py:45
  10.9 0.9 %collective-permute-start.1 = (bf16[96,576]{1,0:T(8,128)(2,1)S(1)}, bf16[96,576]{1,0:T(8,128)(2,1)S(1)}, u32[]{:S(2)}, u32[]{:S(2)}) collective-permute-start(bf16[96,576]{1,0:T(8,128)(2,1)S(1)} %shard_map.122), channel_id=1, source_target_pairs={{0,4},{4,0},{8,12},{12,8},{1,5},{5,1},{9,13},{13,9},{2,6},{6,2},{1... | collective-permute-start | bytes 331784 | tf_op jit(solution)/shard_map/ppermute | solution.py:45
  11.8 4.1 %collective-permute-done.1.mine_ref = bf16[96,576]{1,0:T(8,128)(2,1)S(1)} collective-permute-done((bf16[96,576]{1,0:T(8,128)(2,1)S(1)}, bf16[96,576]{1,0:T(8,128)(2,1)S(1)}, u32[]{:S(2)}, u32[]{:S(2)}) %collective-permute-start.1) | collective-permute-done | bytes 110624 | tf_op jit(solution)/shard_map/ppermute | solution.py:45
  15.9 0.0 collective-permute-start.2
  15.9 1.2 %collective-permute-start.3 = (bf16[16,2176]{1,0:T(8,128)(2,1)S(1)}, bf16[16,2176]{1,0:T(8,128)(2,1)S(1)}, u32[]{:S(2)}, u32[]{:S(2)}) collective-permute-start(bf16[16,2176]{1,0:T(8,128)(2,1)S(1)} %get-tuple-element.23.first_ref), channel_id=1, source_target_pairs={{0,4},{4,0},{8,12},{12,8},{1,5},{5,1},{9,13},{13,9},{2,6},{6,2},{1... | collective-permute-start | bytes 208904 | tf_op jit(solution)/shard_map/ppermute | solution.py:45
  17.1 0.6 %prompt_lift.3.row_ref = bf16[768,576]{1,0:T(8,128)(2,1)S(1)} custom-call(bf16[96,16,192]{2,1,0:T(8,128)(2,1)S(1)} %get-tuple-element.16.query_ref, bf16[16,128,512]{2,1,0:T(8,128)(2,1)S(1)} %get-tuple-element.17.key_up_ref), custom_call_target="tpu_custom_call" | custom-call | flops 200000000 | bytes 3000000 | tf_op jit(solution)/shard_map/prompt_lift/pallas_call | solution.py:526
  17.7 2.8 %collective-permute-done.3.second_ref = bf16[16,2176]{1,0:T(8,128)(2,1)S(1)} collective-permute-done((bf16[16,2176]{1,0:T(8,128)(2,1)S(1)}, bf16[16,2176]{1,0:T(8,128)(2,1)S(1)}, u32[]{:S(2)}, u32[]{:S(2)}) %collective-permute-start.3) | collective-permute-done | bytes 69664 | tf_op jit(solution)/shard_map/ppermute | solution.py:45
  20.5 0.3 merge_parts.1.first_ref
  20.8 2.8 %collective-permute-start.4 = (bf16[16,2176]{1,0:T(8,128)(2,1)S(1)}, bf16[16,2176]{1,0:T(8,128)(2,1)S(1)}, u32[]{:S(2)}, u32[]{:S(2)}) collective-permute-start(bf16[16,2176]{1,0:T(8,128)(2,1)S(1)} %merge_parts.1.first_ref), channel_id=1, source_target_pairs={{0,8},{4,12},{8,0},{12,4},{1,9},{5,13},{9,1},{13,5},{2,10},{6,14},... | collective-permute-start | bytes 208904 | tf_op jit(solution)/shard_map/ppermute | solution.py:45
  23.5 0.0 collective-permute-done.2.other_ref
  23.6 2.1 %prompt_front.1 = (bf16[96,1024]{1,0:T(8,128)(2,1)S(1)}, bf16[1024,1792]{1,0:T(8,128)(2,1)S(1)}) custom-call(bf16[768,576]{1,0:T(8,128)(2,1)S(1)} %prompt_lift.3.row_ref, bf16[384,576]{1,0:T(8,128)(2,1)S(1)} %shard_map.123.key_ref, s32[8,384]{1,0:T(8,128)S(1)} %get-tuple-element.19.key_pos_ref, s32[96,128]{1,0:T(8,128)S(1)} %get-tuple-element.20.query_pos_ref, ...), custom_call_target="tpu_custom_call" | custom-call | flops 800000000 | bytes 6000000 | tf_op jit(solution)/shard_map/prompt_front/pallas_call | solution.py:599
  25.7 1.8 %collective-permute-done.4.second_ref = bf16[16,2176]{1,0:T(8,128)(2,1)S(1)} collective-permute-done((bf16[16,2176]{1,0:T(8,128)(2,1)S(1)}, bf16[16,2176]{1,0:T(8,128)(2,1)S(1)}, u32[]{:S(2)}, u32[]{:S(2)}) %collective-permute-start.4) | collective-permute-done | bytes 69664 | tf_op jit(solution)/shard_map/ppermute | solution.py:45
  27.5 1.3 %finish_steps.1 = (f32[2,16,448]{2,1,0:T(8,128)S(1)}, bf16[2,16,448]{2,1,0:T(8,128)(2,1)S(1)}) custom-call(bf16[16,2176]{1,0:T(8,128)(2,1)S(1)} %merge_parts.1.first_ref, bf16[16,2176]{1,0:T(8,128)(2,1)S(1)} %collective-permute-done.4.second_ref, bf16[1024,1792]{1,0:T(8,128)(2,1)S(1)} %get-tuple-element.24.early_ref, ...), custom_call_target="tpu_custom_call" | custom-call | flops 500000000 | bytes 8000000 | tf_op jit(solution)/shard_map/finish_steps/pallas_call | solution.py:453
  28.8 0.0 collective-permute-start.5
  28.8 0.6 %prompt_lift.2.row_ref = bf16[768,576]{1,0:T(8,128)(2,1)S(1)} custom-call(bf16[96,16,192]{2,1,0:T(8,128)(2,1)S(1)} %get-tuple-element.16.query_ref, bf16[16,128,512]{2,1,0:T(8,128)(2,1)S(1)} %get-tuple-element.17.key_up_ref), custom_call_target="tpu_custom_call" | custom-call | flops 200000000 | bytes 3000000 | tf_op jit(solution)/shard_map/prompt_lift/pallas_call | solution.py:526
  29.5 0.6 %collective-permute-done.5.received_ref = bf16[2,16,448]{2,1,0:T(8,128)(2,1)S(1)} collective-permute-done((bf16[2,16,448]{2,1,0:T(8,128)(2,1)S(1)}, bf16[2,16,448]{2,1,0:T(8,128)(2,1)S(1)}, u32[]{:S(2)}, u32[]{:S(2)}) %collective-permute-start.5) | collective-permute-done | bytes 28704 | tf_op jit(solution)/shard_map/ppermute | solution.py:45
  30.0 1.6 %collective-permute-start.6 = (bf16[1,16,448]{2,1,0:T(8,128)(2,1)S(1)}, bf16[1,16,448]{2,1,0:T(8,128)(2,1)S(1)}, u32[]{:S(2)}, u32[]{:S(2)}) collective-permute-start(bf16[1,16,448]{2,1,0:T(8,128)(2,1)S(1)} %get-tuple-element.29), channel_id=1, source_target_pairs={{0,2},{2,0},{1,3},{3,1},{4,6},{6,4},{5,7},{7,5},{8,10},{10,8},{9,1... | collective-permute-start | bytes 43016 | tf_op jit(solution)/shard_map/ppermute | solution.py:45
  31.6 2.5 %prompt_back.1 = bf16[96,2048]{1,0:T(8,128)(2,1)} custom-call(bf16[768,576]{1,0:T(8,128)(2,1)S(1)} %prompt_lift.2.row_ref, bf16[384,576]{1,0:T(8,128)(2,1)S(1)} %shard_map.123.key_ref, s32[8,384]{1,0:T(8,128)S(1)} %get-tuple-element.19.key_pos_ref, s32[96,128]{1,0:T(8,128)S(1)} %get-tuple-element.20.query_pos_ref, ...), custom_call_target="tpu_custom_call" | custom-call | flops 800000000 | bytes 6000000 | tf_op jit(solution)/shard_map/prompt_back/pallas_call | solution.py:659
  34.1 0.0 collective-permute-done.6.received_ref
  34.1 0.6 %sum_steps.1 = bf16[4,4,448]{2,1,0:T(4,128)(2,1)} custom-call(f32[1,16,448]{2,1,0:T(8,128)S(1)} %get-tuple-element.28.keep_ref, bf16[1,16,448]{2,1,0:T(8,128)(2,1)S(1)} %collective-permute-done.6.received_ref), custom_call_target="tpu_custom_call" | custom-call | flops 100000 | bytes 100000 | tf_op jit(solution)/shard_map/sum_steps/pallas_call | solution.py:497
  (3 shorter events, 0.1 us)
Async XLA Ops:
  0.6 10.3 %collective-permute-start = (bf16[96,576]{1,0:T(8,128)(2,1)}, bf16[96,576]{1,0:T(8,128)(2,1)S(1)}, u32[]{:S(2)}, u32[]{:S(2)}) collective-permute-start(bf16[96,576]{1,0:T(8,128)(2,1)} %latent_hbm.1), channel_id=1, source_target_pairs={{0,8},{4,12},{8,0},{12,4},{1,9},{5,13},{9,1},{13,5},{2,10},{6,14},... | collective-permute-start | bytes 331784 | tf_op jit(solution)/shard_map/ppermute | solution.py:45
  10.9 4.9 %collective-permute-start.1 = (bf16[96,576]{1,0:T(8,128)(2,1)S(1)}, bf16[96,576]{1,0:T(8,128)(2,1)S(1)}, u32[]{:S(2)}, u32[]{:S(2)}) collective-permute-start(bf16[96,576]{1,0:T(8,128)(2,1)S(1)} %shard_map.122), channel_id=1, source_target_pairs={{0,4},{4,0},{8,12},{12,8},{1,5},{5,1},{9,13},{13,9},{2,6},{6,2},{1... | collective-permute-start | bytes 331784 | tf_op jit(solution)/shard_map/ppermute | solution.py:45
  15.9 7.7 %collective-permute-start.2 = (bf16[96,576]{1,0:T(8,128)(2,1)S(1)}, bf16[96,576]{1,0:T(8,128)(2,1)S(1)}, u32[]{:S(2)}, u32[]{:S(2)}) collective-permute-start(bf16[96,576]{1,0:T(8,128)(2,1)S(1)} %collective-permute-done.1.mine_ref), channel_id=1, source_target_pairs={{0,1},{1,0},{2,3},{3,2},{4,5},{5,4},{6,7},{7,6},{8,9},{9,8},{10,11... | collective-permute-start | bytes 331784 | tf_op jit(solution)/shard_map/ppermute | solution.py:45
  15.9 4.6 %collective-permute-start.3 = (bf16[16,2176]{1,0:T(8,128)(2,1)S(1)}, bf16[16,2176]{1,0:T(8,128)(2,1)S(1)}, u32[]{:S(2)}, u32[]{:S(2)}) collective-permute-start(bf16[16,2176]{1,0:T(8,128)(2,1)S(1)} %get-tuple-element.23.first_ref), channel_id=1, source_target_pairs={{0,4},{4,0},{8,12},{12,8},{1,5},{5,1},{9,13},{13,9},{2,6},{6,2},{1... | collective-permute-start | bytes 208904 | tf_op jit(solution)/shard_map/ppermute | solution.py:45
  20.8 6.7 %collective-permute-start.4 = (bf16[16,2176]{1,0:T(8,128)(2,1)S(1)}, bf16[16,2176]{1,0:T(8,128)(2,1)S(1)}, u32[]{:S(2)}, u32[]{:S(2)}) collective-permute-start(bf16[16,2176]{1,0:T(8,128)(2,1)S(1)} %merge_parts.1.first_ref), channel_id=1, source_target_pairs={{0,8},{4,12},{8,0},{12,4},{1,9},{5,13},{9,1},{13,5},{2,10},{6,14},... | collective-permute-start | bytes 208904 | tf_op jit(solution)/shard_map/ppermute | solution.py:45
  28.8 1.2 %collective-permute-start.5 = (bf16[2,16,448]{2,1,0:T(8,128)(2,1)S(1)}, bf16[2,16,448]{2,1,0:T(8,128)(2,1)S(1)}, u32[]{:S(2)}, u32[]{:S(2)}) collective-permute-start(bf16[2,16,448]{2,1,0:T(8,128)(2,1)S(1)} %get-tuple-element.27), channel_id=1, source_target_pairs={{0,1},{1,0},{2,3},{3,2},{4,5},{5,4},{6,7},{7,6},{8,9},{9,8},{10,11... | collective-permute-start | bytes 86024 | tf_op jit(solution)/shard_map/ppermute | solution.py:45
  30.0 4.1 %collective-permute-start.6 = (bf16[1,16,448]{2,1,0:T(8,128)(2,1)S(1)}, bf16[1,16,448]{2,1,0:T(8,128)(2,1)S(1)}, u32[]{:S(2)}, u32[]{:S(2)}) collective-permute-start(bf16[1,16,448]{2,1,0:T(8,128)(2,1)S(1)} %get-tuple-element.29), channel_id=1, source_target_pairs={{0,2},{2,0},{1,3},{3,1},{4,6},{6,4},{5,7},{7,5},{8,10},{10,8},{9,1... | collective-permute-start | bytes 43016 | tf_op jit(solution)/shard_map/ppermute | solution.py:45

commit v4 on v3

--- a/solution.py
+++ b/solution.py
@@ -45,6 +45,42 @@
     return lax.ppermute(value, axis, [(i, i ^ step) for i in range(size)])
 
 
+def mark_kernel(out_ref):
+    out_ref[...] = jnp.zeros_like(out_ref)
+
+
+def mark():
+    return pl.pallas_call(
+        mark_kernel,
+        out_shape=pltpu.VMEM((8, LANES), F32),
+        out_specs=VMEM,
+        compiler_params=params(1),
+        cost_estimate=pl.CostEstimate(flops=8 * 10**9, bytes_accessed=10**4, transcendentals=0),
+        name="mark",
+    )()
+
+
+def own_half_kernel(latent_hbm, out_ref, sem):
+    half = out_ref.shape[0]
+    start = pl.multiple_of(lax.axis_index("role") * half, half)
+    copy = pltpu.make_async_copy(latent_hbm.at[pl.ds(start, half)], out_ref, sem)
+    copy.start()
+    copy.wait()
+
+
+def own_half(latent):
+    return pl.pallas_call(
+        own_half_kernel,
+        out_shape=pltpu.VMEM((latent.shape[0] // 2, latent.shape[1]), BF16),
+        in_specs=[ANY],
+        out_specs=VMEM,
+        scratch_shapes=[pltpu.SemaphoreType.DMA],
+        compiler_params=params(1),
+        cost_estimate=pl.CostEstimate(flops=10**4, bytes_accessed=10**5, transcendentals=0),
+        name="own_half",
+    )(in_hbm(latent))
+
+
 def in_hbm(value):
     return pltpu.with_memory_space_constraint(value, pltpu.HBM)
 
@@ -73,31 +109,24 @@
 
 def step_kernel(
     rate,
+    mark_ref,
     order_hbm,
     length_hbm,
     dest_hbm,
-    query_hbm,
-    key_up_hbm,
-    cache_hbm,
-    latent_hbm,
-    fresh_hbm,
-    value_up_hbm,
+    query_ref,
+    key_up_ref,
+    cache_ref,
+    latent_ref,
+    fresh_ref,
+    value_up_ref,
     prompt_hbm,
-    weight_hbm,
     out_ref,
-    key_up_ref,
-    value_up_ref,
-    latent_ref,
     prompt_ref,
-    weight_ref,
     key_pos_ref,
     query_pos_ref,
     order_ref,
     length_ref,
     dest_ref,
-    query_ref,
-    cache_ref,
-    fresh_ref,
     nope_ref,
     row_ref,
     extra_ref,
@@ -120,25 +149,13 @@
         copies[-1].start()
         return copies[-1]
 
-    query_copy = fetch(query_hbm, query_ref)
-    quarter = heads // 4
-    key_up_copies = [
-        fetch(key_up_hbm.at[at : at + quarter], key_up_ref.at[at : at + quarter])
-        for at in range(0, heads, quarter)
-    ]
-    latent_copy = fetch(latent_hbm, latent_ref)
-    fresh_copy = fetch(fresh_hbm, fresh_ref)
     scalar_copies = [
         fetch(length_hbm, length_ref),
         fetch(dest_hbm, dest_ref),
         fetch(order_hbm, order_ref),
     ]
-    cache_copy = fetch(cache_hbm, cache_ref)
-    value_up_copy = fetch(value_up_hbm, value_up_ref)
     prompt_copy = fetch(prompt_hbm, prompt_ref)
-    weight_copy = fetch(weight_hbm.at[: weight_ref.shape[0]], weight_ref)
-
-    query_copy.wait()
+
     query = query_ref[...].astype(F32)
     query = jnp.concatenate(
         [query[:, request].reshape(block, width) for request in range(requests)], axis=0
@@ -146,8 +163,6 @@
     nope_ref[...] = query[:, :nope]
     rope = query[:, nope:]
     for head in range(heads):
-        if head % quarter == 0:
-            key_up_copies[head // quarter].wait()
         part = nope_ref[pl.ds(head, pairs, stride=heads), :].astype(BF16)
         lifted = dot(part, key_up_ref[head]).astype(BF16).astype(F32)
         for lane in range(0, latent, LANES):
@@ -157,8 +172,6 @@
     row_parts = [row_ref[index] for index in range(latent // LANES)] + [rope]
     query_rows = jnp.concatenate(row_parts, axis=1).astype(BF16)
 
-    latent_copy.wait()
-    fresh_copy.wait()
     extra_ref[:tokens, :] = latent_ref[...].astype(F32)
     for step in range(steps):
         extra_ref[tokens + step * requests : tokens + (step + 1) * requests, :] = fresh_ref[
@@ -179,7 +192,6 @@
     )
     more = jnp.where(seen, more, HIDDEN)
     position = place * span + lax.broadcasted_iota(jnp.int32, (1, span), 1)
-    cache_copy.wait()
     scores = [
         jnp.where(
             position < length_ref[request],
@@ -205,13 +217,12 @@
         axis=0,
     )
     mixed = mixed + dot(more.astype(BF16), extra[:, :latent])
-    mixed = mixed / jnp.maximum(total, TINY)
+    mixed = mixed * (1.0 / jnp.maximum(total, TINY))
     for lane in range(0, latent, LANES):
         mixed_ref[lane // LANES] = mixed[:, lane : lane + LANES]
     high = jnp.broadcast_to(high, (rows, LANES))
     total = jnp.broadcast_to(total, (rows, LANES))
 
-    value_up_copy.wait()
     value_width = value_up_ref.shape[2]
     for head in range(heads):
         parts = [
@@ -240,12 +251,10 @@
         jnp.int32, query_pos_ref.shape, 0
     )
     prompt_copy.wait()
-    weight_copy.wait()
 
 
 def step_part(
     rate,
-    early_rows,
     block_order,
     cache_length,
     block_dest,
@@ -256,7 +265,6 @@
     fresh,
     value_up,
     prompt_query,
-    out_weight,
 ):
     steps, requests, heads, _ = step_query.shape
     nope, latent_width = key_up.shape[1:]
@@ -269,49 +277,37 @@
         functools.partial(step_kernel, rate),
         out_shape=(
             shape((pairs, heads * value_up.shape[2] + LANES), BF16),
-            shape(key_up.shape, BF16),
-            shape(value_up.shape, BF16),
-            shape(latent.shape, BF16),
             shape(prompt_query.shape, BF16),
-            shape((early_rows, out_weight.shape[1]), BF16),
             shape((8, tokens * lax.axis_size("ctx")), jnp.int32),
             shape((tokens, LANES), jnp.int32),
         ),
-        in_specs=[ANY] * 11,
-        out_specs=[VMEM] * 8,
+        in_specs=[VMEM] + [ANY] * 3 + [VMEM] * 6 + [ANY],
+        out_specs=[VMEM] * 4,
         scratch_shapes=[
             pltpu.SMEM(block_order.shape, jnp.int32),
             pltpu.SMEM(cache_length.shape, jnp.int32),
             pltpu.SMEM(block_dest.shape, jnp.int32),
-            pltpu.VMEM(step_query.shape, BF16),
-            pltpu.VMEM(cache.shape, BF16),
-            pltpu.VMEM(fresh.shape, BF16),
             pltpu.VMEM((rows, nope), F32),
             pltpu.VMEM((latent_width // LANES, rows, LANES), F32),
             pltpu.VMEM((tokens + pairs, full), F32),
             pltpu.VMEM((latent_width // LANES, rows, LANES), F32),
-            pltpu.SemaphoreType.DMA((14,)),
+            pltpu.SemaphoreType.DMA((4,)),
         ],
-        compiler_params=params(24),
+        compiler_params=params(12),
         cost_estimate=pl.CostEstimate(flops=10**9, bytes_accessed=10**7, transcendentals=10**5),
         name="step_part",
     )(
-        *(
-            in_hbm(value)
-            for value in (
-                block_order,
-                cache_length,
-                block_dest,
-                step_query,
-                key_up,
-                cache,
-                latent,
-                fresh,
-                value_up,
-                prompt_query,
-                out_weight,
-            )
-        )
+        mark(),
+        in_hbm(block_order),
+        in_hbm(cache_length),
+        in_hbm(block_dest),
+        in_vmem(step_query),
+        in_vmem(key_up),
+        in_vmem(cache),
+        in_vmem(latent),
+        in_vmem(fresh),
+        in_vmem(value_up),
+        in_hbm(prompt_query),
     )
 
 
@@ -333,9 +329,9 @@
     share_a = total_a * jnp.exp2((high_a - high) * rate)
     share_b = total_b * jnp.exp2((high_b - high) * rate)
     total = share_a + share_b
-    safe = jnp.maximum(total, TINY)
-    share_a = share_a / safe
-    share_b = share_b / safe
+    inverse = 1.0 / jnp.maximum(total, TINY)
+    share_a = share_a * inverse
+    share_b = share_b * inverse
     merged = []
     for head in range(heads):
         at = slice(head * value_width, (head + 1) * value_width)
@@ -372,30 +368,24 @@
     )(in_vmem(first), in_vmem(second))
 
 
-def halves_kernel(first_ref, second_ref, out_ref):
-    half = first_ref.shape[0] // 2
-    for index in range(2):
-
-        @pl.when(lax.axis_index("role") == index)
-        def _():
-            at = slice(index * half, (index + 1) * half)
-            out_ref[:half, :] = first_ref[at, :]
-            out_ref[half:, :] = second_ref[at, :]
-
-
-def gather_kernel(own_ref, far_ref, mine_ref, other_ref, out_ref):
+def join_kernel(first_ref, second_ref, out_ref):
+    rows = first_ref.shape[0]
+    out_ref[:rows, :] = first_ref[...]
+    out_ref[rows:, :] = second_ref[...]
+
+
+def gather_kernel(own_ref, mine_ref, other_ref, out_ref):
     tokens = own_ref.shape[0]
     half = tokens // 2
     out_ref[:tokens, :] = own_ref[...]
-    out_ref[2 * tokens : 3 * tokens, :] = far_ref[...]
     for index, sources in enumerate(((mine_ref, other_ref), (other_ref, mine_ref))):
 
         @pl.when(lax.axis_index("role") == index)
         def _():
             for part, source in enumerate(sources):
-                for slot in range(2):
-                    at = (2 * slot + 1) * tokens + part * half
-                    out_ref[at : at + half, :] = source[slot * half : (slot + 1) * half, :]
+                for place, slot in enumerate((2, 1, 3)):
+                    at = slot * tokens + part * half
+                    out_ref[at : at + half, :] = source[place * half : (place + 1) * half, :]
 
 
 def half_kernel(keys_ref, out_ref):
@@ -431,12 +421,11 @@
 
 
 def finish_kernel(
-    rate, heads, parts, first_ref, second_ref, early_ref, late_ref, keep_ref, give_ref
+    rate, heads, parts, first_ref, second_ref, weight_ref, keep_ref, give_ref
 ):
     merged, _, _ = merge(rate, first_ref, second_ref, heads)
     rows = jnp.concatenate(merged, axis=1)
-    early = early_ref.shape[0]
-    product = dot(rows[:, :early], early_ref[...]) + dot(rows[:, early:], late_ref[...])
+    product = dot(rows, weight_ref[...])
     width = product.shape[1] // parts
     upper = lax.axis_index("role") == 1
     for index in range(parts // 2):
@@ -447,20 +436,20 @@
         give_ref[index] = jnp.where(upper, low, high).astype(BF16)
 
 
-def finish_steps(rate, heads, parts, first, second, early, late):
+def finish_steps(rate, heads, parts, first, second, weight):
     pairs = first.shape[0]
-    shape = (parts // 2, pairs, early.shape[1] // parts)
+    shape = (parts // 2, pairs, weight.shape[1] // parts)
     return pl.pallas_call(
         functools.partial(finish_kernel, rate, heads, parts),
         out_shape=(pltpu.VMEM(shape, F32), pltpu.VMEM(shape, BF16)),
-        in_specs=[VMEM] * 4,
+        in_specs=[VMEM] * 3,
         out_specs=[VMEM] * 2,
         compiler_params=params(4),
         cost_estimate=pl.CostEstimate(
             flops=5 * 10**8, bytes_accessed=8 * 10**6, transcendentals=10**4
         ),
         name="finish_steps",
-    )(*(in_vmem(v) for v in (first, second, early, late)))
+    )(*(in_vmem(v) for v in (first, second, weight)))
 
 
 def fold_kernel(step, keep_ref, received_ref, new_keep_ref, give_ref):
@@ -540,77 +529,63 @@
     )(in_vmem(prompt_query), in_vmem(key_up))
 
 
-def attend(rate, group, heads, row_ref, key_ref, key_pos_ref, query_pos_ref, value_up_ref, put):
+def attend(
+    rate, group, heads, row_ref, key_ref, key_pos_ref, query_pos_ref, value_up_ref, put
+):
     tokens = query_pos_ref.shape[0]
     count = key_ref.shape[0]
     latent = value_up_ref.shape[1]
     visible = (key_pos_ref[:1, :] <= query_pos_ref[:, :1])[None]
-    for first in range(heads.start, heads.stop, group):
-        at = slice((first - heads.start) * tokens, (first - heads.start + group) * tokens)
-        scores = dot_nt(row_ref[at, :], key_ref[...])
+
+    def score(first):
+        base = first % (row_ref.shape[0] // tokens)
+        at = slice(base * tokens, (base + group) * tokens)
+        return dot_nt(row_ref[at, :], key_ref[...])
+
+    firsts = list(range(heads.start, heads.stop, group))
+    ahead = score(firsts[0])
+    for first in firsts:
+        scores = ahead
+        if first != firsts[-1]:
+            ahead = score(first + group)
         scores = jnp.where(visible, scores.reshape(group, tokens, count), HIDDEN)
         scores = scores.reshape(group * tokens, count)
         weights = jnp.exp2((scores - jnp.max(scores, axis=1, keepdims=True)) * rate)
-        total = jnp.sum(weights, axis=1, keepdims=True)
-        mixed = dot(weights.astype(BF16), key_ref[:, :latent])
-        mixed = (mixed / total).astype(BF16)
+        inverse = 1.0 / jnp.sum(weights, axis=1, keepdims=True)
+        mixed = dot(weights.astype(BF16), key_ref[:, :latent]).astype(BF16)
         for index in range(group):
-            put(
-                first + index,
-                dot(
-                    mixed[index * tokens : (index + 1) * tokens], value_up_ref[first + index]
-                ).astype(BF16),
-            )
+            part = slice(index * tokens, (index + 1) * tokens)
+            value = dot(mixed[part], value_up_ref[first + index]) * inverse[part]
+            put(first + index, value.astype(BF16))
 
 
 def front_kernel(
-    rate,
-    group,
-    heads,
-    row_ref,
-    key_ref,
-    key_pos_ref,
-    query_pos_ref,
-    value_up_ref,
-    weight_hbm,
-    out_ref,
-    weight_ref,
-    sem,
+    rate, group, heads, row_ref, key_ref, key_pos_ref, query_pos_ref, value_up_ref, out_ref
 ):
     width = value_up_ref.shape[2]
-    skipped = weight_hbm.shape[0] - weight_ref.shape[0]
-    copy = pltpu.make_async_copy(weight_hbm.at[skipped:], weight_ref, sem)
-    copy.start()
 
     def put(head, value):
-        out_ref[:, head * width : (head + 1) * width] = value
+        at = (head - heads.start) * width
+        out_ref[:, at : at + width] = value
 
     attend(
         rate, group, heads, row_ref, key_ref, key_pos_ref, query_pos_ref, value_up_ref, put
     )
-    copy.wait()
-
-
-def prompt_front(
-    rate, group, heads, rows, keys, key_pos, query_pos, value_up, out_weight, late_rows
-):
+
+
+def prompt_front(rate, group, heads, rows, keys, key_pos, query_pos, value_up):
     tokens = query_pos.shape[0]
-    shape = pltpu.VMEM
     return pl.pallas_call(
         functools.partial(front_kernel, rate, group, heads),
-        out_shape=(
-            shape((tokens, len(heads) * value_up.shape[2]), BF16),
-            shape((late_rows, out_weight.shape[1]), BF16),
-        ),
-        in_specs=[VMEM] * 5 + [ANY],
-        out_specs=[VMEM] * 2,
-        scratch_shapes=[pltpu.SemaphoreType.DMA],
+        out_shape=pltpu.VMEM((tokens, len(heads) * value_up.shape[2]), BF16),
+        in_specs=[VMEM] * 5,
+        out_specs=VMEM,
         compiler_params=params(16),
         cost_estimate=pl.CostEstimate(
-            flops=8 * 10**8, bytes_accessed=6 * 10**6, transcendentals=3 * 10**5
+            flops=4 * 10**8, bytes_accessed=3 * 10**6, transcendentals=3 * 10**5
         ),
         name="prompt_front",
-    )(*(in_vmem(v) for v in (rows, keys, key_pos, query_pos, value_up)), in_hbm(out_weight))
+    )(*(in_vmem(v) for v in (rows, keys, key_pos, query_pos, value_up)))
 
 
 def back_kernel(
@@ -622,15 +597,22 @@
     key_pos_ref,
     query_pos_ref,
     value_up_ref,
-    front_ref,
-    out_hbm,
-    back_ref,
-    sems,
+    *refs,
 ):
+    *front_refs, out_hbm, back_ref, sems = refs
     width = value_up_ref.shape[2]
-    edge = heads.start * width
-    copies = [pltpu.make_async_copy(front_ref, out_hbm.at[:, :edge], sems.at[0])]
-    copies[0].start()
+    edge = 0
+    copies = []
+    for front_ref in front_refs:
+        size = front_ref.shape[1]
+        copies.append(
+            pltpu.make_async_copy(
+                front_ref, out_hbm.at[:, edge : edge + size], sems.at[len(copies)]
+            )
+        )
+        copies[-1].start()
+        edge += size
+    assert edge == heads.start * width
 
     def put(head, value):
         at = (head - heads.start) * width
@@ -653,24 +635,24 @@
         copy.wait()
 
 
-def prompt_back(rate, group, heads, rows, keys, key_pos, query_pos, value_up, front):
+def prompt_back(rate, group, heads, rows, keys, key_pos, query_pos, value_up, *fronts):
     tokens = query_pos.shape[0]
     width = value_up.shape[2]
     return pl.pallas_call(
         functools.partial(back_kernel, rate, group, heads),
         out_shape=jax.ShapeDtypeStruct((tokens, heads.stop * width), BF16),
-        in_specs=[VMEM] * 6,
+        in_specs=[VMEM] * (5 + len(fronts)),
         out_specs=ANY,
         scratch_shapes=[
             pltpu.VMEM((tokens, len(heads) * width), BF16),
-            pltpu.SemaphoreType.DMA((1 + len(heads) // group,)),
+            pltpu.SemaphoreType.DMA((len(fronts) + len(heads) // group,)),
         ],
         compiler_params=params(16),
         cost_estimate=pl.CostEstimate(
             flops=8 * 10**8, bytes_accessed=6 * 10**6, transcendentals=3 * 10**5
         ),
         name="prompt_back",
-    )(*(in_vmem(v) for v in (rows, keys, key_pos, query_pos, value_up, front)))
+    )(*(in_vmem(v) for v in (rows, keys, key_pos, query_pos, value_up, *fronts)))
 
 
 def per_device(
@@ -692,24 +674,18 @@
     steps = step_query.shape[0]
     head_size = lax.axis_size("head")
     role_size = lax.axis_size("role")
-    contracted = out_weight.shape[0]
-    early_rows = contracted // 2
 
     rounds = doublings(context_size)
     assert role_size == 2 and context_size >= 4
-    far = swap(prompt_latent, "ctx", 2)
+    half = own_half(prompt_latent)
+    far = swap(half, "ctx", 2)
     (
         running,
-        key_up,
-        value_up,
-        latent,
         prompt_query,
-        early_weight,
         key_pos,
         query_pos,
     ) = step_part(
         rate,
-        early_rows,
         block_order,
         cache_length,
         block_dest,
@@ -720,9 +696,8 @@
         step_latent,
         value_up,
         prompt_query,
-        out_weight,
-    )
-    group = 4 if heads % 8 == 0 else 1
+    )
+    group = 4 if heads % 16 == 0 else 2 if heads % 8 == 0 else 1
     middle = heads // 2
     rows = prompt_lift(range(middle), prompt_query, key_up)
     more_rows = prompt_lift(range(middle, heads), prompt_query, key_up)
@@ -730,33 +705,34 @@
         far_running = swap(running, "ctx", step)
         if step != rounds[-1]:
             running = merge_parts(rate, heads, running, far_running)
-    tokens = latent.shape[0]
-    mine = swap(move_rows(halves_kernel, tokens, latent, far), "ctx", 1)
+    near = swap(move_rows(join_kernel, 2 * half.shape[0], half, far), "ctx", 1)
+    mine = move_rows(join_kernel, 3 * half.shape[0], far, near)
     other = swap(mine, "role", 1)
-    keys = move_rows(gather_kernel, 4 * tokens, latent, far, mine, other)
+    latent = prompt_latent
+    keys = move_rows(gather_kernel, 4 * latent.shape[0], latent, mine, other)
     for step in rounds[2:]:
-        half = move_rows(half_kernel, keys.shape[0] // 2, keys)
-        received = swap(half, "ctx", step)
+        sent = move_rows(half_kernel, keys.shape[0] // 2, keys)
+        received = swap(sent, "ctx", step)
         keys = move_rows(
             extend_kernel, 2 * keys.shape[0], keys, received, swap(received, "role", 1)
         )
-    front, late_weight = prompt_front(
+    first, second = range(middle // 2), range(middle // 2, middle)
+    front_a = prompt_front(rate, group, first, rows, keys, key_pos, query_pos, value_up)
+    front_b = prompt_front(rate, group, second, rows, keys, key_pos, query_pos, value_up)
+    prompt_out = prompt_back(
         rate,
         group,
-        range(middle),
-        rows,
+        range(middle, heads),
+        more_rows,
         keys,
         key_pos,
         query_pos,
         value_up,
-        out_weight,
-        contracted - early_rows,
-    )
-    prompt_out = prompt_back(
-        rate, group, range(middle, heads), more_rows, keys, key_pos, query_pos, value_up, front
+        front_a,
+        front_b,
     )
     keep, give = finish_steps(
-        rate, heads, head_size * role_size, running, far_running, early_weight, late_weight
+        rate, heads, head_size * role_size, running, far_running, out_weight
     )
     partial = swap(give, "role", 1)
     for step in reversed(doublings(head_size)):

time: 34.9 us -> 34.7 us (level)
  Pallas kernels: 12.4 us -> 11 us
  waiting for transfers between devices: 11.1 us -> 11.9 us
    pallas_call x1, Pallas kernels: 4.29 us -> 2.34 us  [step_part(): pl.pallas_call(functools.partial(step_kernel, rate), out_shape=(shape((pa...]
    pallas_call x0 -> x2, Pallas kernels: none -> 1 us  [the longest x1 1 us: own_half(): pl.pallas_call(own_half_kernel, out_shape=pltpu.VMEM((latent.shape[0] //...]
    ppermute x7, waiting for transfers between devices: 11.1 us -> 11.9 us  [swap(): return lax.ppermute(value, axis, [(i, i ^ step) for i in range(size)])]
    pallas_call x1 -> x2, Pallas kernels: 2.06 us -> 2 us  [prompt_front(): pl.pallas_call(functools.partial(front_kernel, rate, group, heads), out_s...]
  transfers between devices with their start and end apart: 7 -> 7, of which waited for: 5 -> 6; matrix products, arithmetic and copies ran while one was open for 0% -> 0% of each run, Pallas kernels for 30% -> 17%
where the time goes in v4:
time: 34.7 us; the launch traced here: 34.6 us
  waiting for transfers between devices  11.9 us (34%)
  Pallas kernels  11 us (32%)
  starting transfers between devices  10.8 us (31%)
  between operations  0.79 us (2%)
    ppermute x7, waiting for transfers between devices, swap(): return lax.ppermute(value, axis, [(i, i ^ step) for i in range(size)])  11.9 us
    ppermute x7, starting transfers between devices, swap(): return lax.ppermute(value, axis, [(i, i ^ step) for i in range(size)])  10.8 us
    pallas_call x1, Pallas kernels, step_part(): pl.pallas_call(functools.partial(step_kernel, rate), out_shape=(shape((pa...  2.34 us
    pallas_call x1, Pallas kernels, prompt_back(): pl.pallas_call(functools.partial(back_kernel, rate, group, heads), out_sh...  2.16 us
    pallas_call x2, Pallas kernels, prompt_front(): pl.pallas_call(functools.partial(front_kernel, rate, group, heads), out_s...  2 us
    pallas_call x1, Pallas kernels, finish_steps(): pl.pallas_call(functools.partial(finish_kernel, rate, heads, parts), out_...  1.34 us
    pallas_call x2, Pallas kernels, prompt_lift(): pl.pallas_call(functools.partial(lift_kernel, heads), out_shape=pltpu.VME...  1.23 us
    pallas_call x1, Pallas kernels, own_half(): pl.pallas_call(own_half_kernel, out_shape=pltpu.VMEM((latent.shape[0] //...  1 us
  transfers between devices with their start and end apart: 7, of which 6 were waited for; matrix products, arithmetic and copies ran while one was open for 0% of the time, Pallas kernels for 17%

profile of v4, /device:TPU:0, one launch (start us, length us, event | category | flops | bytes accessed | tf_op | source)
XLA Modules:
  0.0 34.6 jit_solution(10038050425729908453)
XLA Ops:
  0.6 0.0 slice-start
  0.6 1.0 %own_half.1.first_ref = bf16[48,576]{1,0:T(8,128)(2,1)S(1)} custom-call(bf16[96,576]{1,0:T(8,128)(2,1)} %own_ref.1), custom_call_target="tpu_custom_call" | custom-call | flops 10000 | bytes 100000 | tf_op jit(solution)/shard_map/own_half/pallas_call | solution.py:72
  1.6 0.0 copy-start
  1.7 0.0 copy-start.1
  1.7 0.0 copy-start.2
  1.7 0.0 copy-start.3
  1.7 0.0 copy-start.4
  1.7 0.0 copy-start.5
  1.7 0.0 slice-start.1
  1.7 4.1 %collective-permute-start = (bf16[48,576]{1,0:T(8,128)(2,1)S(1)}, bf16[48,576]{1,0:T(8,128)(2,1)S(1)}, u32[]{:S(2)}, u32[]{:S(2)}) collective-permute-start(bf16[48,576]{1,0:T(8,128)(2,1)S(1)} %own_half.1.first_ref), channel_id=1, source_target_pairs={{0,8},{4,12},{8,0},{12,4},{1,9},{5,13},{9,1},{13,5},{2,10},{6,14},... | collective-permute-start | bytes 165896 | tf_op jit(solution)/shard_map/ppermute | solution.py:45
  5.9 2.9 %collective-permute-done.second_ref.first_ref = bf16[48,576]{1,0:T(8,128)(2,1)S(1)} collective-permute-done((bf16[48,576]{1,0:T(8,128)(2,1)S(1)}, bf16[48,576]{1,0:T(8,128)(2,1)S(1)}, u32[]{:S(2)}, u32[]{:S(2)}) %collective-permute-start) | collective-permute-done | bytes 55328 | tf_op jit(solution)/shard_map/ppermute | solution.py:45
  8.7 1.3 %collective-permute-start.1 = (bf16[96,576]{1,0:T(8,128)(2,1)S(1)}, bf16[96,576]{1,0:T(8,128)(2,1)S(1)}, u32[]{:S(2)}, u32[]{:S(2)}) collective-permute-start(bf16[96,576]{1,0:T(8,128)(2,1)S(1)} %shard_map.122), channel_id=1, source_target_pairs={{0,4},{4,0},{8,12},{12,8},{1,5},{5,1},{9,13},{13,9},{2,6},{6,2},{1... | collective-permute-start | bytes 331784 | tf_op jit(solution)/shard_map/ppermute | solution.py:45
  10.1 0.0 copy-done
  10.1 0.0 copy-done.1
  10.1 0.0 copy-done.2
  10.1 0.0 copy-done.3
  10.1 0.0 copy-done.4
  10.1 0.0 copy-done.5
  10.1 2.3 %step_part.1 = (bf16[16,2176]{1,0:T(8,128)(2,1)S(1)}, bf16[96,16,192]{2,1,0:T(8,128)(2,1)S(1)}, s32[8,384]{1,0:T(8,128)S(1)}, s32[96,128]{1,0:T(8,128)S(1)}) custom-call(f32[8,128]{1,0:T(8,128)S(1)} %mark.1.mark_ref, s32[4]{0:T(128)} %order_hbm.1, s32[4]{0:T(128)} %length_hbm.1, s32[4]{0:T(128)} %dest_hbm.1, bf16[4,4,16,192]{3,2,1,0:T(8,128)(2,1)S(1)} %copy-done.4, ...), custom_call_target="tpu_custom_call" | custom-call | flops 1000000000 | bytes 10000000 | tf_op jit(solution)/shard_map/step_part/pallas_call | solution.py:276
  12.4 0.8 %collective-permute-start.3 = (bf16[16,2176]{1,0:T(8,128)(2,1)S(1)}, bf16[16,2176]{1,0:T(8,128)(2,1)S(1)}, u32[]{:S(2)}, u32[]{:S(2)}) collective-permute-start(bf16[16,2176]{1,0:T(8,128)(2,1)S(1)} %get-tuple-element.13.first_ref), channel_id=1, source_target_pairs={{0,4},{4,0},{8,12},{12,8},{1,5},{5,1},{9,13},{13,9},{2,6},{6,2},{1... | collective-permute-start | bytes 208904 | tf_op jit(solution)/shard_map/ppermute | solution.py:45
  13.3 0.5 %collective-permute-done.1.second_ref = bf16[96,576]{1,0:T(8,128)(2,1)S(1)} collective-permute-done((bf16[96,576]{1,0:T(8,128)(2,1)S(1)}, bf16[96,576]{1,0:T(8,128)(2,1)S(1)}, u32[]{:S(2)}, u32[]{:S(2)}) %collective-permute-start.1) | collective-permute-done | bytes 110624 | tf_op jit(solution)/shard_map/ppermute | solution.py:45
  13.8 0.1 collective-permute-start.2
  13.9 2.9 %collective-permute-done.3.second_ref = bf16[16,2176]{1,0:T(8,128)(2,1)S(1)} collective-permute-done((bf16[16,2176]{1,0:T(8,128)(2,1)S(1)}, bf16[16,2176]{1,0:T(8,128)(2,1)S(1)}, u32[]{:S(2)}, u32[]{:S(2)}) %collective-permute-start.3) | collective-permute-done | bytes 69664 | tf_op jit(solution)/shard_map/ppermute | solution.py:45
  16.8 0.3 merge_parts.1.first_ref
  17.1 3.4 %collective-permute-start.4 = (bf16[16,2176]{1,0:T(8,128)(2,1)S(1)}, bf16[16,2176]{1,0:T(8,128)(2,1)S(1)}, u32[]{:S(2)}, u32[]{:S(2)}) collective-permute-start(bf16[16,2176]{1,0:T(8,128)(2,1)S(1)} %merge_parts.1.first_ref), channel_id=1, source_target_pairs={{0,8},{4,12},{8,0},{12,4},{1,9},{5,13},{9,1},{13,5},{2,10},{6,14},... | collective-permute-start | bytes 208904 | tf_op jit(solution)/shard_map/ppermute | solution.py:45
  20.5 2.9 %collective-permute-done.4.second_ref = bf16[16,2176]{1,0:T(8,128)(2,1)S(1)} collective-permute-done((bf16[16,2176]{1,0:T(8,128)(2,1)S(1)}, bf16[16,2176]{1,0:T(8,128)(2,1)S(1)}, u32[]{:S(2)}, u32[]{:S(2)}) %collective-permute-start.4) | collective-permute-done | bytes 69664 | tf_op jit(solution)/shard_map/ppermute | solution.py:45
  23.3 0.0 slice-done
  23.3 0.0 slice-done.1
  23.3 1.3 %finish_steps.1 = (f32[2,16,448]{2,1,0:T(8,128)S(1)}, bf16[2,16,448]{2,1,0:T(8,128)(2,1)S(1)}) custom-call(bf16[16,2176]{1,0:T(8,128)(2,1)S(1)} %merge_parts.1.first_ref, bf16[16,2176]{1,0:T(8,128)(2,1)S(1)} %collective-permute-done.4.second_ref, bf16[2048,1792]{1,0:T(8,128)(2,1)S(1)} %bitcast.2), custom_call_target="tpu_custom_call" | custom-call | flops 500000000 | bytes 8000000 | tf_op jit(solution)/shard_map/finish_steps/pallas_call | solution.py:442
  24.7 0.0 collective-permute-start.5
  24.7 0.6 %prompt_lift.3.row_ref = bf16[768,576]{1,0:T(8,128)(2,1)S(1)} custom-call(bf16[96,16,192]{2,1,0:T(8,128)(2,1)S(1)} %get-tuple-element.10.query_ref, bf16[16,128,512]{2,1,0:T(8,128)(2,1)S(1)} %copy-done.1), custom_call_target="tpu_custom_call" | custom-call | flops 200000000 | bytes 3000000 | tf_op jit(solution)/shard_map/prompt_lift/pallas_call | solution.py:515
  25.3 0.6 %collective-permute-done.5.received_ref = bf16[2,16,448]{2,1,0:T(8,128)(2,1)S(1)} collective-permute-done((bf16[2,16,448]{2,1,0:T(8,128)(2,1)S(1)}, bf16[2,16,448]{2,1,0:T(8,128)(2,1)S(1)}, u32[]{:S(2)}, u32[]{:S(2)}) %collective-permute-start.5) | collective-permute-done | bytes 28704 | tf_op jit(solution)/shard_map/ppermute | solution.py:45
  25.9 1.0 %collective-permute-start.6 = (bf16[1,16,448]{2,1,0:T(8,128)(2,1)S(1)}, bf16[1,16,448]{2,1,0:T(8,128)(2,1)S(1)}, u32[]{:S(2)}, u32[]{:S(2)}) collective-permute-start(bf16[1,16,448]{2,1,0:T(8,128)(2,1)S(1)} %get-tuple-element.17), channel_id=1, source_target_pairs={{0,2},{2,0},{1,3},{3,1},{4,6},{6,4},{5,7},{7,5},{8,10},{10,8},{9,1... | collective-permute-start | bytes 43016 | tf_op jit(solution)/shard_map/ppermute | solution.py:45
  26.9 0.6 %prompt_lift.2.row_ref = bf16[768,576]{1,0:T(8,128)(2,1)S(1)} custom-call(bf16[96,16,192]{2,1,0:T(8,128)(2,1)S(1)} %get-tuple-element.10.query_ref, bf16[16,128,512]{2,1,0:T(8,128)(2,1)S(1)} %copy-done.1), custom_call_target="tpu_custom_call" | custom-call | flops 200000000 | bytes 3000000 | tf_op jit(solution)/shard_map/prompt_lift/pallas_call | solution.py:515
  27.5 2.2 %collective-permute-done.6.received_ref = bf16[1,16,448]{2,1,0:T(8,128)(2,1)S(1)} collective-permute-done((bf16[1,16,448]{2,1,0:T(8,128)(2,1)S(1)}, bf16[1,16,448]{2,1,0:T(8,128)(2,1)S(1)}, u32[]{:S(2)}, u32[]{:S(2)}) %collective-permute-start.6) | collective-permute-done | bytes 14368 | tf_op jit(solution)/shard_map/ppermute | solution.py:45
  29.7 0.6 %sum_steps.1 = bf16[4,4,448]{2,1,0:T(4,128)(2,1)} custom-call(f32[1,16,448]{2,1,0:T(8,128)S(1)} %get-tuple-element.16.keep_ref, bf16[1,16,448]{2,1,0:T(8,128)(2,1)S(1)} %collective-permute-done.6.received_ref), custom_call_target="tpu_custom_call" | custom-call | flops 100000 | bytes 100000 | tf_op jit(solution)/shard_map/sum_steps/pallas_call | solution.py:486
  30.4 0.0 collective-permute-done.2.other_ref
  30.4 1.0 %prompt_front.3.refs_1_ = bf16[96,512]{1,0:T(8,128)(2,1)S(1)} custom-call(bf16[768,576]{1,0:T(8,128)(2,1)S(1)} %prompt_lift.3.row_ref, bf16[384,576]{1,0:T(8,128)(2,1)S(1)} %shard_map.124.key_ref, s32[8,384]{1,0:T(8,128)S(1)} %get-tuple-element.11.key_pos_ref, s32[96,128]{1,0:T(8,128)S(1)} %get-tuple-element.12.query_pos_ref, bf16[16,512,128]{2,1,0:T(8,128)(2,1)S(1)} %copy-done), custom_call_target="tpu_custom_call" | custom-call | flops 400000000 | bytes 3000000 | tf_op jit(solution)/shard_map/prompt_front/pallas_call | solution.py:578
  31.4 1.0 %prompt_front.2.refs_0_ = bf16[96,512]{1,0:T(8,128)(2,1)S(1)} custom-call(bf16[768,576]{1,0:T(8,128)(2,1)S(1)} %prompt_lift.3.row_ref, bf16[384,576]{1,0:T(8,128)(2,1)S(1)} %shard_map.124.key_ref, s32[8,384]{1,0:T(8,128)S(1)} %get-tuple-element.11.key_pos_ref, s32[96,128]{1,0:T(8,128)S(1)} %get-tuple-element.12.query_pos_ref, bf16[16,512,128]{2,1,0:T(8,128)(2,1)S(1)} %copy-done), custom_call_target="tpu_custom_call" | custom-call | flops 400000000 | bytes 3000000 | tf_op jit(solution)/shard_map/prompt_front/pallas_call | solution.py:578
  32.4 2.2 %prompt_back.1 = bf16[96,2048]{1,0:T(8,128)(2,1)} custom-call(bf16[768,576]{1,0:T(8,128)(2,1)S(1)} %prompt_lift.2.row_ref, bf16[384,576]{1,0:T(8,128)(2,1)S(1)} %shard_map.124.key_ref, s32[8,384]{1,0:T(8,128)S(1)} %get-tuple-element.11.key_pos_ref, s32[96,128]{1,0:T(8,128)S(1)} %get-tuple-element.12.query_pos_ref, bf16[16,512,128]{2,1,0:T(8,128)(2,1)S(1)} %copy-done, ...), custom_call_target="tpu_custom_call" | custom-call | flops 800000000 | bytes 6000000 | tf_op jit(solution)/shard_map/prompt_back/pallas_call | solution.py:641
  (6 shorter events, 0.1 us)
Async XLA Ops:
  0.6 22.7 %slice-start = ((s8[7340032]{0:T(1024)(128)(4,1)}), s8[4194304]{0:T(1024)(128)(4,1)S(1)}, s32[]{:S(2)}) async-start(s8[7340032]{0:T(1024)(128)(4,1)} %bitcast.1), calls=%async_computation | async-start | bytes 8388608
  1.6 8.4 %copy-start = (bf16[16,512,128]{2,1,0:T(8,128)(2,1)S(1)}, bf16[16,512,128]{2,1,0:T(8,128)(2,1)}, u32[]{:S(2)}) copy-start(bf16[16,512,128]{2,1,0:T(8,128)(2,1)} %value_up_ref.7) | copy-start | bytes 6291460
  1.7 8.4 %copy-start.1 = (bf16[16,128,512]{2,1,0:T(8,128)(2,1)S(1)}, bf16[16,128,512]{2,1,0:T(8,128)(2,1)}, u32[]{:S(2)}) copy-start(bf16[16,128,512]{2,1,0:T(8,128)(2,1)} %key_up_ref.5) | copy-start | bytes 6291460
  1.7 8.4 %copy-start.2 = (bf16[4,384,576]{1,2,0:T(8,128)(2,1)S(1)}, bf16[4,384,576]{1,2,0:T(8,128)(2,1)}, u32[]{:S(2)}) copy-start(bf16[4,384,576]{1,2,0:T(8,128)(2,1)} %param.18) | copy-start | bytes 5308420
  1.7 8.4 %copy-start.3 = (bf16[96,576]{1,0:T(8,128)(2,1)S(1)}, bf16[96,576]{1,0:T(8,128)(2,1)}, u32[]{:S(2)}) copy-start(bf16[96,576]{1,0:T(8,128)(2,1)} %own_ref.1) | copy-start | bytes 331780
  1.7 8.4 %copy-start.4 = (bf16[4,4,16,192]{3,2,1,0:T(8,128)(2,1)S(1)}, bf16[4,4,16,192]{3,2,1,0:T(8,128)(2,1)}, u32[]{:S(2)}) copy-start(bf16[4,4,16,192]{3,2,1,0:T(8,128)(2,1)} %query_ref.1) | copy-start | bytes 294916
  1.7 8.4 %copy-start.5 = (bf16[4,4,576]{2,1,0:T(4,128)(2,1)S(1)}, bf16[4,4,576]{2,1,0:T(4,128)(2,1)}, u32[]{:S(2)}) copy-start(bf16[4,4,576]{2,1,0:T(4,128)(2,1)} %fresh_ref.1) | copy-start | bytes 55300
  1.7 21.6 %slice-start.1 = ((s8[7340032]{0:T(1024)(128)(4,1)}), s8[3145728]{0:T(1024)(128)(4,1)S(1)}, s32[]{:S(2)}) async-start(s8[7340032]{0:T(1024)(128)(4,1)} %bitcast.1), calls=%async_computation.1 | async-start | bytes 6291456
  1.7 7.0 %collective-permute-start = (bf16[48,576]{1,0:T(8,128)(2,1)S(1)}, bf16[48,576]{1,0:T(8,128)(2,1)S(1)}, u32[]{:S(2)}, u32[]{:S(2)}) collective-permute-start(bf16[48,576]{1,0:T(8,128)(2,1)S(1)} %own_half.1.first_ref), channel_id=1, source_target_pairs={{0,8},{4,12},{8,0},{12,4},{1,9},{5,13},{9,1},{13,5},{2,10},{6,14},... | collective-permute-start | bytes 165896 | tf_op jit(solution)/shard_map/ppermute | solution.py:45
  8.7 5.0 %collective-permute-start.1 = (bf16[96,576]{1,0:T(8,128)(2,1)S(1)}, bf16[96,576]{1,0:T(8,128)(2,1)S(1)}, u32[]{:S(2)}, u32[]{:S(2)}) collective-permute-start(bf16[96,576]{1,0:T(8,128)(2,1)S(1)} %shard_map.122), channel_id=1, source_target_pairs={{0,4},{4,0},{8,12},{12,8},{1,5},{5,1},{9,13},{13,9},{2,6},{6,2},{1... | collective-permute-start | bytes 331784 | tf_op jit(solution)/shard_map/ppermute | solution.py:45
  12.4 4.4 %collective-permute-start.3 = (bf16[16,2176]{1,0:T(8,128)(2,1)S(1)}, bf16[16,2176]{1,0:T(8,128)(2,1)S(1)}, u32[]{:S(2)}, u32[]{:S(2)}) collective-permute-start(bf16[16,2176]{1,0:T(8,128)(2,1)S(1)} %get-tuple-element.13.first_ref), channel_id=1, source_target_pairs={{0,4},{4,0},{8,12},{12,8},{1,5},{5,1},{9,13},{13,9},{2,6},{6,2},{1... | collective-permute-start | bytes 208904 | tf_op jit(solution)/shard_map/ppermute | solution.py:45
  13.8 16.6 %collective-permute-start.2 = (bf16[144,576]{1,0:T(8,128)(2,1)S(1)}, bf16[144,576]{1,0:T(8,128)(2,1)S(1)}, u32[]{:S(2)}, u32[]{:S(2)}) collective-permute-start(bf16[144,576]{1,0:T(8,128)(2,1)S(1)} %shard_map.123.mine_ref), channel_id=1, source_target_pairs={{0,1},{1,0},{2,3},{3,2},{4,5},{5,4},{6,7},{7,6},{8,9},{9,8},{10,11... | collective-permute-start | bytes 497672 | tf_op jit(solution)/shard_map/ppermute | solution.py:45
  17.1 6.2 %collective-permute-start.4 = (bf16[16,2176]{1,0:T(8,128)(2,1)S(1)}, bf16[16,2176]{1,0:T(8,128)(2,1)S(1)}, u32[]{:S(2)}, u32[]{:S(2)}) collective-permute-start(bf16[16,2176]{1,0:T(8,128)(2,1)S(1)} %merge_parts.1.first_ref), channel_id=1, source_target_pairs={{0,8},{4,12},{8,0},{12,4},{1,9},{5,13},{9,1},{13,5},{2,10},{6,14},... | collective-permute-start | bytes 208904 | tf_op jit(solution)/shard_map/ppermute | solution.py:45
  24.7 1.2 %collective-permute-start.5 = (bf16[2,16,448]{2,1,0:T(8,128)(2,1)S(1)}, bf16[2,16,448]{2,1,0:T(8,128)(2,1)S(1)}, u32[]{:S(2)}, u32[]{:S(2)}) collective-permute-start(bf16[2,16,448]{2,1,0:T(8,128)(2,1)S(1)} %get-tuple-element.15), channel_id=1, source_target_pairs={{0,1},{1,0},{2,3},{3,2},{4,5},{5,4},{6,7},{7,6},{8,9},{9,8},{10,11... | collective-permute-start | bytes 86024 | tf_op jit(solution)/shard_map/ppermute | solution.py:45
  25.9 3.8 %collective-permute-start.6 = (bf16[1,16,448]{2,1,0:T(8,128)(2,1)S(1)}, bf16[1,16,448]{2,1,0:T(8,128)(2,1)S(1)}, u32[]{:S(2)}, u32[]{:S(2)}) collective-permute-start(bf16[1,16,448]{2,1,0:T(8,128)(2,1)S(1)} %get-tuple-element.17), channel_id=1, source_target_pairs={{0,2},{2,0},{1,3},{3,1},{4,6},{6,4},{5,7},{7,5},{8,10},{10,8},{9,1... | collective-permute-start | bytes 43016 | tf_op jit(solution)/shard_map/ppermute | solution.py:45

commit v5 on v4

--- a/solution.py
+++ b/solution.py
@@ -45,42 +45,6 @@
     return lax.ppermute(value, axis, [(i, i ^ step) for i in range(size)])
 
 
-def mark_kernel(out_ref):
-    out_ref[...] = jnp.zeros_like(out_ref)
-
-
-def mark():
-    return pl.pallas_call(
-        mark_kernel,
-        out_shape=pltpu.VMEM((8, LANES), F32),
-        out_specs=VMEM,
-        compiler_params=params(1),
-        cost_estimate=pl.CostEstimate(flops=8 * 10**9, bytes_accessed=10**4, transcendentals=0),
-        name="mark",
-    )()
-
-
-def own_half_kernel(latent_hbm, out_ref, sem):
-    half = out_ref.shape[0]
-    start = pl.multiple_of(lax.axis_index("role") * half, half)
-    copy = pltpu.make_async_copy(latent_hbm.at[pl.ds(start, half)], out_ref, sem)
-    copy.start()
-    copy.wait()
-
-
-def own_half(latent):
-    return pl.pallas_call(
-        own_half_kernel,
-        out_shape=pltpu.VMEM((latent.shape[0] // 2, latent.shape[1]), BF16),
-        in_specs=[ANY],
-        out_specs=VMEM,
-        scratch_shapes=[pltpu.SemaphoreType.DMA],
-        compiler_params=params(1),
-        cost_estimate=pl.CostEstimate(flops=10**4, bytes_accessed=10**5, transcendentals=0),
-        name="own_half",
-    )(in_hbm(latent))
-
-
 def in_hbm(value):
     return pltpu.with_memory_space_constraint(value, pltpu.HBM)
 
@@ -109,24 +73,30 @@
 
 def step_kernel(
     rate,
-    mark_ref,
     order_hbm,
     length_hbm,
     dest_hbm,
-    query_ref,
-    key_up_ref,
-    cache_ref,
-    latent_ref,
-    fresh_ref,
-    value_up_ref,
+    query_hbm,
+    key_up_hbm,
+    cache_hbm,
+    latent_hbm,
+    fresh_hbm,
+    value_up_hbm,
     prompt_hbm,
     out_ref,
+    key_up_ref,
+    value_up_ref,
+    latent_ref,
+    half_ref,
     prompt_ref,
     key_pos_ref,
     query_pos_ref,
     order_ref,
     length_ref,
     dest_ref,
+    query_ref,
+    cache_ref,
+    fresh_ref,
     nope_ref,
     row_ref,
     extra_ref,
@@ -149,13 +119,22 @@
         copies[-1].start()
         return copies[-1]
 
+    query_copy = fetch(query_hbm, query_ref)
+    quarter = heads // 4
+    key_up_copies = [
+        fetch(key_up_hbm.at[at : at + quarter], key_up_ref.at[at : at + quarter])
+        for at in range(0, heads, quarter)
+    ]
+    latent_copy = fetch(latent_hbm, latent_ref)
+    fresh_copy = fetch(fresh_hbm, fresh_ref)
     scalar_copies = [
         fetch(length_hbm, length_ref),
         fetch(dest_hbm, dest_ref),
         fetch(order_hbm, order_ref),
     ]
-    prompt_copy = fetch(prompt_hbm, prompt_ref)
-
+    cache_copy = fetch(cache_hbm, cache_ref)
+
+    query_copy.wait()
     query = query_ref[...].astype(F32)
     query = jnp.concatenate(
         [query[:, request].reshape(block, width) for request in range(requests)], axis=0
@@ -163,14 +142,27 @@
     nope_ref[...] = query[:, :nope]
     rope = query[:, nope:]
     for head in range(heads):
+        if head % quarter == 0:
+            key_up_copies[head // quarter].wait()
         part = nope_ref[pl.ds(head, pairs, stride=heads), :].astype(BF16)
         lifted = dot(part, key_up_ref[head]).astype(BF16).astype(F32)
         for lane in range(0, latent, LANES):
             row_ref[lane // LANES, pl.ds(head, pairs, stride=heads), :] = lifted[
                 :, lane : lane + LANES
             ]
+    value_up_copy = fetch(value_up_hbm, value_up_ref)
+    prompt_copy = fetch(prompt_hbm, prompt_ref)
     row_parts = [row_ref[index] for index in range(latent // LANES)] + [rope]
     query_rows = jnp.concatenate(row_parts, axis=1).astype(BF16)
+
+    latent_copy.wait()
+    fresh_copy.wait()
+    half = half_ref.shape[0]
+    for index in range(2):
+
+        @pl.when(lax.axis_index("role") == index)
+        def _():
+            half_ref[...] = latent_ref[index * half : (index + 1) * half, :]
 
     extra_ref[:tokens, :] = latent_ref[...].astype(F32)
     for step in range(steps):
@@ -192,6 +184,7 @@
     )
     more = jnp.where(seen, more, HIDDEN)
     position = place * span + lax.broadcasted_iota(jnp.int32, (1, span), 1)
+    cache_copy.wait()
     scores = [
         jnp.where(
             position < length_ref[request],
@@ -223,6 +216,7 @@
     high = jnp.broadcast_to(high, (rows, LANES))
     total = jnp.broadcast_to(total, (rows, LANES))
 
+    value_up_copy.wait()
     value_width = value_up_ref.shape[2]
     for head in range(heads):
         parts = [
@@ -277,37 +271,48 @@
         functools.partial(step_kernel, rate),
         out_shape=(
             shape((pairs, heads * value_up.shape[2] + LANES), BF16),
+            shape(key_up.shape, BF16),
+            shape(value_up.shape, BF16),
+            shape(latent.shape, BF16),
+            shape((tokens // 2, full), BF16),
             shape(prompt_query.shape, BF16),
             shape((8, tokens * lax.axis_size("ctx")), jnp.int32),
             shape((tokens, LANES), jnp.int32),
         ),
-        in_specs=[VMEM] + [ANY] * 3 + [VMEM] * 6 + [ANY],
-        out_specs=[VMEM] * 4,
+        in_specs=[ANY] * 10,
+        out_specs=[VMEM] * 8,
         scratch_shapes=[
             pltpu.SMEM(block_order.shape, jnp.int32),
             pltpu.SMEM(cache_length.shape, jnp.int32),
             pltpu.SMEM(block_dest.shape, jnp.int32),
+            pltpu.VMEM(step_query.shape, BF16),
+            pltpu.VMEM(cache.shape, BF16),
+            pltpu.VMEM(fresh.shape, BF16),
             pltpu.VMEM((rows, nope), F32),
             pltpu.VMEM((latent_width // LANES, rows, LANES), F32),
             pltpu.VMEM((tokens + pairs, full), F32),
             pltpu.VMEM((latent_width // LANES, rows, LANES), F32),
-            pltpu.SemaphoreType.DMA((4,)),
+            pltpu.SemaphoreType.DMA((13,)),
         ],
-        compiler_params=params(12),
+        compiler_params=params(16),
         cost_estimate=pl.CostEstimate(flops=10**9, bytes_accessed=10**7, transcendentals=10**5),
         name="step_part",
     )(
-        mark(),
-        in_hbm(block_order),
-        in_hbm(cache_length),
-        in_hbm(block_dest),
-        in_vmem(step_query),
-        in_vmem(key_up),
-        in_vmem(cache),
-        in_vmem(latent),
-        in_vmem(fresh),
-        in_vmem(value_up),
-        in_hbm(prompt_query),
+        *(
+            in_hbm(value)
+            for value in (
+                block_order,
+                cache_length,
+                block_dest,
+                step_query,
+                key_up,
+                cache,
+                latent,
+                fresh,
+                value_up,
+                prompt_query,
+            )
+        )
     )
 
 
@@ -363,7 +368,9 @@
         in_specs=[VMEM] * 2,
         out_specs=VMEM,
         compiler_params=params(2),
-        cost_estimate=pl.CostEstimate(flops=10**5, bytes_accessed=2 * 10**5, transcendentals=10**4),
+        cost_estimate=pl.CostEstimate(
+            flops=8 * 10**9, bytes_accessed=2 * 10**5, transcendentals=10**4
+        ),
         name="merge_parts",
     )(in_vmem(first), in_vmem(second))
 
@@ -473,48 +480,27 @@
     )(in_vmem(keep), in_vmem(received))
 
 
-def sum_kernel(keep_ref, received_ref, out_ref):
-    share = keep_ref[0] + received_ref[0].astype(F32)
-    steps, requests, _ = out_ref.shape
-    for step in range(steps):
-        rows = [share[at : at + 1] for at in range(step, steps * requests, steps)]
-        out_ref[step] = jnp.concatenate(rows, axis=0).astype(BF16)
-
-
-def sum_steps(steps, keep, received):
-    pairs, width = keep.shape[1:]
-    return pl.pallas_call(
-        sum_kernel,
-        out_shape=jax.ShapeDtypeStruct((steps, pairs // steps, width), BF16),
-        in_specs=[VMEM] * 2,
-        out_specs=VMEM,
-        compiler_params=params(1),
-        cost_estimate=pl.CostEstimate(flops=10**5, bytes_accessed=10**5, transcendentals=0),
-        name="sum_steps",
-    )(in_vmem(keep), in_vmem(received))
-
-
-def lift_kernel(heads, query_ref, key_up_ref, row_ref, nope_ref, rope_ref):
+def lift_kernel(query_ref, key_up_ref, row_ref, nope_ref, rope_ref):
     tokens, every, width = query_ref.shape
     nope, latent = key_up_ref.shape[1:]
     nope_ref[...] = query_ref[:, :, :nope].astype(F32).reshape(tokens * every, nope)
     rope_ref[:, : width - nope] = (
         query_ref[:, :, nope:].astype(F32).reshape(tokens * every, width - nope)
     )
-    for index, head in enumerate(heads):
-        at = slice(index * tokens, (index + 1) * tokens)
+    for head in range(every):
+        at = slice(head * tokens, (head + 1) * tokens)
         part = nope_ref[pl.ds(head, tokens, stride=every), :].astype(BF16)
         row_ref[at, :latent] = dot(part, key_up_ref[head]).astype(BF16)
         rope = rope_ref[pl.ds(head, tokens, stride=every), :]
         row_ref[at, latent:] = rope[:, : width - nope].astype(BF16)
 
 
-def prompt_lift(heads, prompt_query, key_up):
+def prompt_lift(prompt_query, key_up):
     tokens, every, width = prompt_query.shape
     nope, latent_width = key_up.shape[1:]
     return pl.pallas_call(
-        functools.partial(lift_kernel, heads),
-        out_shape=pltpu.VMEM((tokens * len(heads), latent_width + width - nope), BF16),
+        lift_kernel,
+        out_shape=pltpu.VMEM((tokens * every, latent_width + width - nope), BF16),
         in_specs=[VMEM] * 2,
         out_specs=VMEM,
         scratch_shapes=[
@@ -523,7 +509,7 @@
         ],
         compiler_params=params(8),
         cost_estimate=pl.CostEstimate(
-            flops=2 * 10**8, bytes_accessed=3 * 10**6, transcendentals=0
+            flops=8 * 10**8, bytes_accessed=3 * 10**6, transcendentals=0
         ),
         name="prompt_lift",
     )(in_vmem(prompt_query), in_vmem(key_up))
@@ -538,8 +524,7 @@
     visible = (key_pos_ref[:1, :] <= query_pos_ref[:, :1])[None]
 
     def score(first):
-        base = first % (row_ref.shape[0] // tokens)
-        at = slice(base * tokens, (base + group) * tokens)
+        at = slice(first * tokens, (first + group) * tokens)
         return dot_nt(row_ref[at, :], key_ref[...])
 
     firsts = list(range(heads.start, heads.stop, group))
@@ -597,36 +582,40 @@
     key_pos_ref,
     query_pos_ref,
     value_up_ref,
-    *refs,
+    front_ref,
+    keep_ref,
+    received_ref,
+    out_hbm,
+    steps_hbm,
+    back_ref,
+    steps_ref,
+    sems,
 ):
-    *front_refs, out_hbm, back_ref, sems = refs
     width = value_up_ref.shape[2]
-    edge = 0
+    edge = heads.start * width
     copies = []
-    for front_ref in front_refs:
-        size = front_ref.shape[1]
-        copies.append(
-            pltpu.make_async_copy(
-                front_ref, out_hbm.at[:, edge : edge + size], sems.at[len(copies)]
-            )
-        )
+
+    def send(source, target):
+        copies.append(pltpu.make_async_copy(source, target, sems.at[len(copies)]))
         copies[-1].start()
-        edge += size
-    assert edge == heads.start * width
+
+    send(front_ref, out_hbm.at[:, :edge])
+    share = keep_ref[0] + received_ref[0].astype(F32)
+    steps, requests, _ = steps_ref.shape
+    for step in range(steps):
+        rows = [share[at : at + 1] for at in range(step, steps * requests, steps)]
+        steps_ref[step] = jnp.concatenate(rows, axis=0).astype(BF16)
+    send(steps_ref, steps_hbm)
 
     def put(head, value):
         at = (head - heads.start) * width
         back_ref[:, at : at + width] = value
         if (head - heads.start + 1) % group == 0:
             start = at + width - group * width
-            copies.append(
-                pltpu.make_async_copy(
-                    back_ref.at[:, start : at + width],
-                    out_hbm.at[:, edge + start : edge + at + width],
-                    sems.at[len(copies)],
-                )
+            send(
+                back_ref.at[:, start : at + width],
+                out_hbm.at[:, edge + start : edge + at + width],
             )
-            copies[-1].start()
 
     attend(
         rate, group, heads, row_ref, key_ref, key_pos_ref, query_pos_ref, value_up_ref, put
@@ -635,24 +624,37 @@
         copy.wait()
 
 
-def prompt_back(rate, group, heads, rows, keys, key_pos, query_pos, value_up, *fronts):
+def prompt_back(
+    rate, group, heads, steps, rows, keys, key_pos, query_pos, value_up, front, keep, received
+):
     tokens = query_pos.shape[0]
     width = value_up.shape[2]
+    pairs, columns = keep.shape[1:]
+    step_shape = (steps, pairs // steps, columns)
     return pl.pallas_call(
         functools.partial(back_kernel, rate, group, heads),
-        out_shape=jax.ShapeDtypeStruct((tokens, heads.stop * width), BF16),
-        in_specs=[VMEM] * (5 + len(fronts)),
-        out_specs=ANY,
+        out_shape=(
+            jax.ShapeDtypeStruct((tokens, heads.stop * width), BF16),
+            jax.ShapeDtypeStruct(step_shape, BF16),
+        ),
+        in_specs=[VMEM] * 8,
+        out_specs=[ANY] * 2,
         scratch_shapes=[
             pltpu.VMEM((tokens, len(heads) * width), BF16),
-            pltpu.SemaphoreType.DMA((len(fronts) + len(heads) // group,)),
+            pltpu.VMEM(step_shape, BF16),
+            pltpu.SemaphoreType.DMA((2 + len(heads) // group,)),
         ],
         compiler_params=params(16),
         cost_estimate=pl.CostEstimate(
             flops=8 * 10**8, bytes_accessed=6 * 10**6, transcendentals=3 * 10**5
         ),
         name="prompt_back",
-    )(*(in_vmem(v) for v in (rows, keys, key_pos, query_pos, value_up, *fronts)))
+    )(
+        *(
+            in_vmem(v)
+            for v in (rows, keys, key_pos, query_pos, value_up, front, keep, received)
+        )
+    )
 
 
 def per_device(
@@ -677,10 +679,12 @@
 
     rounds = doublings(context_size)
     assert role_size == 2 and context_size >= 4
-    half = own_half(prompt_latent)
-    far = swap(half, "ctx", 2)
     (
         running,
+        key_up,
+        value_up,
+        latent,
+        half,
         prompt_query,
         key_pos,
         query_pos,
@@ -698,17 +702,16 @@
         prompt_query,
     )
     group = 4 if heads % 16 == 0 else 2 if heads % 8 == 0 else 1
-    middle = heads // 2
-    rows = prompt_lift(range(middle), prompt_query, key_up)
-    more_rows = prompt_lift(range(middle, heads), prompt_query, key_up)
+    edge = heads - heads // 4
+    rows = prompt_lift(prompt_query, key_up)
     for step in rounds:
         far_running = swap(running, "ctx", step)
         if step != rounds[-1]:
             running = merge_parts(rate, heads, running, far_running)
+    far = swap(half, "ctx", 2)
     near = swap(move_rows(join_kernel, 2 * half.shape[0], half, far), "ctx", 1)
     mine = move_rows(join_kernel, 3 * half.shape[0], far, near)
     other = swap(mine, "role", 1)
-    latent = prompt_latent
     keys = move_rows(gather_kernel, 4 * latent.shape[0], latent, mine, other)
     for step in rounds[2:]:
         sent = move_rows(half_kernel, keys.shape[0] // 2, keys)
@@ -716,30 +719,28 @@
         keys = move_rows(
             extend_kernel, 2 * keys.shape[0], keys, received, swap(received, "role", 1)
         )
-    first, second = range(middle // 2), range(middle // 2, middle)
-    front_a = prompt_front(rate, group, first, rows, keys, key_pos, query_pos, value_up)
-    front_b = prompt_front(rate, group, second, rows, keys, key_pos, query_pos, value_up)
-    prompt_out = prompt_back(
+    front = prompt_front(rate, group, range(edge), rows, keys, key_pos, query_pos, value_up)
+    keep, give = finish_steps(
+        rate, heads, head_size * role_size, running, far_running, out_weight
+    )
+    partial = swap(give, "role", 1)
+    for step in reversed(doublings(head_size)):
+        keep, give = fold_steps(step, keep, partial)
+        partial = swap(give, "head", step)
+    return prompt_back(
         rate,
         group,
-        range(middle, heads),
-        more_rows,
+        range(edge, heads),
+        steps,
+        rows,
         keys,
         key_pos,
         query_pos,
         value_up,
-        front_a,
-        front_b,
-    )
-    keep, give = finish_steps(
-        rate, heads, head_size * role_size, running, far_running, out_weight
-    )
-    partial = swap(give, "role", 1)
-    for step in reversed(doublings(head_size)):
-        keep, give = fold_steps(step, keep, partial)
-        partial = swap(give, "head", step)
-    step_out = sum_steps(steps, keep, partial)
-    return (prompt_out, step_out)
+        front,
+        keep,
+        partial,
+    )
 
 
 def solution(mesh):

time: 34.7 us -> 28.2 us (0.81)
  waiting for transfers between devices: 11.9 us -> 6.29 us
  starting transfers between devices: 10.8 us -> 10.1 us
    ppermute x7, waiting for transfers between devices: 11.9 us -> 6.29 us  [swap(): return lax.ppermute(value, axis, [(i, i ^ step) for i in range(size)])]
    pallas_call x1, Pallas kernels: 2.34 us -> 4.2 us  [step_part(): pl.pallas_call(functools.partial(step_kernel, rate), out_shape=(shape((pa...]
    pallas_call x5 -> x1, Pallas kernels: 2.86 us -> 1.18 us  [prompt_lift(): pl.pallas_call(lift_kernel, out_shape=pltpu.VMEM((tokens * every, latent_...]
    ppermute x7, starting transfers between devices: 10.8 us -> 10.1 us  [swap(): return lax.ppermute(value, axis, [(i, i ^ step) for i in range(size)])]
    pallas_call x1, Pallas kernels: 2.16 us -> 1.66 us  [prompt_back(): pl.pallas_call(functools.partial(back_kernel, rate, group, heads), out_sh...]
    pallas_call x2 -> x1, Pallas kernels: 2 us -> 2.22 us  [prompt_front(): pl.pallas_call(functools.partial(front_kernel, rate, group, heads), out_s...]
  transfers between devices with their start and end apart: 7 -> 7, of which waited for: 6 -> 3; matrix products, arithmetic and copies ran while one was open for 0% -> 0% of each run, Pallas kernels for 17% -> 18%
where the time goes in v5:
time: 28.2 us; the launch traced here: 28.1 us
  Pallas kernels  11 us (39%)
  starting transfers between devices  10.1 us (36%)
  waiting for transfers between devices  6.29 us (22%)
  between operations  0.72 us (3%)
    ppermute x7, starting transfers between devices, swap(): return lax.ppermute(value, axis, [(i, i ^ step) for i in range(size)])  10.1 us
    ppermute x7, waiting for transfers between devices, swap(): return lax.ppermute(value, axis, [(i, i ^ step) for i in range(size)])  6.29 us
    pallas_call x1, Pallas kernels, step_part(): pl.pallas_call(functools.partial(step_kernel, rate), out_shape=(shape((pa...  4.2 us
    pallas_call x1, Pallas kernels, prompt_front(): pl.pallas_call(functools.partial(front_kernel, rate, group, heads), out_s...  2.22 us
    pallas_call x1, Pallas kernels, prompt_back(): pl.pallas_call(functools.partial(back_kernel, rate, group, heads), out_sh...  1.66 us
    pallas_call x1, Pallas kernels, finish_steps(): pl.pallas_call(functools.partial(finish_kernel, rate, heads, parts), out_...  1.34 us
    pallas_call x1, Pallas kernels, prompt_lift(): pl.pallas_call(lift_kernel, out_shape=pltpu.VMEM((tokens * every, latent_...  1.18 us
  transfers between devices with their start and end apart: 7, of which 3 were waited for; matrix products, arithmetic and copies ran while one was open for 0% of the time, Pallas kernels for 18%

profile of v5, /device:TPU:0, one launch (start us, length us, event | category | flops | bytes accessed | tf_op | source)
XLA Modules:
  0.0 28.1 jit_solution(2875404602114574085)
XLA Ops:
  0.6 4.2 %step_part.1 = (bf16[16,2176]{1,0:T(8,128)(2,1)S(1)}, bf16[16,128,512]{2,1,0:T(8,128)(2,1)S(1)}, bf16[16,512,128]{2,1,0:T(8,128)(2,1)S(1)}, bf16[96,576]{1,0:T(8...) custom-call(s32[4]{0:T(128)} %order_hbm.1, ...), custom_call_target="tpu_custom_call" | custom-call | flops 1000000000 | bytes 10000000 | tf_op jit(solution)/shard_map/step_part/pallas_call | solution.py:270
  4.8 3.1 %collective-permute-start.3 = (bf16[16,2176]{1,0:T(8,128)(2,1)S(1)}, bf16[16,2176]{1,0:T(8,128)(2,1)S(1)}, u32[]{:S(2)}, u32[]{:S(2)}) collective-permute-start(bf16[16,2176]{1,0:T(8,128)(2,1)S(1)} %get-tuple-element.21.first_ref), channel_id=1, source_target_pairs={{0,4},{4,0},{8,12},{12,8},{1,5},{5,1},{9,13},{13,9},{2,6},{6,2},{1... | collective-permute-start | bytes 208904 | tf_op jit(solution)/shard_map/ppermute | solution.py:45
  8.0 2.6 %collective-permute-start = (bf16[48,576]{1,0:T(8,128)(2,1)S(1)}, bf16[48,576]{1,0:T(8,128)(2,1)S(1)}, u32[]{:S(2)}, u32[]{:S(2)}) collective-permute-start(bf16[48,576]{1,0:T(8,128)(2,1)S(1)} %get-tuple-element.17.first_ref), channel_id=1, source_target_pairs={{0,8},{4,12},{8,0},{12,4},{1,9},{5,13},{9,1},{13,5},{2,10},{6,14},... | collective-permute-start | bytes 165896 | tf_op jit(solution)/shard_map/ppermute | solution.py:45
  10.6 3.2 %collective-permute-done.second_ref.first_ref = bf16[48,576]{1,0:T(8,128)(2,1)S(1)} collective-permute-done((bf16[48,576]{1,0:T(8,128)(2,1)S(1)}, bf16[48,576]{1,0:T(8,128)(2,1)S(1)}, u32[]{:S(2)}, u32[]{:S(2)}) %collective-permute-start) | collective-permute-done | bytes 55328 | tf_op jit(solution)/shard_map/ppermute | solution.py:45
  13.8 0.0 slice-start
  13.8 0.0 slice-start.1
  13.8 0.6 %collective-permute-start.1 = (bf16[96,576]{1,0:T(8,128)(2,1)S(1)}, bf16[96,576]{1,0:T(8,128)(2,1)S(1)}, u32[]{:S(2)}, u32[]{:S(2)}) collective-permute-start(bf16[96,576]{1,0:T(8,128)(2,1)S(1)} %shard_map.122), channel_id=1, source_target_pairs={{0,4},{4,0},{8,12},{12,8},{1,5},{5,1},{9,13},{13,9},{2,6},{6,2},{1... | collective-permute-start | bytes 331784 | tf_op jit(solution)/shard_map/ppermute | solution.py:45
  14.4 0.0 collective-permute-done.3.second_ref
  14.4 0.3 merge_parts.1.first_ref
  14.7 2.1 %collective-permute-start.4 = (bf16[16,2176]{1,0:T(8,128)(2,1)S(1)}, bf16[16,2176]{1,0:T(8,128)(2,1)S(1)}, u32[]{:S(2)}, u32[]{:S(2)}) collective-permute-start(bf16[16,2176]{1,0:T(8,128)(2,1)S(1)} %merge_parts.1.first_ref), channel_id=1, source_target_pairs={{0,8},{4,12},{8,0},{12,4},{1,9},{5,13},{9,1},{13,5},{2,10},{6,14},... | collective-permute-start | bytes 208904 | tf_op jit(solution)/shard_map/ppermute | solution.py:45
  16.8 2.0 %collective-permute-done.1.second_ref = bf16[96,576]{1,0:T(8,128)(2,1)S(1)} collective-permute-done((bf16[96,576]{1,0:T(8,128)(2,1)S(1)}, bf16[96,576]{1,0:T(8,128)(2,1)S(1)}, u32[]{:S(2)}, u32[]{:S(2)}) %collective-permute-start.1) | collective-permute-done | bytes 110624 | tf_op jit(solution)/shard_map/ppermute | solution.py:45
  18.8 0.1 collective-permute-start.2
  18.9 1.1 %collective-permute-done.4.second_ref = bf16[16,2176]{1,0:T(8,128)(2,1)S(1)} collective-permute-done((bf16[16,2176]{1,0:T(8,128)(2,1)S(1)}, bf16[16,2176]{1,0:T(8,128)(2,1)S(1)}, u32[]{:S(2)}, u32[]{:S(2)}) %collective-permute-start.4) | collective-permute-done | bytes 69664 | tf_op jit(solution)/shard_map/ppermute | solution.py:45
  20.0 0.0 slice-done
  20.0 0.0 slice-done.1
  20.0 1.3 %finish_steps.1 = (f32[2,16,448]{2,1,0:T(8,128)S(1)}, bf16[2,16,448]{2,1,0:T(8,128)(2,1)S(1)}) custom-call(bf16[16,2176]{1,0:T(8,128)(2,1)S(1)} %merge_parts.1.first_ref, bf16[16,2176]{1,0:T(8,128)(2,1)S(1)} %collective-permute-done.4.second_ref, bf16[2048,1792]{1,0:T(8,128)(2,1)S(1)} %bitcast.2), custom_call_target="tpu_custom_call" | custom-call | flops 500000000 | bytes 8000000 | tf_op jit(solution)/shard_map/finish_steps/pallas_call | solution.py:449
  21.3 0.0 collective-permute-start.5
  21.4 1.2 %prompt_lift.1.row_ref = bf16[1536,576]{1,0:T(8,128)(2,1)S(1)} custom-call(bf16[96,16,192]{2,1,0:T(8,128)(2,1)S(1)} %get-tuple-element.14.query_ref, bf16[16,128,512]{2,1,0:T(8,128)(2,1)S(1)} %get-tuple-element.15.key_up_ref), custom_call_target="tpu_custom_call" | custom-call | flops 800000000 | bytes 3000000 | tf_op jit(solution)/shard_map/prompt_lift/pallas_call | solution.py:501
  22.5 0.0 collective-permute-done.5.received_ref
  22.6 1.6 %collective-permute-start.6 = (bf16[1,16,448]{2,1,0:T(8,128)(2,1)S(1)}, bf16[1,16,448]{2,1,0:T(8,128)(2,1)S(1)}, u32[]{:S(2)}, u32[]{:S(2)}) collective-permute-start(bf16[1,16,448]{2,1,0:T(8,128)(2,1)S(1)} %get-tuple-element.25), channel_id=1, source_target_pairs={{0,2},{2,0},{1,3},{3,1},{4,6},{6,4},{5,7},{7,5},{8,10},{10,8},{9,1... | collective-permute-start | bytes 43016 | tf_op jit(solution)/shard_map/ppermute | solution.py:45
  24.1 0.0 collective-permute-done.2.other_ref
  24.2 2.2 %prompt_front.1.front_ref = bf16[96,1536]{1,0:T(8,128)(2,1)S(1)} custom-call(bf16[1536,576]{1,0:T(8,128)(2,1)S(1)} %prompt_lift.1.row_ref, bf16[384,576]{1,0:T(8,128)(2,1)S(1)} %shard_map.124.key_ref, s32[8,384]{1,0:T(8,128)S(1)} %get-tuple-element.18.key_pos_ref, s32[96,128]{1,0:T(8,128)S(1)} %get-tuple-element.19.query_pos_ref, ...), custom_call_target="tpu_custom_call" | custom-call | flops 400000000 | bytes 3000000 | tf_op jit(solution)/shard_map/prompt_front/pallas_call | solution.py:563
  26.4 0.0 collective-permute-done.6.received_ref
  26.4 1.7 %prompt_back.1 = (bf16[96,2048]{1,0:T(8,128)(2,1)}, bf16[4,4,448]{2,1,0:T(4,128)(2,1)}) custom-call(bf16[1536,576]{1,0:T(8,128)(2,1)S(1)} %prompt_lift.1.row_ref, bf16[384,576]{1,0:T(8,128)(2,1)S(1)} %shard_map.124.key_ref, s32[8,384]{1,0:T(8,128)S(1)} %get-tuple-element.18.key_pos_ref, s32[96,128]{1,0:T(8,128)S(1)} %get-tuple-element.19.query_pos_ref, ...), custom_call_target="tpu_custom_call" | custom-call | flops 800000000 | bytes 6000000 | tf_op jit(solution)/shard_map/prompt_back/pallas_call | solution.py:634
  (5 shorter events, 0.1 us)
Async XLA Ops:
  4.8 9.6 %collective-permute-start.3 = (bf16[16,2176]{1,0:T(8,128)(2,1)S(1)}, bf16[16,2176]{1,0:T(8,128)(2,1)S(1)}, u32[]{:S(2)}, u32[]{:S(2)}) collective-permute-start(bf16[16,2176]{1,0:T(8,128)(2,1)S(1)} %get-tuple-element.21.first_ref), channel_id=1, source_target_pairs={{0,4},{4,0},{8,12},{12,8},{1,5},{5,1},{9,13},{13,9},{2,6},{6,2},{1... | collective-permute-start | bytes 208904 | tf_op jit(solution)/shard_map/ppermute | solution.py:45
  8.0 5.8 %collective-permute-start = (bf16[48,576]{1,0:T(8,128)(2,1)S(1)}, bf16[48,576]{1,0:T(8,128)(2,1)S(1)}, u32[]{:S(2)}, u32[]{:S(2)}) collective-permute-start(bf16[48,576]{1,0:T(8,128)(2,1)S(1)} %get-tuple-element.17.first_ref), channel_id=1, source_target_pairs={{0,8},{4,12},{8,0},{12,4},{1,9},{5,13},{9,1},{13,5},{2,10},{6,14},... | collective-permute-start | bytes 165896 | tf_op jit(solution)/shard_map/ppermute | solution.py:45
  13.8 6.2 %slice-start = ((s8[7340032]{0:T(1024)(128)(4,1)}), s8[4194304]{0:T(1024)(128)(4,1)S(1)}, s32[]{:S(2)}) async-start(s8[7340032]{0:T(1024)(128)(4,1)} %bitcast.1), calls=%async_computation | async-start | bytes 8388608
  13.8 6.2 %slice-start.1 = ((s8[7340032]{0:T(1024)(128)(4,1)}), s8[3145728]{0:T(1024)(128)(4,1)S(1)}, s32[]{:S(2)}) async-start(s8[7340032]{0:T(1024)(128)(4,1)} %bitcast.1), calls=%async_computation.1 | async-start | bytes 6291456
  13.8 4.9 %collective-permute-start.1 = (bf16[96,576]{1,0:T(8,128)(2,1)S(1)}, bf16[96,576]{1,0:T(8,128)(2,1)S(1)}, u32[]{:S(2)}, u32[]{:S(2)}) collective-permute-start(bf16[96,576]{1,0:T(8,128)(2,1)S(1)} %shard_map.122), channel_id=1, source_target_pairs={{0,4},{4,0},{8,12},{12,8},{1,5},{5,1},{9,13},{13,9},{2,6},{6,2},{1... | collective-permute-start | bytes 331784 | tf_op jit(solution)/shard_map/ppermute | solution.py:45
  14.7 5.3 %collective-permute-start.4 = (bf16[16,2176]{1,0:T(8,128)(2,1)S(1)}, bf16[16,2176]{1,0:T(8,128)(2,1)S(1)}, u32[]{:S(2)}, u32[]{:S(2)}) collective-permute-start(bf16[16,2176]{1,0:T(8,128)(2,1)S(1)} %merge_parts.1.first_ref), channel_id=1, source_target_pairs={{0,8},{4,12},{8,0},{12,4},{1,9},{5,13},{9,1},{13,5},{2,10},{6,14},... | collective-permute-start | bytes 208904 | tf_op jit(solution)/shard_map/ppermute | solution.py:45
  18.8 5.3 %collective-permute-start.2 = (bf16[144,576]{1,0:T(8,128)(2,1)S(1)}, bf16[144,576]{1,0:T(8,128)(2,1)S(1)}, u32[]{:S(2)}, u32[]{:S(2)}) collective-permute-start(bf16[144,576]{1,0:T(8,128)(2,1)S(1)} %shard_map.123.mine_ref), channel_id=1, source_target_pairs={{0,1},{1,0},{2,3},{3,2},{4,5},{5,4},{6,7},{7,6},{8,9},{9,8},{10,11... | collective-permute-start | bytes 497672 | tf_op jit(solution)/shard_map/ppermute | solution.py:45
  21.3 1.2 %collective-permute-start.5 = (bf16[2,16,448]{2,1,0:T(8,128)(2,1)S(1)}, bf16[2,16,448]{2,1,0:T(8,128)(2,1)S(1)}, u32[]{:S(2)}, u32[]{:S(2)}) collective-permute-start(bf16[2,16,448]{2,1,0:T(8,128)(2,1)S(1)} %get-tuple-element.23), channel_id=1, source_target_pairs={{0,1},{1,0},{2,3},{3,2},{4,5},{5,4},{6,7},{7,6},{8,9},{9,8},{10,11... | collective-permute-start | bytes 86024 | tf_op jit(solution)/shard_map/ppermute | solution.py:45
  22.6 3.8 %collective-permute-start.6 = (bf16[1,16,448]{2,1,0:T(8,128)(2,1)S(1)}, bf16[1,16,448]{2,1,0:T(8,128)(2,1)S(1)}, u32[]{:S(2)}, u32[]{:S(2)}) collective-permute-start(bf16[1,16,448]{2,1,0:T(8,128)(2,1)S(1)} %get-tuple-element.25), channel_id=1, source_target_pairs={{0,2},{2,0},{1,3},{3,1},{4,6},{6,4},{5,7},{7,5},{8,10},{10,8},{9,1... | collective-permute-start | bytes 43016 | tf_op jit(solution)/shard_map/ppermute | solution.py:45
